TPU v7x, 32 devices: a whole 2x2x4 slice. The times are simulated.
32 devices in a mesh: dp: 4 (over y, x), sp: 8 (over z, core).
Axes of the slice: x: 2, y: 2, z: 4, core: 2. Of those that a mesh axis runs over, the one named last changes fastest.
Arguments:
- inputs: bfloat16 [4, 2048, 1024], P('dp', 'sp'), may hold values from -6 to 6
- block_order: int32 [16], replicated, may hold values from 0 to 15, as said below
- first_gain: bfloat16 [1024], P(('dp', 'sp')), may hold values from 0.5 to 1.5
- first_shift: bfloat16 [1024], P(('dp', 'sp')), may hold values from -4 to 4
- joint_weight: bfloat16 [1024, 3072], P(('dp', 'sp')), may hold values from -0.1875 to 0.1875
- query_bias: bfloat16 [1024], P(('dp', 'sp')), may hold values from -4 to 4
- value_bias: bfloat16 [1024], P(('dp', 'sp')), may hold values from -0.625 to 0.625
- mixer_weight: bfloat16 [1024, 1024], P(('dp', 'sp')), may hold values from -1 to 1
- mixer_bias: bfloat16 [1024], P(('dp', 'sp')), may hold values from -4 to 4
- second_gain: bfloat16 [1024], P(('dp', 'sp')), may hold values from 0.5 to 1.5
- second_shift: bfloat16 [1024], P(('dp', 'sp')), may hold values from -4 to 4
- expand_weight: bfloat16 [1024, 4096], P(('dp', 'sp')), may hold values from -0.1875 to 0.1875
- expand_bias: bfloat16 [4096], P(('dp', 'sp')), may hold values from -4 to 4
- reduce_weight: bfloat16 [4096, 1024], P(('dp', 'sp')), may hold values from -0.09375 to 0.09375
- reduce_bias: bfloat16 [1024], P(('dp', 'sp')), may hold values from -4 to 4
- cotangent: bfloat16 [4, 2048, 1024], P('dp', 'sp'), may hold values from -6 to 6
Outputs:
- output: bfloat16 [4, 2048, 1024], P('dp', 'sp')
- input_gradient: bfloat16 [4, 2048, 1024], P('dp', 'sp')
- first_gain_gradient: float32 [1024], P(('dp', 'sp'))
- first_shift_gradient: float32 [1024], P(('dp', 'sp'))
- joint_weight_gradient: float32 [1024, 3072], P(('dp', 'sp'))
- query_bias_gradient: float32 [1024], P(('dp', 'sp'))
- value_bias_gradient: float32 [1024], P(('dp', 'sp'))
- mixer_weight_gradient: float32 [1024, 1024], P(('dp', 'sp'))
- mixer_bias_gradient: float32 [1024], P(('dp', 'sp'))
- second_gain_gradient: float32 [1024], P(('dp', 'sp'))
- second_shift_gradient: float32 [1024], P(('dp', 'sp'))
- expand_weight_gradient: float32 [1024, 4096], P(('dp', 'sp'))
- expand_bias_gradient: float32 [4096], P(('dp', 'sp'))
- reduce_weight_gradient: float32 [4096, 1024], P(('dp', 'sp'))
- reduce_bias_gradient: float32 [1024], P(('dp', 'sp'))
Inputs may be any that keep to these rules, and one draw needn't show every extreme that they name: `block_order`: every block 0 to 15 appears once; slot 2j holds a block below 8 and slot 2j+1 holds 15 minus it.
All inputs are finite; a program needn't handle non-finite values.
Results may differ from a plain program's by a relative error of at most 0.018.
Values may be sent and summed in bfloat16 or wider, within the bound.
No kernel may reach another device: no remote copies, remote signals or barrier semaphores. Data moves between devices by JAX's collectives and lax.ppermute only.
A program may use at most 192 MiB of HBM per device.

v0:
```python
import jax
import jax.numpy as jnp
from jax import lax
from jax.sharding import PartitionSpec as P

D = 1024
H = 16
HD = 64


EPS = 1e-05


def passed_along(value, axis, steps):
    count = lax.axis_size(axis)
    pairs = [(source, (source + steps) % count) for source in range(count)]
    return lax.ppermute(value, axis, pairs)


def layer_norm(values, scaling, offset):
    average = jnp.mean(values, axis=-1, keepdims=True)
    centred = values - average
    spread = jnp.mean(centred * centred, axis=-1, keepdims=True)
    return centred * lax.rsqrt(spread + EPS) * scaling + offset


def gelu_tanh(values):
    return jax.nn.gelu(values, approximate=True)


def product(left, right):
    return jnp.dot(left, right, preferred_element_type=jnp.float32)


def inner_rows(left, right):
    return lax.dot_general(
        left, right, (((0,), (0,)), ((), ())), preferred_element_type=jnp.float32
    )


def inner_cols(left, right):
    return lax.dot_general(
        left, right, (((1,), (1,)), ((), ())), preferred_element_type=jnp.float32
    )


def tile_forward(queries, key_rows, value_rows, visible, factor):
    scores = jnp.einsum("tqhd,tkhd->thqk", queries, key_rows, preferred_element_type=jnp.float32)
    powers = jnp.exp(scores * factor)
    if visible is not None:
        powers = jnp.where(visible[:, None], powers, 0.0)
    unnorm = jnp.einsum(
        "thqk,tkhd->tqhd",
        powers.astype(jnp.bfloat16),
        value_rows,
        preferred_element_type=jnp.float32,
    )
    return (unnorm, jnp.sum(powers, axis=-1))


def tile_backward(queries, grad_unnorm, grad_totals, key_rows, value_rows, visible, factor):
    scores = jnp.einsum("tqhd,tkhd->thqk", queries, key_rows, preferred_element_type=jnp.float32)
    powers = jnp.exp(scores * factor)
    if visible is not None:
        powers = jnp.where(visible[:, None], powers, 0.0)
    grad_powers = (
        jnp.einsum("tqhd,tkhd->thqk", grad_unnorm, value_rows, preferred_element_type=jnp.float32)
        + grad_totals[..., None]
    )
    grad_scores = (powers * grad_powers * factor).astype(jnp.bfloat16)
    grad_queries = jnp.einsum(
        "thqk,tkhd->tqhd", grad_scores, key_rows, preferred_element_type=jnp.float32
    )
    grad_keys = jnp.einsum(
        "thqk,tqhd->tkhd", grad_scores, queries, preferred_element_type=jnp.float32
    )
    grad_values = jnp.einsum(
        "thqk,tqhd->tkhd",
        powers.astype(jnp.bfloat16),
        grad_unnorm,
        preferred_element_type=jnp.float32,
    )
    return (grad_queries, grad_keys, grad_values)


def halves(stacked, half_rows, along):
    return (
        lax.slice_in_dim(stacked, 0, half_rows, axis=along),
        lax.slice_in_dim(stacked, half_rows, 2 * half_rows, axis=along),
    )


def query_stack(later_block, stacked, half_rows, along):
    lower_part, upper_part = halves(stacked, half_rows, along)
    return jnp.stack([upper_part, jnp.where(later_block, lower_part, upper_part)])


def key_stack(later_block, stacked, half_rows, along):
    lower_part, upper_part = halves(stacked, half_rows, along)
    return jnp.stack([lower_part, jnp.where(later_block, lower_part, upper_part)])


def query_spread(later_block, tile_pair, along):
    nothing = jnp.zeros_like(tile_pair[0])
    lower_part = jnp.where(later_block, tile_pair[1], nothing)
    upper_part = tile_pair[0] + jnp.where(later_block, nothing, tile_pair[1])
    return jnp.concatenate([lower_part, upper_part], axis=along)


def key_spread(later_block, tile_pair, along):
    nothing = jnp.zeros_like(tile_pair[0])
    lower_part = tile_pair[0] + jnp.where(later_block, tile_pair[1], nothing)
    upper_part = jnp.where(later_block, nothing, tile_pair[1])
    return jnp.concatenate([lower_part, upper_part], axis=along)


def pair_forward(later_block, queries, key_rows, value_rows, factor):
    half_rows = queries.shape[0] // 2
    unnorm, totals = tile_forward(
        query_stack(later_block, queries, half_rows, 0),
        key_stack(later_block, key_rows, half_rows, 0),
        key_stack(later_block, value_rows, half_rows, 0),
        None,
        factor,
    )
    return (query_spread(later_block, unnorm, 0), query_spread(later_block, totals, 1))


def pair_backward(later_block, queries, grad_unnorm, grad_totals, key_rows, value_rows, factor):
    half_rows = queries.shape[0] // 2
    grads = tile_backward(
        query_stack(later_block, queries, half_rows, 0),
        query_stack(later_block, grad_unnorm, half_rows, 0),
        query_stack(later_block, grad_totals, half_rows, 1),
        key_stack(later_block, key_rows, half_rows, 0),
        key_stack(later_block, value_rows, half_rows, 0),
        None,
        factor,
    )
    return (
        query_spread(later_block, grads[0], 0),
        key_spread(later_block, grads[1], 0),
        key_spread(later_block, grads[2], 0),
    )


def body(
    inputs,
    block_order,
    first_gain,
    first_shift,
    joint_weight,
    query_bias,
    value_bias,
    mixer_weight,
    mixer_bias,
    second_gain,
    second_shift,
    expand_weight,
    expand_bias,
    reduce_weight,
    reduce_bias,
    cotangent,
):
    owned_shards = (
        first_gain,
        first_shift,
        joint_weight,
        query_bias,
        value_bias,
        mixer_weight,
        mixer_bias,
        second_gain,
        second_shift,
        expand_weight,
        expand_bias,
        reduce_weight,
        reduce_bias,
    )
    gathered = (
        lax.all_gather(owned_shards[0], ("dp", "sp"), axis=0, tiled=True),
        lax.all_gather(owned_shards[1], ("dp", "sp"), axis=0, tiled=True),
        lax.all_gather(owned_shards[2], ("dp", "sp"), axis=0, tiled=True),
        lax.all_gather(owned_shards[3], ("dp", "sp"), axis=0, tiled=True),
        lax.all_gather(owned_shards[4], ("dp", "sp"), axis=0, tiled=True),
        lax.all_gather(owned_shards[5], ("dp", "sp"), axis=0, tiled=True),
        lax.all_gather(owned_shards[6], ("dp", "sp"), axis=0, tiled=True),
        lax.all_gather(owned_shards[7], ("dp", "sp"), axis=0, tiled=True),
        lax.all_gather(owned_shards[8], ("dp", "sp"), axis=0, tiled=True),
        lax.all_gather(owned_shards[9], ("dp", "sp"), axis=0, tiled=True),
        lax.all_gather(owned_shards[10], ("dp", "sp"), axis=0, tiled=True),
        lax.all_gather(owned_shards[11], ("dp", "sp"), axis=0, tiled=True),
        lax.all_gather(owned_shards[12], ("dp", "sp"), axis=0, tiled=True),
    )
    (
        gain_one,
        shift_one,
        joint_full,
        query_shift,
        value_shift,
        mixer_full,
        mixer_shift,
        gain_two,
        shift_two,
        expand_full,
        expand_shift,
        reduce_full,
        reduce_shift,
    ) = gathered
    factor = HD ** (-0.5)
    members = lax.axis_size("sp")
    position = lax.axis_index("sp")
    token_rows = inputs[0].astype(jnp.float32)
    row_count = token_rows.shape[0]
    half_rows = row_count // 2
    own_low = block_order[2 * position]
    offsets = jnp.arange(half_rows, dtype=jnp.int32)
    own_places = jnp.concatenate(
        [own_low * half_rows + offsets, block_order[2 * position + 1] * half_rows + offsets]
    )
    visible = (own_places[None, :] <= own_places[:, None])[None]
    normed, first_pull = jax.vjp(
        layer_norm, token_rows, gain_one.astype(jnp.float32), shift_one.astype(jnp.float32)
    )
    normed_low = normed.astype(jnp.bfloat16)
    joint_shift = jnp.concatenate([query_shift, jnp.zeros_like(query_shift), value_shift]).astype(
        jnp.float32
    )
    joint_rows = (product(normed_low, joint_full) + joint_shift).astype(jnp.bfloat16)
    queries = joint_rows[:, :D].reshape(row_count, H, HD)
    key_rows = joint_rows[:, D : 2 * D].reshape(row_count, H, HD)
    value_rows = joint_rows[:, 2 * D :].reshape(row_count, H, HD)
    unnorm, totals = tile_forward(queries[None], key_rows[None], value_rows[None], visible, factor)

    def forward_turn(turn_index, state_in):
        moving_keys, moving_values, unnorm_sum, totals_sum = state_in
        moving_keys, moving_values = passed_along((moving_keys, moving_values), "sp", 1)
        source = (position - turn_index) % members
        later_block = own_low > block_order[2 * source]
        extra_unnorm, extra_totals = pair_forward(
            later_block, queries, moving_keys, moving_values, factor
        )
        return (moving_keys, moving_values, unnorm_sum + extra_unnorm, totals_sum + extra_totals)

    final_state = lax.fori_loop(
        1, members, forward_turn, (key_rows, value_rows, unnorm[0], totals[0])
    )
    unnorm = final_state[2]
    totals_rows = jnp.transpose(final_state[3])
    mixed = unnorm / totals_rows[:, :, None]
    mixed_rows = mixed.reshape(row_count, D).astype(jnp.bfloat16)
    middle = token_rows + (product(mixed_rows, mixer_full) + mixer_shift.astype(jnp.float32))
    second, second_pull = jax.vjp(
        layer_norm, middle, gain_two.astype(jnp.float32), shift_two.astype(jnp.float32)
    )
    second_low = second.astype(jnp.bfloat16)
    before = product(second_low, expand_full) + expand_shift.astype(jnp.float32)
    active, gelu_pull = jax.vjp(gelu_tanh, before)
    active_low = active.astype(jnp.bfloat16)
    result = middle + (product(active_low, reduce_full) + reduce_shift.astype(jnp.float32))
    joint_back, mixer_back, expand_back, reduce_back = (
        lax.all_gather(joint_weight, ("dp", "sp"), axis=0, tiled=True),
        lax.all_gather(mixer_weight, ("dp", "sp"), axis=0, tiled=True),
        lax.all_gather(expand_weight, ("dp", "sp"), axis=0, tiled=True),
        lax.all_gather(reduce_weight, ("dp", "sp"), axis=0, tiled=True),
    )
    upstream = cotangent[0]
    upstream_full = upstream.astype(jnp.float32)
    reduce_gradient = inner_rows(active_low, upstream)
    reduce_shift_gradient = jnp.sum(upstream_full, axis=0)
    grad_active = inner_cols(upstream, reduce_back)
    grad_before = gelu_pull(grad_active)[0].astype(jnp.bfloat16)
    expand_gradient = inner_rows(second_low, grad_before)
    expand_shift_gradient = jnp.sum(grad_before.astype(jnp.float32), axis=0)
    grad_second = inner_cols(grad_before, expand_back)
    grad_middle_norm, gain_two_gradient, shift_two_gradient = second_pull(grad_second)
    grad_middle = upstream_full + grad_middle_norm
    grad_branch = grad_middle.astype(jnp.bfloat16)
    mixer_gradient = inner_rows(mixed_rows, grad_branch)
    mixer_shift_gradient = jnp.sum(grad_branch.astype(jnp.float32), axis=0)
    grad_mixed = inner_cols(grad_branch, mixer_back).astype(jnp.bfloat16).reshape(row_count, H, HD)
    grad_mixed_full = grad_mixed.astype(jnp.float32)
    grad_unnorm = (grad_mixed_full / totals_rows[:, :, None]).astype(jnp.bfloat16)
    grad_totals = jnp.transpose(-jnp.sum(grad_mixed_full * mixed, axis=-1) / totals_rows)
    own_grads = tile_backward(
        queries[None],
        grad_unnorm[None],
        grad_totals[None],
        key_rows[None],
        value_rows[None],
        visible,
        factor,
    )

    def keys_turn(turn_index, state_in):
        moving_keys, moving_values, key_carry, value_carry, query_sum = state_in
        moving_keys, moving_values = passed_along((moving_keys, moving_values), "sp", 1)
        key_carry, value_carry = (
            passed_along(key_carry.astype(jnp.bfloat16), "sp", 1).astype(key_carry.dtype),
            passed_along(value_carry.astype(jnp.bfloat16), "sp", 1).astype(value_carry.dtype),
        )
        source = (position - turn_index) % members
        later_block = own_low > block_order[2 * source]
        extra_query, extra_key, extra_value = pair_backward(
            later_block, queries, grad_unnorm, grad_totals, moving_keys, moving_values, factor
        )
        return (
            moving_keys,
            moving_values,
            key_carry + extra_key,
            value_carry + extra_value,
            query_sum + extra_query,
        )

    final_back = lax.fori_loop(
        1,
        members,
        keys_turn,
        (key_rows, value_rows, own_grads[1][0], own_grads[2][0], own_grads[0][0]),
    )
    key_sum, value_sum = (
        passed_along(final_back[2].astype(jnp.bfloat16), "sp", 1).astype(jnp.float32),
        passed_along(final_back[3].astype(jnp.bfloat16), "sp", 1).astype(jnp.float32),
    )
    query_sum = final_back[4]
    grad_joint = jnp.concatenate(
        [
            query_sum.reshape(row_count, D),
            key_sum.reshape(row_count, D),
            value_sum.reshape(row_count, D),
        ],
        axis=1,
    ).astype(jnp.bfloat16)
    joint_gradient = inner_rows(normed_low, grad_joint)
    joint_sums = jnp.sum(grad_joint.astype(jnp.float32), axis=0)
    query_shift_gradient = joint_sums[:D]
    value_shift_gradient = joint_sums[2 * D :]
    grad_normed = inner_cols(grad_joint, joint_back)
    grad_rows_norm, gain_one_gradient, shift_one_gradient = first_pull(grad_normed)
    input_gradient = (grad_middle + grad_rows_norm).astype(jnp.bfloat16)
    gradient_sums = (
        lax.psum_scatter(gain_one_gradient, ("dp", "sp"), scatter_dimension=0, tiled=True),
        lax.psum_scatter(shift_one_gradient, ("dp", "sp"), scatter_dimension=0, tiled=True),
        lax.psum_scatter(joint_gradient, ("dp", "sp"), scatter_dimension=0, tiled=True),
        lax.psum_scatter(query_shift_gradient, ("dp", "sp"), scatter_dimension=0, tiled=True),
        lax.psum_scatter(value_shift_gradient, ("dp", "sp"), scatter_dimension=0, tiled=True),
        lax.psum_scatter(mixer_gradient, ("dp", "sp"), scatter_dimension=0, tiled=True),
        lax.psum_scatter(mixer_shift_gradient, ("dp", "sp"), scatter_dimension=0, tiled=True),
        lax.psum_scatter(gain_two_gradient, ("dp", "sp"), scatter_dimension=0, tiled=True),
        lax.psum_scatter(shift_two_gradient, ("dp", "sp"), scatter_dimension=0, tiled=True),
        lax.psum_scatter(expand_gradient, ("dp", "sp"), scatter_dimension=0, tiled=True),
        lax.psum_scatter(expand_shift_gradient, ("dp", "sp"), scatter_dimension=0, tiled=True),
        lax.psum_scatter(reduce_gradient, ("dp", "sp"), scatter_dimension=0, tiled=True),
        lax.psum_scatter(reduce_shift_gradient, ("dp", "sp"), scatter_dimension=0, tiled=True),
    )
    return (result.astype(jnp.bfloat16)[None], input_gradient[None]) + tuple(gradient_sums)


def solution(mesh):
    in_specs = (
        P("dp", "sp", None),
        P(),
        P(("dp", "sp")),
        P(("dp", "sp")),
        P(("dp", "sp"), None),
        P(("dp", "sp")),
        P(("dp", "sp")),
        P(("dp", "sp"), None),
        P(("dp", "sp")),
        P(("dp", "sp")),
        P(("dp", "sp")),
        P(("dp", "sp"), None),
        P(("dp", "sp")),
        P(("dp", "sp"), None),
        P(("dp", "sp")),
        P("dp", "sp", None),
    )
    out_specs = (
        P("dp", "sp", None),
        P("dp", "sp", None),
        P(("dp", "sp")),
        P(("dp", "sp")),
        P(("dp", "sp"), None),
        P(("dp", "sp")),
        P(("dp", "sp")),
        P(("dp", "sp"), None),
        P(("dp", "sp")),
        P(("dp", "sp")),
        P(("dp", "sp")),
        P(("dp", "sp"), None),
        P(("dp", "sp")),
        P(("dp", "sp"), None),
        P(("dp", "sp")),
    )
    return jax.shard_map(body, mesh=mesh, in_specs=in_specs, out_specs=out_specs, check_vma=False)
```

profile of v0, /device:TPU:0, one launch (start us, length us, event | category | flops | bytes accessed | tf_op | source)
XLA Modules:
  0.0 1173.2 jit_solution(14329705952864803916)
XLA Ops:
  16.7 42.4 %all-reduce.18 = (bf16[1024]{0:T(1024)(128)(2,1)S(1)}, bf16[1024]{0:T(1024)(128)(2,1)S(1)}, bf16[1024]{0:T(1024)(128)(2,1)S(1)}, bf16[1024]{0:T(1024)(128)(2,1)S...) all-reduce(bf16[1024]{0:T(1024)(128)(2,1)S(1)} %dynamic-update-slic, ...), channel_id=1, replica_groups=mesh['dp'=4,'sp'=8] {'dp','sp'}, use_global_device_ids=true, to_apply=%add.3 | all-reduce | flops 8192 | bytes 32768
  64.5 41.0 %all-gather = bf16[32,1,128]{2,1,0:T(2,128)(2,1)S(1)} all-gather(bf16[1,1,128]{2,1,0:T(2,128)(2,1)} %bitcast.240), channel_id=1, replica_groups=mesh['dp'=4,'sp'=8] {'dp','sp'}, dimensions={0}, use_global_device_ids=true | all-gather | bytes 8448 | tf_op jit(solution)/shard_map/all_gather | solution.py:191
  105.6 4.9 fusion.46
  121.8 185.0 %while.44 = (s32[]{:T(128)}, bf16[256,16,64]{0,2,1:T(8,128)(2,1)}, bf16[256,16,64]{0,2,1:T(8,128)(2,1)}, f32[256,16,64]{0,2,1:T(8,128)S(1)}, f32[16,256]{1,0:T(8...) while((s32[]{:T(128)}, bf16[256,16,64]{0,2,1:T(8,128)(2,1)}, ...), condition=%wide.region_5.6_spmd, body=%wide.region_3.5_spmd.sunk | while | flops 138422288 | bytes 21594524 | solution.py:245
  124.2 11.1 collective-permute-done
  135.3 8.6 collective-permute-done.1
  149.0 8.8 collective-permute-done
  157.7 11.1 collective-permute-done.1
  173.9 8.7 collective-permute-done
  182.6 9.1 collective-permute-done.1
  196.8 9.1 collective-permute-done
  205.9 5.6 collective-permute-done.1
  216.6 19.9 %collective-permute-done = bf16[256,16,64]{0,2,1:T(8,128)(2,1)S(1)} collective-permute-done((bf16[256,16,64]{0,2,1:T(8,128)(2,1)}, bf16[256,16,64]{0,2,1:T(8,128)(2,1)S(1)}, u32[]{:S(2)}, u32[]{:S(2)}) %collective-permute-start) | collective-permute-done | bytes 524320 | tf_op jit(solution)/shard_map/while/body/eval_jaxpr/ppermute | solution.py:17
  236.5 12.3 %collective-permute-done.1 = bf16[256,16,64]{0,2,1:T(8,128)(2,1)S(1)} collective-permute-done((bf16[256,16,64]{0,2,1:T(8,128)(2,1)}, bf16[256,16,64]{0,2,1:T(8,128)(2,1)S(1)}, u32[]{:S(2)}, u32[]{:S(2)}) %collective-permute-start.1) | collective-permute-done | bytes 524320 | tf_op jit(solution)/shard_map/while/body/eval_jaxpr/ppermute | solution.py:17
  253.9 8.7 collective-permute-done
  262.6 10.5 collective-permute-done.1
  278.1 13.6 %collective-permute-done = bf16[256,16,64]{0,2,1:T(8,128)(2,1)S(1)} collective-permute-done((bf16[256,16,64]{0,2,1:T(8,128)(2,1)}, bf16[256,16,64]{0,2,1:T(8,128)(2,1)S(1)}, u32[]{:S(2)}, u32[]{:S(2)}) %collective-permute-start) | collective-permute-done | bytes 524320 | tf_op jit(solution)/shard_map/while/body/eval_jaxpr/ppermute | solution.py:17
  291.7 12.0 %collective-permute-done.1 = bf16[256,16,64]{0,2,1:T(8,128)(2,1)S(1)} collective-permute-done((bf16[256,16,64]{0,2,1:T(8,128)(2,1)}, bf16[256,16,64]{0,2,1:T(8,128)(2,1)S(1)}, u32[]{:S(2)}, u32[]{:S(2)}) %collective-permute-start.1) | collective-permute-done | bytes 524320 | tf_op jit(solution)/shard_map/while/body/eval_jaxpr/ppermute | solution.py:17
  310.6 8.1 convolution_add_fusion
  318.7 16.5 %all-gather.12.cloned.1.call-done = bf16[4096,1024]{1,0:T(8,128)(2,1)} async-done(((bf16[128,1024]{1,0:T(8,128)(2,1)}), bf16[4096,1024]{1,0:T(8,128)(2,1)}) %all-gather.12.cloned.1.call-update) | async-done | bytes 8388624 | tf_op jit(solution)/shard_map/all_gather | solution.py:192
  335.1 11.9 %convert_reduce_fusion = (f32[4096]{0:T(1024)S(1)}, bf16[256,4096]{1,0:T(8,128)(2,1)S(1)}) fusion(f32[256,4096]{1,0:T(8,128)} %convolution_add_fusion, bf16[4096,1024]{1,0:T(8,128)(2,1)} %all-gather.12.cloned.1.call-done, bf16[1,256,1024]{2,1,0:T(8,128)(2,1)S(1)} %copy-done.9), kind=kOutput, calls=%fused_computation.89 | convolution fusion | flops 2170548224 | bytes 15220736 | tf_op jit(solution)/shard_map/dot_general | solution.py:42
  368.9 243.1 %while.45 = (s32[]{:T(128)}, bf16[256,16,64]{0,2,1:T(8,128)(2,1)}, bf16[256,16,64]{0,2,1:T(8,128)(2,1)}, bf16[256,16,64]{0,2,1:T(8,128)(2,1)}, bf16[256,16,64]{0...) while((s32[]{:T(128)}, bf16[256,16,64]{0,2,1:T(8,128)(2,1)}, ...), condition=%wide.region_12.13_spmd, body=%wide.region_11.12_spmd.sunk | while | flops 345380864 | bytes 44646916 | solution.py:315
  373.7 8.5 collective-permute-done.2
  383.2 8.1 collective-permute-done.3
  402.0 6.3 collective-permute-done.5
  412.5 11.4 collective-permute-done.2
  424.8 7.6 collective-permute-done.3
  443.2 6.3 collective-permute-done.5
  453.6 11.4 collective-permute-done.2
  466.0 7.6 collective-permute-done.3
  484.4 6.3 collective-permute-done.5
  494.8 9.6 collective-permute-done.2
  525.5 8.5 collective-permute-done.2
  555.0 8.5 collective-permute-done.2
  564.5 4.7 collective-permute-done.3
  584.6 8.5 collective-permute-done.2
  594.1 4.7 collective-permute-done.3
  612.3 10.4 collective-permute-done.7
  622.7 5.6 collective-permute-done.6
  628.3 7.6 fusion.83
  637.1 10.7 fusion.88
  648.9 11.8 %fusion.68 = f32[4096,1024]{1,0:T(8,128)} fusion(bf16[1,256,1024]{2,1,0:T(8,128)(2,1)S(1)} %copy-done.10, f32[256,4096]{1,0:T(8,128)} %convolution_add_fusion), kind=kOutput, calls=%fused_computation.139 | convolution fusion | flops 2156920832 | bytes 21495808 | tf_op jit(solution)/shard_map/dot_general | solution.py:36
  661.4 8.9 fusion.58
  670.9 5.2 fusion.89
  678.0 40.9 %all-reduce.17 = (f32[1024]{0:T(1024)S(1)}, f32[1024]{0:T(1024)S(1)}, f32[1024]{0:T(1024)S(1)}, f32[1024]{0:T(1024)S(1)}, f32[1024]{0:T(1024)S(1)}, /*index=5*/f...) all-reduce(f32[1024]{0:T(1024)S(1)} %get-tuple-element.554, ...), channel_id=2, replica_groups=mesh['dp'=4,'sp'=8] {'dp','sp'}, use_global_device_ids=true, to_apply=%region_16.17.clone | all-reduce | flops 12288 | bytes 98304
  724.2 65.8 %reduce-scatter.5.cloned.1.call-done = f32[32,3072]{1,0:T(8,128)} async-done(((f32[1024,3072]{1,0:T(8,128)}), f32[32,3072]{1,0:T(8,128)}) %reduce-scatter.5.cloned.1.call-update) | async-done | bytes 393232 | tf_op jit(solution)/shard_map/reduce_scatter | solution.py:344
  790.0 188.7 %reduce-scatter.9.cloned.1.call-done = f32[32,4096]{1,0:T(8,128)} async-done(((f32[1024,4096]{1,0:T(8,128)}), f32[32,4096]{1,0:T(8,128)}) %reduce-scatter.9.cloned.1.call-update) | async-done | bytes 524304 | tf_op jit(solution)/shard_map/reduce_scatter | solution.py:351
  978.8 187.4 %reduce-scatter.11.cloned.1.call-done = f32[128,1024]{1,0:T(8,128)} async-done(((f32[4096,1024]{1,0:T(8,128)}), f32[128,1024]{1,0:T(8,128)}) %reduce-scatter.11.cloned.1.call-update) | async-done | bytes 524304 | tf_op jit(solution)/shard_map/reduce_scatter | solution.py:353
  (401 shorter events, 202.8 us)
Async XLA Ops:
  7.2 98.4 %all-gather.6.cloned.1.call-start = ((), (), s32[]{:S(2)}) async-start(), calls=%async_computation.4 | async-start | bytes 6488064 | tf_op jit(solution)/shard_map/all_gather | solution.py:183
  7.9 299.8 %all-gather.8.cloned.1.call-start = ((), (), s32[]{:S(2)}) async-start(), calls=%async_computation.5 | async-start | bytes 2162688 | tf_op jit(solution)/shard_map/all_gather | solution.py:186
  8.7 301.9 %all-gather.10.cloned.1.call-start = ((), (), s32[]{:S(2)}) async-start(), calls=%async_computation.6 | async-start | bytes 8650752 | tf_op jit(solution)/shard_map/all_gather | solution.py:190
  9.4 325.7 %all-gather.12.cloned.1.call-start = ((), (), s32[]{:S(2)}) async-start(), calls=%async_computation.7 | async-start | bytes 8650752 | tf_op jit(solution)/shard_map/all_gather | solution.py:192
  10.0 714.3 %reduce-scatter.7.cloned.1.call-start = ((), (), s32[]{:S(2)}) async-start(), calls=%async_computation.9 | async-start | bytes 4325376 | tf_op jit(solution)/shard_map/reduce_scatter | solution.py:347
  121.8 13.5 %collective-permute-start = (bf16[256,16,64]{0,2,1:T(8,128)(2,1)}, bf16[256,16,64]{0,2,1:T(8,128)(2,1)S(1)}, u32[]{:S(2)}, u32[]{:S(2)}) collective-permute-start(bf16[256,16,64]{0,2,1:T(8,128)(2,1)} %get-tuple-element.875), channel_id=1, source_target_pairs={{0,1},{1,2},{2,3},{3,4},{4,5},{5,6},{6,7},{7,0},{8,9},{9,10},{10,1... | collective-permute-start | bytes 1572872 | tf_op jit(solution)/shard_map/while/body/eval_jaxpr/ppermute | solution.py:17
  122.2 21.7 %collective-permute-start.1 = (bf16[256,16,64]{0,2,1:T(8,128)(2,1)}, bf16[256,16,64]{0,2,1:T(8,128)(2,1)S(1)}, u32[]{:S(2)}, u32[]{:S(2)}) collective-permute-start(bf16[256,16,64]{0,2,1:T(8,128)(2,1)} %get-tuple-element.876), channel_id=1, source_target_pairs={{0,1},{1,2},{2,3},{3,4},{4,5},{5,6},{6,7},{7,0},{8,9},{9,10},{10,1... | collective-permute-start | bytes 1572872 | tf_op jit(solution)/shard_map/while/body/eval_jaxpr/ppermute | solution.py:17
  147.0 10.7 collective-permute-start
  147.0 21.8 %collective-permute-start.1 = (bf16[256,16,64]{0,2,1:T(8,128)(2,1)}, bf16[256,16,64]{0,2,1:T(8,128)(2,1)S(1)}, u32[]{:S(2)}, u32[]{:S(2)}) collective-permute-start(bf16[256,16,64]{0,2,1:T(8,128)(2,1)} %get-tuple-element.876), channel_id=1, source_target_pairs={{0,1},{1,2},{2,3},{3,4},{4,5},{5,6},{6,7},{7,0},{8,9},{9,10},{10,1... | collective-permute-start | bytes 1572872 | tf_op jit(solution)/shard_map/while/body/eval_jaxpr/ppermute | solution.py:17
  172.0 10.6 collective-permute-start
  172.0 19.7 %collective-permute-start.1 = (bf16[256,16,64]{0,2,1:T(8,128)(2,1)}, bf16[256,16,64]{0,2,1:T(8,128)(2,1)S(1)}, u32[]{:S(2)}, u32[]{:S(2)}) collective-permute-start(bf16[256,16,64]{0,2,1:T(8,128)(2,1)} %get-tuple-element.876), channel_id=1, source_target_pairs={{0,1},{1,2},{2,3},{3,4},{4,5},{5,6},{6,7},{7,0},{8,9},{9,10},{10,1... | collective-permute-start | bytes 1572872 | tf_op jit(solution)/shard_map/while/body/eval_jaxpr/ppermute | solution.py:17
  194.8 11.1 collective-permute-start
  194.8 16.7 %collective-permute-start.1 = (bf16[256,16,64]{0,2,1:T(8,128)(2,1)}, bf16[256,16,64]{0,2,1:T(8,128)(2,1)S(1)}, u32[]{:S(2)}, u32[]{:S(2)}) collective-permute-start(bf16[256,16,64]{0,2,1:T(8,128)(2,1)} %get-tuple-element.876), channel_id=1, source_target_pairs={{0,1},{1,2},{2,3},{3,4},{4,5},{5,6},{6,7},{7,0},{8,9},{9,10},{10,1... | collective-permute-start | bytes 1572872 | tf_op jit(solution)/shard_map/while/body/eval_jaxpr/ppermute | solution.py:17
  214.7 21.8 %collective-permute-start = (bf16[256,16,64]{0,2,1:T(8,128)(2,1)}, bf16[256,16,64]{0,2,1:T(8,128)(2,1)S(1)}, u32[]{:S(2)}, u32[]{:S(2)}) collective-permute-start(bf16[256,16,64]{0,2,1:T(8,128)(2,1)} %get-tuple-element.875), channel_id=1, source_target_pairs={{0,1},{1,2},{2,3},{3,4},{4,5},{5,6},{6,7},{7,0},{8,9},{9,10},{10,1... | collective-permute-start | bytes 1572872 | tf_op jit(solution)/shard_map/while/body/eval_jaxpr/ppermute | solution.py:17
  214.7 34.2 %collective-permute-start.1 = (bf16[256,16,64]{0,2,1:T(8,128)(2,1)}, bf16[256,16,64]{0,2,1:T(8,128)(2,1)S(1)}, u32[]{:S(2)}, u32[]{:S(2)}) collective-permute-start(bf16[256,16,64]{0,2,1:T(8,128)(2,1)} %get-tuple-element.876), channel_id=1, source_target_pairs={{0,1},{1,2},{2,3},{3,4},{4,5},{5,6},{6,7},{7,0},{8,9},{9,10},{10,1... | collective-permute-start | bytes 1572872 | tf_op jit(solution)/shard_map/while/body/eval_jaxpr/ppermute | solution.py:17
  251.9 10.6 collective-permute-start
  251.9 21.1 %collective-permute-start.1 = (bf16[256,16,64]{0,2,1:T(8,128)(2,1)}, bf16[256,16,64]{0,2,1:T(8,128)(2,1)S(1)}, u32[]{:S(2)}, u32[]{:S(2)}) collective-permute-start(bf16[256,16,64]{0,2,1:T(8,128)(2,1)} %get-tuple-element.876), channel_id=1, source_target_pairs={{0,1},{1,2},{2,3},{3,4},{4,5},{5,6},{6,7},{7,0},{8,9},{9,10},{10,1... | collective-permute-start | bytes 1572872 | tf_op jit(solution)/shard_map/while/body/eval_jaxpr/ppermute | solution.py:17
  276.2 15.5 %collective-permute-start = (bf16[256,16,64]{0,2,1:T(8,128)(2,1)}, bf16[256,16,64]{0,2,1:T(8,128)(2,1)S(1)}, u32[]{:S(2)}, u32[]{:S(2)}) collective-permute-start(bf16[256,16,64]{0,2,1:T(8,128)(2,1)} %get-tuple-element.875), channel_id=1, source_target_pairs={{0,1},{1,2},{2,3},{3,4},{4,5},{5,6},{6,7},{7,0},{8,9},{9,10},{10,1... | collective-permute-start | bytes 1572872 | tf_op jit(solution)/shard_map/while/body/eval_jaxpr/ppermute | solution.py:17
  276.2 27.5 %collective-permute-start.1 = (bf16[256,16,64]{0,2,1:T(8,128)(2,1)}, bf16[256,16,64]{0,2,1:T(8,128)(2,1)S(1)}, u32[]{:S(2)}, u32[]{:S(2)}) collective-permute-start(bf16[256,16,64]{0,2,1:T(8,128)(2,1)} %get-tuple-element.876), channel_id=1, source_target_pairs={{0,1},{1,2},{2,3},{3,4},{4,5},{5,6},{6,7},{7,0},{8,9},{9,10},{10,1... | collective-permute-start | bytes 1572872 | tf_op jit(solution)/shard_map/while/body/eval_jaxpr/ppermute | solution.py:17
  368.9 421.1 %reduce-scatter.5.cloned.1.call-start = ((), (), s32[]{:S(2)}) async-start(), calls=%async_computation.8 | async-start | bytes 12976128 | tf_op jit(solution)/shard_map/reduce_scatter | solution.py:344
  368.9 13.3 %collective-permute-start.2 = (bf16[256,16,64]{0,2,1:T(8,128)(2,1)}, bf16[256,16,64]{0,2,1:T(8,128)(2,1)S(1)}, u32[]{:S(2)}, u32[]{:S(2)}) collective-permute-start(bf16[256,16,64]{0,2,1:T(8,128)(2,1)} %get-tuple-element.923), channel_id=1, source_target_pairs={{0,1},{1,2},{2,3},{3,4},{4,5},{5,6},{6,7},{7,0},{8,9},{9,10},{10,1... | collective-permute-start | bytes 1572872 | tf_op jit(solution)/shard_map/while/body/eval_jaxpr/ppermute | solution.py:17
  369.3 22.0 %collective-permute-start.3 = (bf16[256,16,64]{0,2,1:T(8,128)(2,1)}, bf16[256,16,64]{0,2,1:T(8,128)(2,1)S(1)}, u32[]{:S(2)}, u32[]{:S(2)}) collective-permute-start(bf16[256,16,64]{0,2,1:T(8,128)(2,1)} %get-tuple-element.924), channel_id=1, source_target_pairs={{0,1},{1,2},{2,3},{3,4},{4,5},{5,6},{6,7},{7,0},{8,9},{9,10},{10,1... | collective-permute-start | bytes 1572872 | tf_op jit(solution)/shard_map/while/body/eval_jaxpr/ppermute | solution.py:17
  370.6 29.2 %collective-permute-start.4 = (bf16[256,16,64]{0,2,1:T(8,128)(2,1)}, bf16[256,16,64]{0,2,1:T(8,128)(2,1)}, u32[]{:S(2)}, u32[]{:S(2)}) collective-permute-start(bf16[256,16,64]{0,2,1:T(8,128)(2,1)} %get-tuple-element.925), channel_id=1, source_target_pairs={{0,1},{1,2},{2,3},{3,4},{4,5},{5,6},{6,7},{7,0},{8,9},{9,10},{10,1... | collective-permute-start | bytes 1572872 | tf_op jit(solution)/shard_map/while/body/eval_jaxpr/ppermute | solution.py:17
  370.9 37.5 %collective-permute-start.5 = (bf16[256,16,64]{0,2,1:T(8,128)(2,1)}, bf16[256,16,64]{0,2,1:T(8,128)(2,1)}, u32[]{:S(2)}, u32[]{:S(2)}) collective-permute-start(bf16[256,16,64]{0,2,1:T(8,128)(2,1)} %get-tuple-element.926), channel_id=1, source_target_pairs={{0,1},{1,2},{2,3},{3,4},{4,5},{5,6},{6,7},{7,0},{8,9},{9,10},{10,1... | collective-permute-start | bytes 1572872 | tf_op jit(solution)/shard_map/while/body/eval_jaxpr/ppermute | solution.py:17
  410.4 13.5 %collective-permute-start.2 = (bf16[256,16,64]{0,2,1:T(8,128)(2,1)}, bf16[256,16,64]{0,2,1:T(8,128)(2,1)S(1)}, u32[]{:S(2)}, u32[]{:S(2)}) collective-permute-start(bf16[256,16,64]{0,2,1:T(8,128)(2,1)} %get-tuple-element.923), channel_id=1, source_target_pairs={{0,1},{1,2},{2,3},{3,4},{4,5},{5,6},{6,7},{7,0},{8,9},{9,10},{10,1... | collective-permute-start | bytes 1572872 | tf_op jit(solution)/shard_map/while/body/eval_jaxpr/ppermute | solution.py:17
  410.4 22.0 %collective-permute-start.3 = (bf16[256,16,64]{0,2,1:T(8,128)(2,1)}, bf16[256,16,64]{0,2,1:T(8,128)(2,1)S(1)}, u32[]{:S(2)}, u32[]{:S(2)}) collective-permute-start(bf16[256,16,64]{0,2,1:T(8,128)(2,1)} %get-tuple-element.924), channel_id=1, source_target_pairs={{0,1},{1,2},{2,3},{3,4},{4,5},{5,6},{6,7},{7,0},{8,9},{9,10},{10,1... | collective-permute-start | bytes 1572872 | tf_op jit(solution)/shard_map/while/body/eval_jaxpr/ppermute | solution.py:17
  410.4 30.6 %collective-permute-start.4 = (bf16[256,16,64]{0,2,1:T(8,128)(2,1)}, bf16[256,16,64]{0,2,1:T(8,128)(2,1)}, u32[]{:S(2)}, u32[]{:S(2)}) collective-permute-start(bf16[256,16,64]{0,2,1:T(8,128)(2,1)} %get-tuple-element.925), channel_id=1, source_target_pairs={{0,1},{1,2},{2,3},{3,4},{4,5},{5,6},{6,7},{7,0},{8,9},{9,10},{10,1... | collective-permute-start | bytes 1572872 | tf_op jit(solution)/shard_map/while/body/eval_jaxpr/ppermute | solution.py:17
  410.4 39.1 %collective-permute-start.5 = (bf16[256,16,64]{0,2,1:T(8,128)(2,1)}, bf16[256,16,64]{0,2,1:T(8,128)(2,1)}, u32[]{:S(2)}, u32[]{:S(2)}) collective-permute-start(bf16[256,16,64]{0,2,1:T(8,128)(2,1)} %get-tuple-element.926), channel_id=1, source_target_pairs={{0,1},{1,2},{2,3},{3,4},{4,5},{5,6},{6,7},{7,0},{8,9},{9,10},{10,1... | collective-permute-start | bytes 1572872 | tf_op jit(solution)/shard_map/while/body/eval_jaxpr/ppermute | solution.py:17
  451.5 13.5 %collective-permute-start.2 = (bf16[256,16,64]{0,2,1:T(8,128)(2,1)}, bf16[256,16,64]{0,2,1:T(8,128)(2,1)S(1)}, u32[]{:S(2)}, u32[]{:S(2)}) collective-permute-start(bf16[256,16,64]{0,2,1:T(8,128)(2,1)} %get-tuple-element.923), channel_id=1, source_target_pairs={{0,1},{1,2},{2,3},{3,4},{4,5},{5,6},{6,7},{7,0},{8,9},{9,10},{10,1... | collective-permute-start | bytes 1572872 | tf_op jit(solution)/shard_map/while/body/eval_jaxpr/ppermute | solution.py:17
  451.5 22.1 %collective-permute-start.3 = (bf16[256,16,64]{0,2,1:T(8,128)(2,1)}, bf16[256,16,64]{0,2,1:T(8,128)(2,1)S(1)}, u32[]{:S(2)}, u32[]{:S(2)}) collective-permute-start(bf16[256,16,64]{0,2,1:T(8,128)(2,1)} %get-tuple-element.924), channel_id=1, source_target_pairs={{0,1},{1,2},{2,3},{3,4},{4,5},{5,6},{6,7},{7,0},{8,9},{9,10},{10,1... | collective-permute-start | bytes 1572872 | tf_op jit(solution)/shard_map/while/body/eval_jaxpr/ppermute | solution.py:17
  451.5 30.6 %collective-permute-start.4 = (bf16[256,16,64]{0,2,1:T(8,128)(2,1)}, bf16[256,16,64]{0,2,1:T(8,128)(2,1)}, u32[]{:S(2)}, u32[]{:S(2)}) collective-permute-start(bf16[256,16,64]{0,2,1:T(8,128)(2,1)} %get-tuple-element.925), channel_id=1, source_target_pairs={{0,1},{1,2},{2,3},{3,4},{4,5},{5,6},{6,7},{7,0},{8,9},{9,10},{10,1... | collective-permute-start | bytes 1572872 | tf_op jit(solution)/shard_map/while/body/eval_jaxpr/ppermute | solution.py:17
  451.5 39.2 %collective-permute-start.5 = (bf16[256,16,64]{0,2,1:T(8,128)(2,1)}, bf16[256,16,64]{0,2,1:T(8,128)(2,1)}, u32[]{:S(2)}, u32[]{:S(2)}) collective-permute-start(bf16[256,16,64]{0,2,1:T(8,128)(2,1)} %get-tuple-element.926), channel_id=1, source_target_pairs={{0,1},{1,2},{2,3},{3,4},{4,5},{5,6},{6,7},{7,0},{8,9},{9,10},{10,1... | collective-permute-start | bytes 1572872 | tf_op jit(solution)/shard_map/while/body/eval_jaxpr/ppermute | solution.py:17
  492.7 11.7 collective-permute-start.2
  492.7 17.3 %collective-permute-start.3 = (bf16[256,16,64]{0,2,1:T(8,128)(2,1)}, bf16[256,16,64]{0,2,1:T(8,128)(2,1)S(1)}, u32[]{:S(2)}, u32[]{:S(2)}) collective-permute-start(bf16[256,16,64]{0,2,1:T(8,128)(2,1)} %get-tuple-element.924), channel_id=1, source_target_pairs={{0,1},{1,2},{2,3},{3,4},{4,5},{5,6},{6,7},{7,0},{8,9},{9,10},{10,1... | collective-permute-start | bytes 1572872 | tf_op jit(solution)/shard_map/while/body/eval_jaxpr/ppermute | solution.py:17
  492.7 23.0 %collective-permute-start.4 = (bf16[256,16,64]{0,2,1:T(8,128)(2,1)}, bf16[256,16,64]{0,2,1:T(8,128)(2,1)}, u32[]{:S(2)}, u32[]{:S(2)}) collective-permute-start(bf16[256,16,64]{0,2,1:T(8,128)(2,1)} %get-tuple-element.925), channel_id=1, source_target_pairs={{0,1},{1,2},{2,3},{3,4},{4,5},{5,6},{6,7},{7,0},{8,9},{9,10},{10,1... | collective-permute-start | bytes 1572872 | tf_op jit(solution)/shard_map/while/body/eval_jaxpr/ppermute | solution.py:17
  492.7 28.6 %collective-permute-start.5 = (bf16[256,16,64]{0,2,1:T(8,128)(2,1)}, bf16[256,16,64]{0,2,1:T(8,128)(2,1)}, u32[]{:S(2)}, u32[]{:S(2)}) collective-permute-start(bf16[256,16,64]{0,2,1:T(8,128)(2,1)} %get-tuple-element.926), channel_id=1, source_target_pairs={{0,1},{1,2},{2,3},{3,4},{4,5},{5,6},{6,7},{7,0},{8,9},{9,10},{10,1... | collective-permute-start | bytes 1572872 | tf_op jit(solution)/shard_map/while/body/eval_jaxpr/ppermute | solution.py:17
  523.4 16.2 %collective-permute-start.3 = (bf16[256,16,64]{0,2,1:T(8,128)(2,1)}, bf16[256,16,64]{0,2,1:T(8,128)(2,1)S(1)}, u32[]{:S(2)}, u32[]{:S(2)}) collective-permute-start(bf16[256,16,64]{0,2,1:T(8,128)(2,1)} %get-tuple-element.924), channel_id=1, source_target_pairs={{0,1},{1,2},{2,3},{3,4},{4,5},{5,6},{6,7},{7,0},{8,9},{9,10},{10,1... | collective-permute-start | bytes 1572872 | tf_op jit(solution)/shard_map/while/body/eval_jaxpr/ppermute | solution.py:17
  523.4 21.9 %collective-permute-start.4 = (bf16[256,16,64]{0,2,1:T(8,128)(2,1)}, bf16[256,16,64]{0,2,1:T(8,128)(2,1)}, u32[]{:S(2)}, u32[]{:S(2)}) collective-permute-start(bf16[256,16,64]{0,2,1:T(8,128)(2,1)} %get-tuple-element.925), channel_id=1, source_target_pairs={{0,1},{1,2},{2,3},{3,4},{4,5},{5,6},{6,7},{7,0},{8,9},{9,10},{10,1... | collective-permute-start | bytes 1572872 | tf_op jit(solution)/shard_map/while/body/eval_jaxpr/ppermute | solution.py:17
  523.4 27.6 %collective-permute-start.5 = (bf16[256,16,64]{0,2,1:T(8,128)(2,1)}, bf16[256,16,64]{0,2,1:T(8,128)(2,1)}, u32[]{:S(2)}, u32[]{:S(2)}) collective-permute-start(bf16[256,16,64]{0,2,1:T(8,128)(2,1)} %get-tuple-element.926), channel_id=1, source_target_pairs={{0,1},{1,2},{2,3},{3,4},{4,5},{5,6},{6,7},{7,0},{8,9},{9,10},{10,1... | collective-permute-start | bytes 1572872 | tf_op jit(solution)/shard_map/while/body/eval_jaxpr/ppermute | solution.py:17
  552.9 16.2 %collective-permute-start.3 = (bf16[256,16,64]{0,2,1:T(8,128)(2,1)}, bf16[256,16,64]{0,2,1:T(8,128)(2,1)S(1)}, u32[]{:S(2)}, u32[]{:S(2)}) collective-permute-start(bf16[256,16,64]{0,2,1:T(8,128)(2,1)} %get-tuple-element.924), channel_id=1, source_target_pairs={{0,1},{1,2},{2,3},{3,4},{4,5},{5,6},{6,7},{7,0},{8,9},{9,10},{10,1... | collective-permute-start | bytes 1572872 | tf_op jit(solution)/shard_map/while/body/eval_jaxpr/ppermute | solution.py:17
  552.9 21.9 %collective-permute-start.4 = (bf16[256,16,64]{0,2,1:T(8,128)(2,1)}, bf16[256,16,64]{0,2,1:T(8,128)(2,1)}, u32[]{:S(2)}, u32[]{:S(2)}) collective-permute-start(bf16[256,16,64]{0,2,1:T(8,128)(2,1)} %get-tuple-element.925), channel_id=1, source_target_pairs={{0,1},{1,2},{2,3},{3,4},{4,5},{5,6},{6,7},{7,0},{8,9},{9,10},{10,1... | collective-permute-start | bytes 1572872 | tf_op jit(solution)/shard_map/while/body/eval_jaxpr/ppermute | solution.py:17
  553.0 27.6 %collective-permute-start.5 = (bf16[256,16,64]{0,2,1:T(8,128)(2,1)}, bf16[256,16,64]{0,2,1:T(8,128)(2,1)}, u32[]{:S(2)}, u32[]{:S(2)}) collective-permute-start(bf16[256,16,64]{0,2,1:T(8,128)(2,1)} %get-tuple-element.926), channel_id=1, source_target_pairs={{0,1},{1,2},{2,3},{3,4},{4,5},{5,6},{6,7},{7,0},{8,9},{9,10},{10,1... | collective-permute-start | bytes 1572872 | tf_op jit(solution)/shard_map/while/body/eval_jaxpr/ppermute | solution.py:17
  582.5 16.2 %collective-permute-start.3 = (bf16[256,16,64]{0,2,1:T(8,128)(2,1)}, bf16[256,16,64]{0,2,1:T(8,128)(2,1)S(1)}, u32[]{:S(2)}, u32[]{:S(2)}) collective-permute-start(bf16[256,16,64]{0,2,1:T(8,128)(2,1)} %get-tuple-element.924), channel_id=1, source_target_pairs={{0,1},{1,2},{2,3},{3,4},{4,5},{5,6},{6,7},{7,0},{8,9},{9,10},{10,1... | collective-permute-start | bytes 1572872 | tf_op jit(solution)/shard_map/while/body/eval_jaxpr/ppermute | solution.py:17
  582.5 21.9 %collective-permute-start.4 = (bf16[256,16,64]{0,2,1:T(8,128)(2,1)}, bf16[256,16,64]{0,2,1:T(8,128)(2,1)}, u32[]{:S(2)}, u32[]{:S(2)}) collective-permute-start(bf16[256,16,64]{0,2,1:T(8,128)(2,1)} %get-tuple-element.925), channel_id=1, source_target_pairs={{0,1},{1,2},{2,3},{3,4},{4,5},{5,6},{6,7},{7,0},{8,9},{9,10},{10,1... | collective-permute-start | bytes 1572872 | tf_op jit(solution)/shard_map/while/body/eval_jaxpr/ppermute | solution.py:17
  582.5 27.6 %collective-permute-start.5 = (bf16[256,16,64]{0,2,1:T(8,128)(2,1)}, bf16[256,16,64]{0,2,1:T(8,128)(2,1)}, u32[]{:S(2)}, u32[]{:S(2)}) collective-permute-start(bf16[256,16,64]{0,2,1:T(8,128)(2,1)} %get-tuple-element.926), channel_id=1, source_target_pairs={{0,1},{1,2},{2,3},{3,4},{4,5},{5,6},{6,7},{7,0},{8,9},{9,10},{10,1... | collective-permute-start | bytes 1572872 | tf_op jit(solution)/shard_map/while/body/eval_jaxpr/ppermute | solution.py:17
  612.1 16.2 %collective-permute-start.6 = (bf16[256,16,64]{0,2,1:T(8,128)(2,1)}, bf16[256,16,64]{0,2,1:T(8,128)(2,1)S(1)}, u32[]{:S(2)}, u32[]{:S(2)}) collective-permute-start(bf16[256,16,64]{0,2,1:T(8,128)(2,1)} %get-tuple-element.529), channel_id=1, source_target_pairs={{0,1},{1,2},{2,3},{3,4},{4,5},{5,6},{6,7},{7,0},{8,9},{9,10},{10,1... | collective-permute-start | bytes 1572872 | tf_op jit(solution)/shard_map/ppermute | solution.py:17
  635.9 342.9 %reduce-scatter.9.cloned.1.call-start = ((), (), s32[]{:S(2)}) async-start(), calls=%async_computation.10 | async-start | bytes 17301504 | tf_op jit(solution)/shard_map/reduce_scatter | solution.py:351
  647.9 518.3 %reduce-scatter.11.cloned.1.call-start = ((), (), s32[]{:S(2)}) async-start(), calls=%async_computation.11 | async-start | bytes 17301504 | tf_op jit(solution)/shard_map/reduce_scatter | solution.py:353
  (23 other events, 399.3 us)
Sparse Core Ops, SparseCore 0:
  11.0 72.3 all-gather.5
  86.4 59.3 all-gather.7
  148.7 98.1 all-gather.9
  249.8 85.2 all-gather.11
  369.0 155.7 reduce-scatter.6
  636.0 153.9 reduce-scatter.4
  793.0 185.7 reduce-scatter.8
  981.7 184.3 reduce-scatter.10
where the time goes:
time: 1180 us; the launch traced here: 1170 us
  waiting for transfers between devices  785 us (67%)
  blocking collectives  124 us (11%)
  matrix products  124 us (11%)
  local copies, waits for them, and re-layouts  54.7 us (5%)
  other arithmetic  45.4 us (4%)
  loops' own time  19.3 us (2%)
  between operations  16.1 us (1%)
    ppermute x44, waiting for transfers between devices, passed_along(): return lax.ppermute(value, axis, pairs)  324 us
    reduce_scatter x1, waiting for transfers between devices, body(): lax.psum_scatter(expand_gradient, ('dp', 'sp'), scatter_dimension=0, tile...  189 us
    reduce_scatter x1, waiting for transfers between devices, body(): lax.psum_scatter(reduce_gradient, ('dp', 'sp'), scatter_dimension=0, tile...  187 us
    unnamed x2, blocking collectives  83.4 us
    reduce_scatter x1, waiting for transfers between devices, body(): lax.psum_scatter(joint_gradient, ('dp', 'sp'), scatter_dimension=0, tiled...  65.8 us
    all_gather x1, blocking collectives, body(): lax.all_gather(owned_shards[10], ('dp', 'sp'), axis=0, tiled=True)  41 us
    dot_general x4, matrix products, inner_rows(): lax.dot_general(left, right, (((0,), (0,)), ((), ())), preferred_element_...  32.8 us
    dot_general x4, matrix products, product(): return jnp.dot(left, right, preferred_element_type=jnp.float32)  24.5 us
  transfers between devices with their start and end apart: 52, of which 48 were waited for; matrix products, arithmetic and copies ran while one was open for 16% of the time, Pallas kernels for 0%

commit v1 on v0

--- a/solution.py
+++ b/solution.py
@@ -1,6 +1,8 @@
 import jax
 import jax.numpy as jnp
 from jax import lax
+from jax.experimental import pallas as pl
+from jax.experimental.pallas import tpu as pltpu
 from jax.sharding import PartitionSpec as P
 
 D = 1024
@@ -144,7 +146,7 @@
     )
 
 
-def body(
+def ring_body(
     inputs,
     block_order,
     first_gain,
@@ -356,6 +358,571 @@
     return (result.astype(jnp.bfloat16)[None], input_gradient[None]) + tuple(gradient_sums)
 
 
+ALL = ("dp", "sp")
+CORE_BIT = 1
+Z_BITS = (0, 2, 4, 6)
+X_BIT = 8
+Y_BIT = 16
+TILE = 512
+BLOCK_ROWS = 128
+
+
+def swapped(value, mask):
+    count = lax.axis_size("dp") * lax.axis_size("sp")
+    return lax.ppermute(value, ALL, [(source, source ^ mask) for source in range(count)])
+
+
+def placed_kernel(slot_ref, *refs, col_blocks):
+    pieces, out_ref, sem = refs[:16], refs[16], refs[17]
+    width = pieces[0].shape[1] // col_blocks
+    copies = []
+    for at in range(16):
+        row = slot_ref[at]
+        for col in range(col_blocks):
+            if col_blocks == 1:
+                target = out_ref.at[row]
+                source = pieces[at]
+            else:
+                source = pieces[at].at[:, pl.ds(col * width, width)]
+                to = pl.multiple_of(slot_ref[16 + col] * width, 128)
+                target = out_ref.at[row, :, pl.ds(to, width)]
+            copy = pltpu.make_async_copy(source, target, sem.at[at * col_blocks + col])
+            copy.start()
+            copies.append(copy)
+    for copy in copies:
+        copy.wait()
+
+
+def placed(pieces, slots, col_blocks=1):
+    rows, cols = pieces[0].shape
+    return pl.pallas_call(
+        lambda *refs: placed_kernel(*refs, col_blocks=col_blocks),
+        out_shape=jax.ShapeDtypeStruct((16, rows, cols), pieces[0].dtype),
+        in_specs=[pl.BlockSpec(memory_space=pltpu.SMEM)] + [pl.BlockSpec(memory_space=pl.ANY)] * 16,
+        out_specs=pl.BlockSpec(memory_space=pltpu.VMEM),
+        scratch_shapes=[pltpu.SemaphoreType.DMA((16 * col_blocks,))],
+        name="placed",
+    )(slots, *pieces)
+
+
+def spread_kernel(slot_ref, whole_ref, *refs, col_blocks):
+    outs, sem = refs[:4], refs[4]
+    width = whole_ref.shape[2] // col_blocks
+    copies = []
+    for at in range(16):
+        row = slot_ref[at]
+        across, along = at // 4, at % 4
+        if along < 2:
+            group, place = (0, across * 2 + along) if across < 2 else (1, (across - 2) * 2 + along)
+        else:
+            group, place = (2 + across % 2, (across // 2) * 2 + along - 2)
+        for col in range(col_blocks):
+            if col_blocks == 1:
+                source, target = whole_ref.at[row], outs[group].at[place]
+            else:
+                to = pl.multiple_of(slot_ref[16 + col] * width, 128)
+                source = whole_ref.at[row, :, pl.ds(to, width)]
+                target = outs[group].at[place, :, pl.ds(col * width, width)]
+            copy = pltpu.make_async_copy(source, target, sem.at[at * col_blocks + col])
+            copy.start()
+            copies.append(copy)
+    for copy in copies:
+        copy.wait()
+
+
+def spread(whole, slots, col_blocks=1):
+    rows, cols = whole.shape[1:]
+    return pl.pallas_call(
+        lambda *refs: spread_kernel(*refs, col_blocks=col_blocks),
+        out_shape=[jax.ShapeDtypeStruct((4, rows, cols), whole.dtype)] * 4,
+        in_specs=[pl.BlockSpec(memory_space=pltpu.SMEM), pl.BlockSpec(memory_space=pl.ANY)],
+        out_specs=[pl.BlockSpec(memory_space=pltpu.VMEM)] * 4,
+        scratch_shapes=[pltpu.SemaphoreType.DMA((16 * col_blocks,))],
+        name="spread",
+    )(slots, whole)
+
+
+def collected(piece):
+    line = [piece] + [swapped(piece, bits) for bits in Z_BITS[1:]]
+    found = {}
+    for along in range(4):
+        first, second = (X_BIT, Y_BIT) if along < 2 else (Y_BIT, X_BIT)
+        found[0, along] = line[along]
+        found[first >> 3, along] = swapped(line[along], first)
+        found[second >> 3, along] = swapped(line[along], second)
+        found[3, along] = swapped(found[first >> 3, along], second)
+    return [found[across, along] for across in range(4) for along in range(4)]
+
+
+def summed(whole, slots, col_blocks=1):
+    low = jnp.bfloat16
+    full = jnp.float32
+    keep_a, send_a, keep_b, send_b = spread(whole, slots, col_blocks)
+    got_a = swapped(send_a, Y_BIT)
+    got_b = swapped(send_b, X_BIT)
+    onward_a = (keep_a[2:].astype(full) + got_a[2:].astype(full)).astype(low)
+    onward_b = (keep_b[2:].astype(full) + got_b[2:].astype(full)).astype(low)
+    here_a = keep_a[:2].astype(full) + got_a[:2].astype(full)
+    here_b = keep_b[:2].astype(full) + got_b[:2].astype(full)
+    here_a = here_a + swapped(onward_a, X_BIT).astype(full)
+    here_b = here_b + swapped(onward_b, Y_BIT).astype(full)
+    return (
+        here_a[0]
+        + swapped(here_a[1].astype(low), Z_BITS[1]).astype(full)
+        + swapped(here_b[0].astype(low), Z_BITS[2]).astype(full)
+        + swapped(here_b[1].astype(low), Z_BITS[3]).astype(full)
+    )
+
+
+def lanes_low(rows):
+    return lax.broadcasted_iota(jnp.int32, (rows, 2 * HD), 1) < HD
+
+
+def head_forward_kernel(place_ref, *refs):
+    pieces, sends, (joint_ref, mixed_ref, totals_ref), (acc_ref,) = (
+        refs[:4],
+        refs[4:8],
+        refs[8:11],
+        refs[11:],
+    )
+    wide = 2 * HD
+    for at in range(16):
+        to = pl.multiple_of(place_ref[at] * BLOCK_ROWS, BLOCK_ROWS)
+        joint_ref[pl.ds(to, BLOCK_ROWS), :] = pieces[at // 4][
+            (at % 4) * BLOCK_ROWS : (at % 4 + 1) * BLOCK_ROWS, :
+        ]
+    first = lanes_low(TILE)
+    sides = (first, jnp.logical_not(first))
+    row_ids = lax.broadcasted_iota(jnp.int32, (TILE, TILE), 0)
+    col_ids = lax.broadcasted_iota(jnp.int32, (TILE, TILE), 1)
+    causal = col_ids <= row_ids
+
+    def tile_part(queries, key_at, masked):
+        key_at = pl.multiple_of(key_at, TILE)
+        key_rows = joint_ref[pl.ds(key_at, TILE), wide : 2 * wide]
+        value_rows = joint_ref[pl.ds(key_at, TILE), 2 * wide :]
+        for side in range(2):
+            powers = jnp.exp(inner_cols(queries[side], key_rows))
+            if masked:
+                powers = jnp.where(causal, powers, 0.0)
+            extended = jnp.where(sides[side], value_rows, jnp.ones_like(value_rows))
+            acc_ref[side] += product(powers.astype(jnp.bfloat16), extended)
+
+    def query_tile(index, carry):
+        query_at = pl.multiple_of(index * TILE, TILE)
+        scaled = joint_ref[pl.ds(query_at, TILE), :wide] * jnp.bfloat16(HD**-0.5)
+        nothing = jnp.zeros_like(scaled)
+        queries = [jnp.where(side, scaled, nothing) for side in sides]
+        acc_ref[...] = jnp.zeros_like(acc_ref)
+
+        def key_tile(key_index, inner):
+            tile_part(queries, key_index * TILE, False)
+            return inner
+
+        lax.fori_loop(0, index, key_tile, 0)
+        tile_part(queries, query_at, True)
+        low_acc, high_acc = acc_ref[0], acc_ref[1]
+        unnorm = jnp.where(first, low_acc, high_acc)
+        totals = pltpu.roll(jnp.where(first, high_acc, low_acc), HD, 1)
+        totals_ref[pl.ds(query_at, TILE), :] = totals
+        mixed_ref[pl.ds(query_at, TILE), :] = unnorm / totals
+        return carry
+
+    lax.fori_loop(0, joint_ref.shape[0] // TILE, query_tile, 0)
+    for at in range(16):
+        to = pl.multiple_of(place_ref[at] * BLOCK_ROWS, BLOCK_ROWS)
+        sends[at // 4][(at % 4) * BLOCK_ROWS : (at % 4 + 1) * BLOCK_ROWS, :] = mixed_ref[
+            pl.ds(to, BLOCK_ROWS), :
+        ].astype(jnp.bfloat16)
+
+
+def head_forward(pieces, places):
+    rows, wide = pieces[0].shape
+    total_rows = 4 * rows
+    vmem = pl.BlockSpec(memory_space=pltpu.VMEM)
+    return pl.pallas_call(
+        head_forward_kernel,
+        out_shape=[jax.ShapeDtypeStruct((rows, 2 * HD), jnp.bfloat16)] * 4
+        + [
+            jax.ShapeDtypeStruct((total_rows, wide), jnp.bfloat16),
+            jax.ShapeDtypeStruct((total_rows, 2 * HD), jnp.float32),
+            jax.ShapeDtypeStruct((total_rows, 2 * HD), jnp.float32),
+        ],
+        in_specs=[pl.BlockSpec(memory_space=pltpu.SMEM)] + [vmem] * 4,
+        out_specs=[vmem] * 7,
+        scratch_shapes=[pltpu.VMEM((2, TILE, 2 * HD), jnp.float32)],
+        name="head_forward",
+    )(places, *pieces)
+
+
+def head_backward_kernel(place_ref, joint_ref, mixed_ref, totals_ref, *refs):
+    pieces, sends, (grad_ref, side_ref, query_ref, key_ref, value_ref, joint_grad) = (
+        refs[:4],
+        refs[4:8],
+        refs[8:],
+    )
+    wide = 2 * HD
+    total_rows = joint_ref.shape[0]
+    for at in range(16):
+        to = pl.multiple_of(place_ref[at] * BLOCK_ROWS, BLOCK_ROWS)
+        grad_ref[pl.ds(to, BLOCK_ROWS), :] = pieces[at // 4][
+            (at % 4) * BLOCK_ROWS : (at % 4 + 1) * BLOCK_ROWS, :
+        ].astype(jnp.float32)
+    first = lanes_low(TILE)
+    sides = (first, jnp.logical_not(first))
+    lane_ids = lax.broadcasted_iota(jnp.int32, (TILE, wide), 1)
+    key_ids = lax.broadcasted_iota(jnp.int32, (TILE, TILE), 0)
+    query_ids = lax.broadcasted_iota(jnp.int32, (TILE, TILE), 1)
+    causal = key_ids <= query_ids
+
+    def prepare(index, carry):
+        at = pl.multiple_of(index * TILE, TILE)
+        grad_mixed = grad_ref[pl.ds(at, TILE), :]
+        totals = totals_ref[pl.ds(at, TILE), :]
+        grad_unnorm = (grad_mixed / totals).astype(jnp.bfloat16).astype(jnp.float32)
+        weighed = grad_mixed * mixed_ref[pl.ds(at, TILE), :] / totals
+        for side in range(2):
+            grad_totals = -jnp.sum(
+                jnp.where(sides[side], weighed, 0.0), axis=1, keepdims=True
+            )
+            coarse = grad_totals.astype(jnp.bfloat16).astype(jnp.float32)
+            fine = grad_totals - coarse
+            base = (1 - side) * HD
+            extra = jnp.where(
+                lane_ids == base, coarse, jnp.where(lane_ids == base + 1, fine, 0.0)
+            )
+            side_ref[side, pl.ds(at, TILE), :] = jnp.where(
+                sides[side], grad_unnorm, extra
+            ).astype(jnp.bfloat16)
+        return carry
+
+    lax.fori_loop(0, total_rows // TILE, prepare, 0)
+    query_ref[...] = jnp.zeros_like(query_ref)
+
+    def tile_part(query_at, key_rows, values, masked):
+        query_at = pl.multiple_of(query_at, TILE)
+        scaled = joint_ref[pl.ds(query_at, TILE), :wide] * jnp.bfloat16(HD**-0.5)
+        nothing = jnp.zeros_like(scaled)
+        for side in range(2):
+            powers = jnp.exp(inner_cols(key_rows, jnp.where(sides[side], scaled, nothing)))
+            if masked:
+                powers = jnp.where(causal, powers, 0.0)
+            upstream = side_ref[side, pl.ds(query_at, TILE), :]
+            grad_scores = (powers * inner_cols(values[side], upstream)).astype(jnp.bfloat16)
+            value_ref[side] += product(powers.astype(jnp.bfloat16), upstream)
+            key_ref[side] += product(grad_scores, scaled)
+            query_ref[side, pl.ds(query_at, TILE), :] += inner_rows(grad_scores, key_rows)
+
+    def key_tile(index, carry):
+        key_at = pl.multiple_of(index * TILE, TILE)
+        key_rows = joint_ref[pl.ds(key_at, TILE), wide : 2 * wide]
+        value_rows = joint_ref[pl.ds(key_at, TILE), 2 * wide :]
+        values = [jnp.where(side, value_rows, jnp.ones_like(value_rows)) for side in sides]
+        key_ref[...] = jnp.zeros_like(key_ref)
+        value_ref[...] = jnp.zeros_like(value_ref)
+        tile_part(key_at, key_rows, values, True)
+
+        def query_tile(query_index, inner):
+            tile_part(query_index * TILE, key_rows, values, False)
+            return inner
+
+        lax.fori_loop(index + 1, total_rows // TILE, query_tile, 0)
+        joint_grad[pl.ds(key_at, TILE), wide : 2 * wide] = jnp.where(
+            first, key_ref[0], key_ref[1]
+        ).astype(jnp.bfloat16)
+        joint_grad[pl.ds(key_at, TILE), 2 * wide :] = jnp.where(
+            first, value_ref[0], value_ref[1]
+        ).astype(jnp.bfloat16)
+        return carry
+
+    lax.fori_loop(0, total_rows // TILE, key_tile, 0)
+
+    def finish(index, carry):
+        at = pl.multiple_of(index * TILE, TILE)
+        joint_grad[pl.ds(at, TILE), :wide] = (
+            jnp.where(first, query_ref[0, pl.ds(at, TILE), :], query_ref[1, pl.ds(at, TILE), :])
+            * HD**-0.5
+        ).astype(jnp.bfloat16)
+        return carry
+
+    lax.fori_loop(0, total_rows // TILE, finish, 0)
+    for at in range(16):
+        to = pl.multiple_of(place_ref[at] * BLOCK_ROWS, BLOCK_ROWS)
+        sends[at // 4][(at % 4) * BLOCK_ROWS : (at % 4 + 1) * BLOCK_ROWS, :] = joint_grad[
+            pl.ds(to, BLOCK_ROWS), :
+        ]
+
+
+def head_backward(joint_sorted, mixed_sorted, totals_sorted, pieces, places):
+    rows = pieces[0].shape[0]
+    total_rows, wide = joint_sorted.shape
+    vmem = pl.BlockSpec(memory_space=pltpu.VMEM)
+    return pl.pallas_call(
+        head_backward_kernel,
+        out_shape=[jax.ShapeDtypeStruct((rows, wide), jnp.bfloat16)] * 4,
+        in_specs=[pl.BlockSpec(memory_space=pltpu.SMEM)] + [vmem] * 7,
+        out_specs=[vmem] * 4,
+        scratch_shapes=[
+            pltpu.VMEM((total_rows, 2 * HD), jnp.float32),
+            pltpu.VMEM((2, total_rows, 2 * HD), jnp.bfloat16),
+            pltpu.VMEM((2, total_rows, 2 * HD), jnp.float32),
+            pltpu.VMEM((2, TILE, 2 * HD), jnp.float32),
+            pltpu.VMEM((2, TILE, 2 * HD), jnp.float32),
+            pltpu.VMEM((total_rows, wide), jnp.bfloat16),
+        ],
+        name="head_backward",
+    )(places, joint_sorted, mixed_sorted, totals_sorted, *pieces)
+
+
+def norm_parts(values):
+    average = jnp.mean(values, axis=-1, keepdims=True)
+    centred = values - average
+    spread_of = jnp.mean(centred * centred, axis=-1, keepdims=True)
+    inverse = lax.rsqrt(spread_of + EPS)
+    return centred * inverse, inverse
+
+
+def norm_pull(grad, scaled, inverse, gain):
+    lifted = grad * gain
+    return (
+        lifted
+        - jnp.mean(lifted, axis=-1, keepdims=True)
+        - scaled * jnp.mean(lifted * scaled, axis=-1, keepdims=True)
+    ) * inverse
+
+
+def chip_body(
+    inputs,
+    block_order,
+    first_gain,
+    first_shift,
+    joint_weight,
+    query_bias,
+    value_bias,
+    mixer_weight,
+    mixer_bias,
+    second_gain,
+    second_shift,
+    expand_weight,
+    expand_bias,
+    reduce_weight,
+    reduce_bias,
+    cotangent,
+):
+    low, full = jnp.bfloat16, jnp.float32
+    position = lax.axis_index("sp")
+    group = lax.axis_index("dp")
+    core = position % 2
+    depth = position // 2
+    even = core == 0
+    own_rows = inputs.shape[1]
+    share = joint_weight.shape[0]
+
+    def own_first(value):
+        return jnp.concatenate([value, swapped(value, CORE_BIT)], axis=0)
+
+    def chip_order(mine, theirs):
+        return jnp.where(
+            even,
+            jnp.concatenate([mine, theirs], axis=0),
+            jnp.concatenate([theirs, mine], axis=0),
+        )
+
+    def cores_exchanged(parts):
+        mine = jnp.where(even, parts[0], parts[1])
+        theirs = jnp.where(even, parts[1], parts[0])
+        return chip_order(mine, swapped(theirs, CORE_BIT))
+
+    chip_ids = jnp.arange(16, dtype=jnp.int32)
+    across, along = chip_ids // 4, chip_ids % 4
+    slots = (across ^ group) * 4 + (along ^ depth)
+    col_slots = jnp.arange(4, dtype=jnp.int32) ^ depth
+    joint_slots = jnp.concatenate([slots, col_slots])
+    mixer_slots = ((slots // 8) ^ core) * 8 + (((slots // 2) % 4) ^ depth) * 2 + slots % 2
+    places = block_order[
+        ((chip_ids // 4) ^ depth) * 4 + (((chip_ids // 2) % 2) ^ core) * 2 + chip_ids % 2
+    ]
+
+    small = jnp.concatenate(
+        [
+            first_gain,
+            first_shift,
+            query_bias,
+            value_bias,
+            mixer_bias,
+            second_gain,
+            second_shift,
+            reduce_bias,
+            expand_bias,
+        ]
+    ).reshape(1, -1)
+    small_line = chip_order(small, swapped(small, CORE_BIT))[None]
+    small_line = jnp.concatenate([small_line] + [swapped(small_line, bits) for bits in Z_BITS[1:]])
+    small_all = jnp.concatenate(
+        [small_line[None]] + [swapped(small_line, bits)[None] for bits in (X_BIT, Y_BIT, X_BIT + Y_BIT)]
+    ).reshape(16, -1)
+    pick = (slots[None, :] == chip_ids[:, None]).astype(low)
+    small_all = product(pick, small_all).reshape(32, -1)
+    count = share
+    (
+        gain_one,
+        shift_one,
+        query_shift,
+        value_shift,
+        mixer_shift,
+        gain_two,
+        shift_two,
+        reduce_shift,
+    ) = [small_all[:, at * count : (at + 1) * count].reshape(-1) for at in range(8)]
+    expand_shift = small_all[:, 8 * count :].reshape(16, 2, 128)
+    expand_shift = jnp.where(even, expand_shift[:, 0], expand_shift[:, 1]).reshape(-1)
+
+    joint_parts = joint_weight.reshape(share, 3, 2, 4, 128).transpose(2, 0, 3, 1, 4).reshape(2, share, 1536)
+    joint_own = cores_exchanged((joint_parts[0], joint_parts[1]))
+    joint_full = placed(collected(joint_own), joint_slots, 4).reshape(D, 1536)
+    mixer_own = cores_exchanged((mixer_weight[:, : D // 2], mixer_weight[:, D // 2 :]))
+    mixer_cols = placed(collected(mixer_own), mixer_slots).reshape(2, D // 2, D // 2)
+    mixer_mine, mixer_theirs = mixer_cols[0], swapped(mixer_cols[1], CORE_BIT)
+    mixer_full = jnp.where(
+        even,
+        jnp.concatenate([mixer_mine, mixer_theirs], axis=1),
+        jnp.concatenate([mixer_theirs, mixer_mine], axis=1),
+    )
+    units = expand_weight.shape[1] // 2
+    expand_parts = expand_weight.reshape(share, 16, 2, 128)
+    expand_own = cores_exchanged(
+        (expand_parts[:, :, 0].reshape(share, units), expand_parts[:, :, 1].reshape(share, units))
+    )
+    expand_full = placed(collected(expand_own), slots).reshape(D, units)
+    reduce_full = placed(collected(reduce_weight), slots).reshape(units, D)
+
+    token_rows = own_first(inputs[0]).astype(full)
+    upstream = own_first(cotangent[0])
+    scaled_one, inverse_one = norm_parts(token_rows)
+    normed = (scaled_one * gain_one + shift_one).astype(low)
+    halves_of = [
+        jnp.where(even, item[: D // 2], item[D // 2 :]).reshape(4, 1, 128)
+        for item in (query_shift, value_shift)
+    ]
+    joint_shift = jnp.concatenate([halves_of[0], jnp.zeros_like(halves_of[0]), halves_of[1]], axis=1)
+    joint_shift = product(
+        (col_slots[:, None] == jnp.arange(4)[None, :]).astype(low), joint_shift.reshape(4, 384).astype(low)
+    ).reshape(-1)
+    joint_rows = (product(normed, joint_full) + joint_shift).astype(low)
+    head_pieces = [joint_rows[:, at * 384 : (at + 1) * 384] for at in range(4)]
+    head_pieces = [head_pieces[0]] + [swapped(head_pieces[at], Z_BITS[at]) for at in (1, 2, 3)]
+    forward = head_forward(head_pieces, places)
+    mixed_out, (joint_sorted, mixed_sorted, totals_sorted) = forward[:4], forward[4:]
+    mixed_rows = jnp.concatenate(
+        [mixed_out[0]] + [swapped(mixed_out[at], Z_BITS[at]) for at in (1, 2, 3)], axis=1
+    )
+
+    def both_cores(part):
+        turned = jnp.concatenate([part[own_rows:], part[:own_rows]], axis=0).astype(low)
+        return part + swapped(turned, CORE_BIT).astype(full)
+
+    def own_sum(part):
+        return part[:own_rows] + swapped(part[own_rows:].astype(low), CORE_BIT).astype(full)
+
+    middle = token_rows + (both_cores(product(mixed_rows, mixer_full)) + mixer_shift)
+    scaled_two, inverse_two = norm_parts(middle)
+    second = (scaled_two * gain_two + shift_two).astype(low)
+    before = product(second, expand_full) + expand_shift
+    active, gelu_pull = jax.vjp(gelu_tanh, before)
+    active = active.astype(low)
+    result = middle[:own_rows] + (own_sum(product(active, reduce_full)) + reduce_shift)
+
+    reduce_gradient = inner_rows(active, upstream).astype(low).reshape(16, 128, D)
+    reduce_sum = summed(reduce_gradient, slots)
+    grad_before = gelu_pull(inner_cols(upstream, reduce_full))[0].astype(low)
+    expand_gradient = inner_rows(second, grad_before).astype(low).reshape(16, 64, units)
+    expand_sum = summed(expand_gradient, slots)
+    expand_shift_gradient = jnp.sum(grad_before.astype(full), axis=0)
+    grad_second = both_cores(inner_cols(grad_before, expand_full))
+    upstream_full = upstream.astype(full)
+    grad_middle = upstream_full + norm_pull(grad_second, scaled_two, inverse_two, gain_two)
+    grad_branch = grad_middle.astype(low)
+    mixer_gradient = inner_rows(mixed_rows, grad_branch).astype(low)
+    grad_mixed = inner_cols(grad_branch, mixer_full).astype(low)
+    grad_pieces = [grad_mixed[:, at * 128 : (at + 1) * 128] for at in range(4)]
+    grad_pieces = [grad_pieces[0]] + [swapped(grad_pieces[at], Z_BITS[at]) for at in (1, 2, 3)]
+    mixer_keep = jnp.where(even, mixer_gradient[:, : D // 2], mixer_gradient[:, D // 2 :])
+    mixer_send = jnp.where(even, mixer_gradient[:, D // 2 :], mixer_gradient[:, : D // 2])
+    mixer_whole = jnp.concatenate([mixer_keep, swapped(mixer_send, CORE_BIT)], axis=0)
+    mixer_sum = summed(mixer_whole.reshape(16, 64, D // 2), mixer_slots)
+    grad_out = head_backward(joint_sorted, mixed_sorted, totals_sorted, grad_pieces, places)
+    grad_joint = jnp.concatenate(
+        [grad_out[0]] + [swapped(grad_out[at], Z_BITS[at]) for at in (1, 2, 3)], axis=1
+    )
+    joint_gradient = inner_rows(normed, grad_joint).astype(low).reshape(16, 64, 1536)
+    joint_sum = summed(joint_gradient, joint_slots, 4)
+    joint_sums = product(
+        (col_slots[:, None] == jnp.arange(4)[None, :]).astype(full),
+        jnp.sum(grad_joint.astype(full), axis=0).reshape(4, 384),
+    ).reshape(4, 3, 128)
+    grad_normed = own_sum(inner_cols(grad_joint, joint_full))
+    own_scaled = scaled_one[:own_rows]
+    input_gradient = (
+        grad_middle[:own_rows] + norm_pull(grad_normed, own_scaled, inverse_one[:own_rows], gain_one)
+    ).astype(low)
+
+    def one_core(values):
+        values = values.reshape(1, -1)
+        nothing = jnp.zeros_like(values)
+        return jnp.where(
+            even, jnp.concatenate([values, nothing]), jnp.concatenate([nothing, values])
+        )
+
+    expand_rows = one_core(expand_shift_gradient).reshape(2, 16, 128).transpose(1, 0, 2)
+    sums = jnp.concatenate(
+        [
+            item.reshape(32, -1)
+            for item in (
+                jnp.sum(grad_normed * own_scaled, axis=0),
+                jnp.sum(grad_normed, axis=0),
+                one_core(joint_sums[:, 0]),
+                one_core(joint_sums[:, 2]),
+                jnp.sum(grad_branch[:own_rows].astype(full), axis=0),
+                jnp.sum(grad_second[:own_rows] * scaled_two[:own_rows], axis=0),
+                jnp.sum(grad_second[:own_rows], axis=0),
+                jnp.sum(upstream_full[:own_rows], axis=0),
+                expand_rows,
+            )
+        ],
+        axis=1,
+    )
+    for mask in (CORE_BIT, Z_BITS[1], Z_BITS[2], X_BIT, Y_BIT):
+        sums = sums + swapped(sums, mask)
+    own_sums = lax.dynamic_slice_in_dim(sums, group * 8 + position, 1, axis=0)[0]
+    vectors = [own_sums[at * count : (at + 1) * count] for at in range(8)] + [own_sums[8 * count :]]
+
+    def finished(total):
+        mine = jnp.where(even, total[:share], total[share:])
+        theirs = swapped(jnp.where(even, total[share:], total[:share]), CORE_BIT)
+        return jnp.where(even, jnp.stack([mine, theirs], axis=0), jnp.stack([theirs, mine], axis=0))
+
+    joint_out = finished(joint_sum).reshape(2, share, 4, 3, 128).transpose(1, 3, 0, 2, 4)
+    mixer_out = finished(mixer_sum).transpose(1, 0, 2)
+    expand_out = finished(expand_sum).reshape(2, share, 16, 128).transpose(1, 2, 0, 3)
+    return (
+        result.astype(low)[None],
+        input_gradient[None],
+        vectors[0],
+        vectors[1],
+        joint_out.reshape(share, 3 * D),
+        vectors[2],
+        vectors[3],
+        mixer_out.reshape(share, D),
+        vectors[4],
+        vectors[5],
+        vectors[6],
+        expand_out.reshape(share, 2 * units),
+        vectors[8],
+        reduce_sum,
+        vectors[7],
+    )
+
+
 def solution(mesh):
     in_specs = (
         P("dp", "sp", None),
@@ -392,4 +959,6 @@
         P(("dp", "sp"), None),
         P(("dp", "sp")),
     )
+    whole_pairs = mesh.shape["dp"] == 4 and mesh.shape["sp"] == 8
+    body = chip_body if whole_pairs else ring_body
     return jax.shard_map(body, mesh=mesh, in_specs=in_specs, out_specs=out_specs, check_vma=False)

time: 1180 us -> 544 us (0.46)
  waiting for transfers between devices: 785 us -> 172 us
  starting transfers between devices: 4.11 us -> 159 us
  blocking collectives: 124 us -> 0 us
  matrix products: 124 us -> 44.5 us
  Pallas kernels: 0 us -> 67.7 us
  loops' own time: 19.3 us -> 0 us
  between operations: 16.1 us -> 2.45 us
  local copies, waits for them, and re-layouts: 54.7 us -> 41.8 us
    reduce_scatter x4 -> x0, waiting for transfers between devices: 442 us -> none  [the longest x1 189 us: body(): lax.psum_scatter(expand_gradient, ('dp', 'sp'), scatter_dimension=0, tile...]
    ppermute x44 -> x126, starting transfers between devices: 3.79 us -> 159 us  [swapped(): lax.ppermute(value, ALL, [(source, source ^ mask) for source in range(cou...]
    ppermute x44 -> x126, waiting for transfers between devices: 324 us -> 172 us  [swapped(): lax.ppermute(value, ALL, [(source, source ^ mask) for source in range(cou...]
    unnamed x2 -> x0, blocking collectives: 83.4 us -> none
    pallas_call x0 -> x10, Pallas kernels: none -> 67.7 us  [the longest x1 20.4 us: head_backward(): pl.pallas_call(head_backward_kernel, out_shape=[jax.ShapeDtypeStruct((row...]
    dot_general x55 -> x0, matrix products: 45.1 us -> none  [the longest x8 9.15 us: tile_backward(): jnp.einsum('tqhd,tkhd->thqk', grad_unnorm, value_rows, preferred_element_...]
    all_gather x1 -> x0, blocking collectives: 41 us -> none  [body(): lax.all_gather(owned_shards[10], ('dp', 'sp'), axis=0, tiled=True)]
    add x50 -> x15, other arithmetic: 33.1 us -> 8.98 us  [the longest x4 5.32 us: summed(): here_a = here_a + swapped(onward_a, X_BIT).astype(full)]
  transfers between devices with their start and end apart: 52 -> 126, of which waited for: 48 -> 45; matrix products, arithmetic and copies ran while one was open for 16% -> 18% of each run, Pallas kernels for 0% -> 13%
where the time goes in v1:
time: 544 us; the launch traced here: 535 us
  waiting for transfers between devices  172 us (32%)
  starting transfers between devices  159 us (29%)
  Pallas kernels  67.7 us (12%)
  other arithmetic  48.8 us (9%)
  matrix products  44.5 us (8%)
  local copies, waits for them, and re-layouts  41.8 us (8%)
    ppermute x126, waiting for transfers between devices, swapped(): lax.ppermute(value, ALL, [(source, source ^ mask) for source in range(cou...  172 us
    ppermute x126, starting transfers between devices, swapped(): lax.ppermute(value, ALL, [(source, source ^ mask) for source in range(cou...  159 us
    pallas_call x1, Pallas kernels, head_backward(): pl.pallas_call(head_backward_kernel, out_shape=[jax.ShapeDtypeStruct((row...  20.4 us
    dot_general x4, matrix products, inner_rows(): lax.dot_general(left, right, (((0,), (0,)), ((), ())), preferred_element_...  18 us
    pallas_call x4, Pallas kernels, spread(): pl.pallas_call(lambda *refs: spread_kernel(*refs, col_blocks=col_blocks),...  17.9 us
    pallas_call x4, Pallas kernels, placed(): pl.pallas_call(lambda *refs: placed_kernel(*refs, col_blocks=col_blocks),...  17.8 us
    dot_general x4, matrix products, inner_cols(): lax.dot_general(left, right, (((1,), (1,)), ((), ())), preferred_element_...  13.6 us
    dot_general x7, matrix products, product(): return jnp.dot(left, right, preferred_element_type=jnp.float32)  12.9 us
  transfers between devices with their start and end apart: 126, of which 45 were waited for; matrix products, arithmetic and copies ran while one was open for 18% of the time, Pallas kernels for 13%

profile of v1, /device:TPU:0, one launch (start us, length us, event | category | flops | bytes accessed | tf_op | source)
XLA Modules:
  0.0 535.4 jit_solution(18183698302185333192)
XLA Ops:
  0.7 6.1 %concatenate.113 = bf16[384]{0:T(512)(128)(2,1)S(1)} concatenate(bf16[32]{0:T(256)(128)(2,1)} %param.18, bf16[32]{0:T(256)(128)(2,1)} %param.19, bf16[32]{0:T(256)(128)(2,1)} %param.21, bf16[32]{0:T(256)(128)(2,1)} %param.22, bf16[32]{0:T(256)(128)(2,1)} %param.24, bf16[32]{0:T(256)(128)(2,1)} %param.25, bf16[32]{0:T(256)(128)(2,1)} %param.26, bf16[32]{0:T(256)(128)(2,1)} %param.30, ...), dimensions={0} | concatenate | bytes 1536 | tf_op jit(solution)/shard_map/concatenate | solution.py:746
  11.4 4.7 collective-permute-start.4
  17.7 2.9 collective-permute-done.3
  38.8 7.8 %collective-permute-done.10.refs_3_ = bf16[64,1536]{1,0:T(8,128)(2,1)S(1)} collective-permute-done((bf16[64,1536]{1,0:T(8,128)(2,1)S(1)}, bf16[64,1536]{1,0:T(8,128)(2,1)S(1)}, u32[]{:S(2)}, u32[]{:S(2)}) %collective-permute-start.10) | collective-permute-done | bytes 196640 | tf_op jit(solution)/shard_map/ppermute | solution.py:372
  52.4 6.1 %collective-permute-done.13.refs_6_ = bf16[64,1536]{1,0:T(8,128)(2,1)S(1)} collective-permute-done((bf16[64,1536]{1,0:T(8,128)(2,1)S(1)}, bf16[64,1536]{1,0:T(8,128)(2,1)S(1)}, u32[]{:S(2)}, u32[]{:S(2)}) %collective-permute-start.13) | collective-permute-done | bytes 196640 | tf_op jit(solution)/shard_map/ppermute | solution.py:372
  64.3 3.8 collective-permute-start.32
  74.3 4.9 placed.4
  79.2 3.8 fusion.7
  91.3 3.1 collective-permute-start.24
  104.4 3.0 placed.5
  108.8 3.3 collective-permute-done.24.refs_1_
  112.7 12.6 %collective-permute-done.25.refs_2_ = bf16[512,384]{1,0:T(8,128)(2,1)} collective-permute-done((bf16[512,384]{1,0:T(8,128)(2,1)}, bf16[512,384]{1,0:T(8,128)(2,1)}, u32[]{:S(2)}, u32[]{:S(2)}) %collective-permute-start.25) | collective-permute-done | bytes 393248 | tf_op jit(solution)/shard_map/ppermute | solution.py:372
  125.2 11.6 %head_forward.1 = (bf16[512,128]{1,0:T(8,128)(2,1)}, bf16[512,128]{1,0:T(8,128)(2,1)}, bf16[512,128]{1,0:T(8,128)(2,1)}, bf16[512,128]{1,0:T(8,128)(2,1)}, bf16[...) custom-call(s32[16]{0:T(128)} %gather_fusion, bf16[512,384]{1,0:T(8,128)(2,1)} %get-tuple-element.85.refs_0_, ...), custom_call_target="tpu_custom_call" | custom-call | tf_op jit(solution)/shard_map/head_forward/pallas_call | solution.py:543
  136.9 10.5 %collective-permute-start.27 = (bf16[512,128]{1,0:T(8,128)(2,1)}, bf16[512,128]{1,0:T(8,128)(2,1)S(1)}, u32[]{:S(2)}, u32[]{:S(2)}) collective-permute-start(bf16[512,128]{1,0:T(8,128)(2,1)} %get-tuple-element.43), channel_id=1, source_target_pairs={{0,2},{1,3},{2,0},{3,1},{4,6},{5,7},{6,4},{7,5},{8,10},{9,11},{10,... | collective-permute-start | bytes 393224 | tf_op jit(solution)/shard_map/ppermute | solution.py:372
  159.3 4.8 collective-permute-start.49
  164.3 6.3 %collective-permute-start.50 = (bf16[64,2048]{1,0:T(8,128)(2,1)S(1)}, bf16[64,2048]{1,0:T(8,128)(2,1)S(1)}, u32[]{:S(2)}, u32[]{:S(2)}) collective-permute-start(bf16[64,2048]{1,0:T(8,128)(2,1)S(1)} %maximum_select_fusion.3.refs_1_), channel_id=1, source_target_pairs={{0,4},{1,5},{2,6},{3,7},{4,0},{5,1},{6,2},{7,3},{8,12},{9,13},{10,... | collective-permute-start | bytes 786440 | tf_op jit(solution)/shard_map/ppermute | solution.py:372
  173.9 3.4 fusion.90
  177.3 8.8 %collective-permute-done.50.refs_3_ = bf16[64,2048]{1,0:T(8,128)(2,1)S(1)} collective-permute-done((bf16[64,2048]{1,0:T(8,128)(2,1)S(1)}, bf16[64,2048]{1,0:T(8,128)(2,1)S(1)}, u32[]{:S(2)}, u32[]{:S(2)}) %collective-permute-start.50) | collective-permute-done | bytes 262176 | tf_op jit(solution)/shard_map/ppermute | solution.py:372
  190.3 6.4 %collective-permute-done.69.refs_7_ = bf16[128,1024]{1,0:T(8,128)(2,1)S(1)} collective-permute-done((bf16[128,1024]{1,0:T(8,128)(2,1)}, bf16[128,1024]{1,0:T(8,128)(2,1)S(1)}, u32[]{:S(2)}, u32[]{:S(2)}) %collective-permute-start.69) | collective-permute-done | bytes 262176 | tf_op jit(solution)/shard_map/ppermute | solution.py:372
  197.6 3.9 collective-permute-done.70.refs_8_
  207.9 3.8 collective-permute-done.75.refs_13_
  217.7 3.3 collective-permute-done.55.refs_8_
  223.4 4.5 collective-permute-done.58.refs_11_
  229.7 3.9 collective-permute-done.59.refs_12_
  234.7 4.5 collective-permute-done.76.refs_14_
  243.4 4.9 placed.7
  251.0 5.0 placed.6
  256.0 3.9 fusion.81
  268.5 6.0 %convert_reduce_fusion = (f32[2048]{0:T(1024)S(1)}, bf16[512,2048]{1,0:T(8,128)(2,1)S(1)}) fusion(f32[512,2048]{1,0:T(8,128)S(1)} %fusion.29, f32[2048]{0:T(1024)S(1)} %bitcast.209, bf16[2048,1024]{1,0:T(8,128)(2,1)S(1)} %bitcast.177, bf16[256,1024]{1,0:T(8,128)(2,1)S(1)} %copy-done.19, bf16[256,1024]{1,0:T(8,128)(2,1)S(1)} %bitcast.189), kind=kOutput, calls=%fused_computation.10 | convolution fusion | flops 2173696000 | bytes 11550720 | tf_op jit(solution)/shard_map/dot_general | solution.py:44
  274.5 3.7 fusion.91
  278.2 4.4 convolution_convert_fusion.1
  285.1 4.9 spread.6
  291.8 7.8 %convolution_convert_fusion = bf16[2048,1024]{1,0:T(8,128)(2,1)} fusion(bf16[256,1024]{1,0:T(8,128)(2,1)} %copy-done.18, bf16[256,1024]{1,0:T(8,128)(2,1)} %bitcast.186, f32[512,2048]{1,0:T(8,128)} %copy-done.102, f32[2048]{0:T(1024)S(1)} %bitcast.210), kind=kOutput, calls=%fused_computation.12 | convolution fusion | flops 2162163712 | bytes 9445376 | tf_op jit(solution)/shard_map/dot_general | solution.py:38
  299.6 4.9 spread.7
  319.0 18.9 %collective-permute-done.119 = bf16[4,128,1024]{2,1,0:T(8,128)(2,1)S(1)} collective-permute-done((bf16[4,128,1024]{2,1,0:T(8,128)(2,1)}, bf16[4,128,1024]{2,1,0:T(8,128)(2,1)S(1)}, u32[]{:S(2)}, u32[]{:S(2)}) %collective-permute-start.119) | collective-permute-done | bytes 1048608 | tf_op jit(solution)/shard_map/ppermute | solution.py:372
  353.2 20.4 %head_backward.1 = (bf16[512,384]{1,0:T(8,128)(2,1)}, bf16[512,384]{1,0:T(8,128)(2,1)}, bf16[512,384]{1,0:T(8,128)(2,1)}, bf16[512,384]{1,0:T(8,128)(2,1)}) custom-call(s32[16]{0:T(128)} %gather_fusion, bf16[2048,384]{1,0:T(8,128)(2,1)} %get-tuple-element.46.joint_ref, f32[2048,128]{1,0:T(8,128)} %get-tuple-element.47.mixed_ref, ...), custom_call_target="tpu_custom_call" | custom-call | tf_op jit(solution)/shard_map/head_backward/pallas_call | solution.py:660
  383.3 3.0 spread.5
  396.2 2.9 collective-permute-start.117
  399.2 18.5 %collective-permute-done.86 = bf16[512,384]{1,0:T(8,128)(2,1)} collective-permute-done((bf16[512,384]{1,0:T(8,128)(2,1)}, bf16[512,384]{1,0:T(8,128)(2,1)}, u32[]{:S(2)}, u32[]{:S(2)}) %collective-permute-start.86) | collective-permute-done | bytes 393248 | tf_op jit(solution)/shard_map/ppermute | solution.py:372
  418.8 10.6 %collective-permute-start.113 = (bf16[64,2048]{1,0:T(8,128)(2,1)}, bf16[64,2048]{1,0:T(8,128)(2,1)}, u32[]{:S(2)}, u32[]{:S(2)}) collective-permute-start(bf16[64,2048]{1,0:T(8,128)(2,1)} %fusion.30), channel_id=1, source_target_pairs={{0,2},{1,3},{2,0},{3,1},{4,6},{5,7},{6,4},{7,5},{8,10},{9,11},{10,... | collective-permute-start | bytes 786440 | tf_op jit(solution)/shard_map/ppermute | solution.py:372
  435.1 5.1 convolution_convert_fusion.2
  440.3 5.0 spread.4
  457.2 9.0 %collective-permute-done.124 = bf16[128,1024]{1,0:T(8,128)(2,1)S(1)} collective-permute-done((bf16[128,1024]{1,0:T(8,128)(2,1)S(1)}, bf16[128,1024]{1,0:T(8,128)(2,1)S(1)}, u32[]{:S(2)}, u32[]{:S(2)}) %collective-permute-start.124) | collective-permute-done | bytes 262176 | tf_op jit(solution)/shard_map/ppermute | solution.py:372
  468.1 7.1 %collective-permute-done.107 = bf16[2,64,512]{2,1,0:T(8,128)(2,1)S(1)} collective-permute-done((bf16[2,64,512]{2,1,0:T(8,128)(2,1)S(1)}, bf16[2,64,512]{2,1,0:T(8,128)(2,1)S(1)}, u32[]{:S(2)}, u32[]{:S(2)}) %collective-permute-start.107) | collective-permute-done | bytes 131104 | tf_op jit(solution)/shard_map/ppermute | solution.py:372
  478.8 2.9 collective-permute-start.105
  502.1 3.2 collective-permute-done.92
  513.1 4.9 collective-permute-done.98
  526.1 6.2 %collective-permute-done.99 = bf16[64,1536]{1,0:T(8,128)(2,1)S(1)} collective-permute-done((bf16[64,1536]{1,0:T(8,128)(2,1)S(1)}, bf16[64,1536]{1,0:T(8,128)(2,1)S(1)}, u32[]{:S(2)}, u32[]{:S(2)}) %collective-permute-start.99) | collective-permute-done | bytes 196640 | tf_op jit(solution)/shard_map/ppermute | solution.py:372
  (585 shorter events, 231.9 us)
Async XLA Ops:
  8.7 19.4 %collective-permute-start.8 = (bf16[32,1536]{1,0:T(8,128)(2,1)S(1)}, bf16[32,1536]{1,0:T(8,128)(2,1)S(1)}, u32[]{:S(2)}, u32[]{:S(2)}) collective-permute-start(bf16[32,1536]{1,0:T(8,128)(2,1)S(1)} %select_n.349), channel_id=1, source_target_pairs={{0,1},{1,0},{2,3},{3,2},{4,5},{5,4},{6,7},{7,6},{8,9},{9,8},{10,11... | collective-permute-start | bytes 294920 | tf_op jit(solution)/shard_map/ppermute | solution.py:372
  8.8 27.4 %collective-permute-start = (bf16[256,1024]{1,0:T(8,128)(2,1)}, bf16[256,1024]{1,0:T(8,128)(2,1)S(1)}, u32[]{:S(2)}, u32[]{:S(2)}) collective-permute-start(bf16[256,1024]{1,0:T(8,128)(2,1)} %bitcast.170), channel_id=1, source_target_pairs={{0,1},{1,0},{2,3},{3,2},{4,5},{5,4},{6,7},{7,6},{8,9},{9,8},{10,11... | collective-permute-start | bytes 1572872 | tf_op jit(solution)/shard_map/ppermute | solution.py:372
  28.2 19.8 %collective-permute-start.9 = (bf16[64,1536]{1,0:T(8,128)(2,1)S(1)}, bf16[64,1536]{1,0:T(8,128)(2,1)S(1)}, u32[]{:S(2)}, u32[]{:S(2)}) collective-permute-start(bf16[64,1536]{1,0:T(8,128)(2,1)S(1)} %maximum_select_fusion.4.refs_1_), channel_id=1, source_target_pairs={{0,2},{1,3},{2,0},{3,1},{4,6},{5,7},{6,4},{7,5},{8,10},{9,11},{10,... | collective-permute-start | bytes 589832 | tf_op jit(solution)/shard_map/ppermute | solution.py:372
  32.3 17.2 %collective-permute-start.11 = (bf16[64,1536]{1,0:T(8,128)(2,1)S(1)}, bf16[64,1536]{1,0:T(8,128)(2,1)S(1)}, u32[]{:S(2)}, u32[]{:S(2)}) collective-permute-start(bf16[64,1536]{1,0:T(8,128)(2,1)S(1)} %maximum_select_fusion.4.refs_1_), channel_id=1, source_target_pairs={{0,6},{1,7},{2,4},{3,5},{4,2},{5,3},{6,0},{7,1},{8,14},{9,15},{10,... | collective-permute-start | bytes 589832 | tf_op jit(solution)/shard_map/ppermute | solution.py:372
  64.3 18.7 %collective-permute-start.32 = (bf16[64,512]{1,0:T(8,128)(2,1)S(1)}, bf16[64,512]{1,0:T(8,128)(2,1)}, u32[]{:S(2)}, u32[]{:S(2)}) collective-permute-start(bf16[64,512]{1,0:T(8,128)(2,1)S(1)} %maximum_select_fusion.8.refs_1_), channel_id=1, source_target_pairs={{0,4},{1,5},{2,6},{3,7},{4,0},{5,1},{6,2},{7,3},{8,12},{9,13},{10,... | collective-permute-start | bytes 196616 | tf_op jit(solution)/shard_map/ppermute | solution.py:372
  91.3 20.8 %collective-permute-start.24 = (bf16[512,384]{1,0:T(8,128)(2,1)}, bf16[512,384]{1,0:T(8,128)(2,1)}, u32[]{:S(2)}, u32[]{:S(2)}) collective-permute-start(bf16[512,384]{1,0:T(8,128)(2,1)} %get-tuple-element.84), channel_id=1, source_target_pairs={{0,2},{1,3},{2,0},{3,1},{4,6},{5,7},{6,4},{7,5},{8,10},{9,11},{10,... | collective-permute-start | bytes 1179656 | tf_op jit(solution)/shard_map/ppermute | solution.py:372
  94.4 30.8 %collective-permute-start.25 = (bf16[512,384]{1,0:T(8,128)(2,1)}, bf16[512,384]{1,0:T(8,128)(2,1)}, u32[]{:S(2)}, u32[]{:S(2)}) collective-permute-start(bf16[512,384]{1,0:T(8,128)(2,1)} %get-tuple-element.83), channel_id=1, source_target_pairs={{0,4},{1,5},{2,6},{3,7},{4,0},{5,1},{6,2},{7,3},{8,12},{9,13},{10,... | collective-permute-start | bytes 1179656 | tf_op jit(solution)/shard_map/ppermute | solution.py:372
  95.7 29.5 %collective-permute-start.26 = (bf16[512,384]{1,0:T(8,128)(2,1)S(1)}, bf16[512,384]{1,0:T(8,128)(2,1)}, u32[]{:S(2)}, u32[]{:S(2)}) collective-permute-start(bf16[512,384]{1,0:T(8,128)(2,1)S(1)} %get-tuple-element.82), channel_id=1, source_target_pairs={{0,6},{1,7},{2,4},{3,5},{4,2},{5,3},{6,0},{7,1},{8,14},{9,15},{10,... | collective-permute-start | bytes 1179656 | tf_op jit(solution)/shard_map/ppermute | solution.py:372
  102.8 45.6 %collective-permute-start.64 = (bf16[128,1024]{1,0:T(8,128)(2,1)S(1)}, bf16[128,1024]{1,0:T(8,128)(2,1)S(1)}, u32[]{:S(2)}, u32[]{:S(2)}) collective-permute-start(bf16[128,1024]{1,0:T(8,128)(2,1)S(1)} %copy-done.34), channel_id=1, source_target_pairs={{0,2},{1,3},{2,0},{3,1},{4,6},{5,7},{6,4},{7,5},{8,10},{9,11},{10,... | collective-permute-start | bytes 786440 | tf_op jit(solution)/shard_map/ppermute | solution.py:372
  103.8 43.5 %collective-permute-start.48 = (bf16[32,2048]{1,0:T(8,128)(2,1)S(1)}, bf16[32,2048]{1,0:T(8,128)(2,1)S(1)}, u32[]{:S(2)}, u32[]{:S(2)}) collective-permute-start(bf16[32,2048]{1,0:T(8,128)(2,1)S(1)} %bitcast.202), channel_id=1, source_target_pairs={{0,1},{1,0},{2,3},{3,2},{4,5},{5,4},{6,7},{7,6},{8,9},{9,8},{10,11... | collective-permute-start | bytes 393224 | tf_op jit(solution)/shard_map/ppermute | solution.py:372
  112.1 39.8 %collective-permute-start.65 = (bf16[128,1024]{1,0:T(8,128)(2,1)S(1)}, bf16[128,1024]{1,0:T(8,128)(2,1)}, u32[]{:S(2)}, u32[]{:S(2)}) collective-permute-start(bf16[128,1024]{1,0:T(8,128)(2,1)S(1)} %copy-done.34), channel_id=1, source_target_pairs={{0,4},{1,5},{2,6},{3,7},{4,0},{5,1},{6,2},{7,3},{8,12},{9,13},{10,... | collective-permute-start | bytes 786440 | tf_op jit(solution)/shard_map/ppermute | solution.py:372
  125.2 47.9 %collective-permute-start.46 = (bf16[512,512]{1,0:T(8,128)(2,1)S(1)}, bf16[512,512]{1,0:T(8,128)(2,1)}, u32[]{:S(2)}, u32[]{:S(2)}) collective-permute-start(bf16[512,512]{1,0:T(8,128)(2,1)S(1)} %bitcast.199), channel_id=1, source_target_pairs={{0,1},{1,0},{2,3},{3,2},{4,5},{5,4},{6,7},{7,6},{8,9},{9,8},{10,11... | collective-permute-start | bytes 1572872 | tf_op jit(solution)/shard_map/ppermute | solution.py:372
  136.9 17.5 %collective-permute-start.27 = (bf16[512,128]{1,0:T(8,128)(2,1)}, bf16[512,128]{1,0:T(8,128)(2,1)S(1)}, u32[]{:S(2)}, u32[]{:S(2)}) collective-permute-start(bf16[512,128]{1,0:T(8,128)(2,1)} %get-tuple-element.43), channel_id=1, source_target_pairs={{0,2},{1,3},{2,0},{3,1},{4,6},{5,7},{6,4},{7,5},{8,10},{9,11},{10,... | collective-permute-start | bytes 393224 | tf_op jit(solution)/shard_map/ppermute | solution.py:372
  164.3 21.8 %collective-permute-start.50 = (bf16[64,2048]{1,0:T(8,128)(2,1)S(1)}, bf16[64,2048]{1,0:T(8,128)(2,1)S(1)}, u32[]{:S(2)}, u32[]{:S(2)}) collective-permute-start(bf16[64,2048]{1,0:T(8,128)(2,1)S(1)} %maximum_select_fusion.3.refs_1_), channel_id=1, source_target_pairs={{0,4},{1,5},{2,6},{3,7},{4,0},{5,1},{6,2},{7,3},{8,12},{9,13},{10,... | collective-permute-start | bytes 786440 | tf_op jit(solution)/shard_map/ppermute | solution.py:372
  170.6 16.7 %collective-permute-start.52 = (bf16[64,2048]{1,0:T(8,128)(2,1)S(1)}, bf16[64,2048]{1,0:T(8,128)(2,1)S(1)}, u32[]{:S(2)}, u32[]{:S(2)}) collective-permute-start(bf16[64,2048]{1,0:T(8,128)(2,1)S(1)} %maximum_select_fusion.3.refs_1_), channel_id=1, source_target_pairs={{0,8},{1,9},{2,10},{3,11},{4,12},{5,13},{6,14},{7,15},{8,0},{9,1},... | collective-permute-start | bytes 786440 | tf_op jit(solution)/shard_map/ppermute | solution.py:372
  172.0 16.6 %collective-permute-start.56 = (bf16[64,2048]{1,0:T(8,128)(2,1)S(1)}, bf16[64,2048]{1,0:T(8,128)(2,1)S(1)}, u32[]{:S(2)}, u32[]{:S(2)}) collective-permute-start(bf16[64,2048]{1,0:T(8,128)(2,1)S(1)} %maximum_select_fusion.3.refs_1_), channel_id=1, source_target_pairs={{0,16},{1,17},{2,18},{3,19},{4,20},{5,21},{6,22},{7,23},{8,24},{9,... | collective-permute-start | bytes 786440 | tf_op jit(solution)/shard_map/ppermute | solution.py:372
  186.1 26.9 %collective-permute-start.80 = (bf16[256,1024]{1,0:T(8,128)(2,1)S(1)}, bf16[256,1024]{1,0:T(8,128)(2,1)S(1)}, u32[]{:S(2)}, u32[]{:S(2)}) collective-permute-start(bf16[256,1024]{1,0:T(8,128)(2,1)S(1)} %bitcast.187), channel_id=1, source_target_pairs={{0,1},{1,0},{2,3},{3,2},{4,5},{5,4},{6,7},{7,6},{8,9},{9,8},{10,11... | collective-permute-start | bytes 1572872 | tf_op jit(solution)/shard_map/ppermute | solution.py:372
  203.8 52.2 %collective-permute-start.47 = (bf16[512,1024]{1,0:T(8,128)(2,1)S(1)}, bf16[512,1024]{1,0:T(8,128)(2,1)}, u32[]{:S(2)}, u32[]{:S(2)}) collective-permute-start(bf16[512,1024]{1,0:T(8,128)(2,1)S(1)} %pad_maximum_fusion.1), channel_id=1, source_target_pairs={{0,1},{1,0},{2,3},{3,2},{4,5},{5,4},{6,7},{7,6},{8,9},{9,8},{10,11... | collective-permute-start | bytes 3145736 | tf_op jit(solution)/shard_map/ppermute | solution.py:372
  216.6 17.0 %collective-permute-start.59 = (bf16[64,2048]{1,0:T(8,128)(2,1)}, bf16[64,2048]{1,0:T(8,128)(2,1)}, u32[]{:S(2)}, u32[]{:S(2)}) collective-permute-start(bf16[64,2048]{1,0:T(8,128)(2,1)} %collective-permute-done.51.refs_4_), channel_id=1, source_target_pairs={{0,16},{1,17},{2,18},{3,19},{4,20},{5,21},{6,22},{7,23},{8,24},{9,... | collective-permute-start | bytes 786440 | tf_op jit(solution)/shard_map/ppermute | solution.py:372
  221.0 18.2 %collective-permute-start.76 = (bf16[128,1024]{1,0:T(8,128)(2,1)}, bf16[128,1024]{1,0:T(8,128)(2,1)}, u32[]{:S(2)}, u32[]{:S(2)}) collective-permute-start(bf16[128,1024]{1,0:T(8,128)(2,1)} %collective-permute-done.68.refs_6_), channel_id=1, source_target_pairs={{0,16},{1,17},{2,18},{3,19},{4,20},{5,21},{6,22},{7,23},{8,24},{9,... | collective-permute-start | bytes 786440 | tf_op jit(solution)/shard_map/ppermute | solution.py:372
  222.2 18.1 %collective-permute-start.77 = (bf16[128,1024]{1,0:T(8,128)(2,1)}, bf16[128,1024]{1,0:T(8,128)(2,1)}, u32[]{:S(2)}, u32[]{:S(2)}) collective-permute-start(bf16[128,1024]{1,0:T(8,128)(2,1)} %collective-permute-done.73.refs_11_), channel_id=1, source_target_pairs={{0,8},{1,9},{2,10},{3,11},{4,12},{5,13},{6,14},{7,15},{8,0},{9,1},... | collective-permute-start | bytes 786440 | tf_op jit(solution)/shard_map/ppermute | solution.py:372
  283.5 22.8 %collective-permute-start.79 = (bf16[256,1024]{1,0:T(8,128)(2,1)}, bf16[256,1024]{1,0:T(8,128)(2,1)}, u32[]{:S(2)}, u32[]{:S(2)}) collective-permute-start(bf16[256,1024]{1,0:T(8,128)(2,1)} %slice.787), channel_id=1, source_target_pairs={{0,1},{1,0},{2,3},{3,2},{4,5},{5,4},{6,7},{7,6},{8,9},{9,8},{10,11... | collective-permute-start | bytes 1572872 | tf_op jit(solution)/shard_map/ppermute | solution.py:372
  284.6 25.4 %collective-permute-start.81 = (bf16[512,1024]{1,0:T(8,128)(2,1)}, bf16[512,1024]{1,0:T(8,128)(2,1)}, u32[]{:S(2)}, u32[]{:S(2)}) collective-permute-start(bf16[512,1024]{1,0:T(8,128)(2,1)} %pad_maximum_fusion.3), channel_id=1, source_target_pairs={{0,1},{1,0},{2,3},{3,2},{4,5},{5,4},{6,7},{7,6},{8,9},{9,8},{10,11... | collective-permute-start | bytes 3145736 | tf_op jit(solution)/shard_map/ppermute | solution.py:372
  290.0 50.0 %collective-permute-start.111 = (bf16[4,64,2048]{2,1,0:T(8,128)(2,1)}, bf16[4,64,2048]{2,1,0:T(8,128)(2,1)}, u32[]{:S(2)}, u32[]{:S(2)}) collective-permute-start(bf16[4,64,2048]{2,1,0:T(8,128)(2,1)} %get-tuple-element.62), channel_id=1, source_target_pairs={{0,16},{1,17},{2,18},{3,19},{4,20},{5,21},{6,22},{7,23},{8,24},{9,... | collective-permute-start | bytes 3145736 | tf_op jit(solution)/shard_map/ppermute | solution.py:372
  291.0 52.2 %collective-permute-start.114 = (bf16[4,64,2048]{2,1,0:T(8,128)(2,1)}, bf16[4,64,2048]{2,1,0:T(8,128)(2,1)}, u32[]{:S(2)}, u32[]{:S(2)}) collective-permute-start(bf16[4,64,2048]{2,1,0:T(8,128)(2,1)} %get-tuple-element.64), channel_id=1, source_target_pairs={{0,8},{1,9},{2,10},{3,11},{4,12},{5,13},{6,14},{7,15},{8,0},{9,1},... | collective-permute-start | bytes 3145736 | tf_op jit(solution)/shard_map/ppermute | solution.py:372
  304.5 33.4 %collective-permute-start.119 = (bf16[4,128,1024]{2,1,0:T(8,128)(2,1)}, bf16[4,128,1024]{2,1,0:T(8,128)(2,1)S(1)}, u32[]{:S(2)}, u32[]{:S(2)}) collective-permute-start(bf16[4,128,1024]{2,1,0:T(8,128)(2,1)} %get-tuple-element.66), channel_id=1, source_target_pairs={{0,16},{1,17},{2,18},{3,19},{4,20},{5,21},{6,22},{7,23},{8,24},{9,... | collective-permute-start | bytes 3145736 | tf_op jit(solution)/shard_map/ppermute | solution.py:372
  306.3 39.2 %collective-permute-start.122 = (bf16[4,128,1024]{2,1,0:T(8,128)(2,1)}, bf16[4,128,1024]{2,1,0:T(8,128)(2,1)}, u32[]{:S(2)}, u32[]{:S(2)}) collective-permute-start(bf16[4,128,1024]{2,1,0:T(8,128)(2,1)} %get-tuple-element.68), channel_id=1, source_target_pairs={{0,8},{1,9},{2,10},{3,11},{4,12},{5,13},{6,14},{7,15},{8,0},{9,1},... | collective-permute-start | bytes 3145736 | tf_op jit(solution)/shard_map/ppermute | solution.py:372
  317.3 32.5 %collective-permute-start.82 = (bf16[512,128]{1,0:T(8,128)(2,1)}, bf16[512,128]{1,0:T(8,128)(2,1)S(1)}, u32[]{:S(2)}, u32[]{:S(2)}) collective-permute-start(bf16[512,128]{1,0:T(8,128)(2,1)} %get-tuple-element.103), channel_id=1, source_target_pairs={{0,2},{1,3},{2,0},{3,1},{4,6},{5,7},{6,4},{7,5},{8,10},{9,11},{10,... | collective-permute-start | bytes 393224 | tf_op jit(solution)/shard_map/ppermute | solution.py:372
  343.2 35.9 %collective-permute-start.102 = (bf16[512,512]{1,0:T(8,128)(2,1)}, bf16[512,512]{1,0:T(8,128)(2,1)}, u32[]{:S(2)}, u32[]{:S(2)}) collective-permute-start(bf16[512,512]{1,0:T(8,128)(2,1)} %get-tuple-element.87), channel_id=1, source_target_pairs={{0,1},{1,0},{2,3},{3,2},{4,5},{5,4},{6,7},{7,6},{8,9},{9,8},{10,11... | collective-permute-start | bytes 1572872 | tf_op jit(solution)/shard_map/ppermute | solution.py:372
  345.5 29.9 %collective-permute-start.112 = (bf16[2,64,2048]{2,1,0:T(8,128)(2,1)}, bf16[2,64,2048]{2,1,0:T(8,128)(2,1)}, u32[]{:S(2)}, u32[]{:S(2)}) collective-permute-start(bf16[2,64,2048]{2,1,0:T(8,128)(2,1)} %add_convert_fusion.7), channel_id=1, source_target_pairs={{0,8},{1,9},{2,10},{3,11},{4,12},{5,13},{6,14},{7,15},{8,0},{9,1},... | collective-permute-start | bytes 1572872 | tf_op jit(solution)/shard_map/ppermute | solution.py:372
  349.9 36.5 %collective-permute-start.115 = (bf16[2,64,2048]{2,1,0:T(8,128)(2,1)}, bf16[2,64,2048]{2,1,0:T(8,128)(2,1)}, u32[]{:S(2)}, u32[]{:S(2)}) collective-permute-start(bf16[2,64,2048]{2,1,0:T(8,128)(2,1)} %add_convert_fusion.6), channel_id=1, source_target_pairs={{0,16},{1,17},{2,18},{3,19},{4,20},{5,21},{6,22},{7,23},{8,24},{9,... | collective-permute-start | bytes 1572872 | tf_op jit(solution)/shard_map/ppermute | solution.py:372
  350.8 38.2 %collective-permute-start.120 = (bf16[2,128,1024]{2,1,0:T(8,128)(2,1)S(1)}, bf16[2,128,1024]{2,1,0:T(8,128)(2,1)}, u32[]{:S(2)}, u32[]{:S(2)}) collective-permute-start(bf16[2,128,1024]{2,1,0:T(8,128)(2,1)S(1)} %add_convert_fusion.4), channel_id=1, source_target_pairs={{0,8},{1,9},{2,10},{3,11},{4,12},{5,13},{6,14},{7,15},{8,0},{9,1},... | collective-permute-start | bytes 1572872 | tf_op jit(solution)/shard_map/ppermute | solution.py:372
  352.1 40.3 %collective-permute-start.123 = (bf16[2,128,1024]{2,1,0:T(8,128)(2,1)}, bf16[2,128,1024]{2,1,0:T(8,128)(2,1)}, u32[]{:S(2)}, u32[]{:S(2)}) collective-permute-start(bf16[2,128,1024]{2,1,0:T(8,128)(2,1)} %add_convert_fusion.3), channel_id=1, source_target_pairs={{0,16},{1,17},{2,18},{3,19},{4,20},{5,21},{6,22},{7,23},{8,24},{9,... | collective-permute-start | bytes 1572872 | tf_op jit(solution)/shard_map/ppermute | solution.py:372
  375.4 20.8 %collective-permute-start.85 = (bf16[512,384]{1,0:T(8,128)(2,1)}, bf16[512,384]{1,0:T(8,128)(2,1)S(1)}, u32[]{:S(2)}, u32[]{:S(2)}) collective-permute-start(bf16[512,384]{1,0:T(8,128)(2,1)} %get-tuple-element.50), channel_id=1, source_target_pairs={{0,2},{1,3},{2,0},{3,1},{4,6},{5,7},{6,4},{7,5},{8,10},{9,11},{10,... | collective-permute-start | bytes 1179656 | tf_op jit(solution)/shard_map/ppermute | solution.py:372
  379.1 38.5 %collective-permute-start.86 = (bf16[512,384]{1,0:T(8,128)(2,1)}, bf16[512,384]{1,0:T(8,128)(2,1)}, u32[]{:S(2)}, u32[]{:S(2)}) collective-permute-start(bf16[512,384]{1,0:T(8,128)(2,1)} %get-tuple-element.51), channel_id=1, source_target_pairs={{0,4},{1,5},{2,6},{3,7},{4,0},{5,1},{6,2},{7,3},{8,12},{9,13},{10,... | collective-permute-start | bytes 1179656 | tf_op jit(solution)/shard_map/ppermute | solution.py:372
  386.4 32.4 %collective-permute-start.87 = (bf16[512,384]{1,0:T(8,128)(2,1)}, bf16[512,384]{1,0:T(8,128)(2,1)S(1)}, u32[]{:S(2)}, u32[]{:S(2)}) collective-permute-start(bf16[512,384]{1,0:T(8,128)(2,1)} %get-tuple-element.52), channel_id=1, source_target_pairs={{0,6},{1,7},{2,4},{3,5},{4,2},{5,3},{6,0},{7,1},{8,14},{9,15},{10,... | collective-permute-start | bytes 1179656 | tf_op jit(solution)/shard_map/ppermute | solution.py:372
  389.0 62.1 %collective-permute-start.103 = (bf16[4,64,512]{2,1,0:T(8,128)(2,1)}, bf16[4,64,512]{2,1,0:T(8,128)(2,1)}, u32[]{:S(2)}, u32[]{:S(2)}) collective-permute-start(bf16[4,64,512]{2,1,0:T(8,128)(2,1)} %get-tuple-element.58), channel_id=1, source_target_pairs={{0,16},{1,17},{2,18},{3,19},{4,20},{5,21},{6,22},{7,23},{8,24},{9,... | collective-permute-start | bytes 786440 | tf_op jit(solution)/shard_map/ppermute | solution.py:372
  392.4 59.7 %collective-permute-start.106 = (bf16[4,64,512]{2,1,0:T(8,128)(2,1)}, bf16[4,64,512]{2,1,0:T(8,128)(2,1)}, u32[]{:S(2)}, u32[]{:S(2)}) collective-permute-start(bf16[4,64,512]{2,1,0:T(8,128)(2,1)} %get-tuple-element.60), channel_id=1, source_target_pairs={{0,8},{1,9},{2,10},{3,11},{4,12},{5,13},{6,14},{7,15},{8,0},{9,1},... | collective-permute-start | bytes 786440 | tf_op jit(solution)/shard_map/ppermute | solution.py:372
  396.2 49.1 %collective-permute-start.117 = (bf16[64,2048]{1,0:T(8,128)(2,1)}, bf16[64,2048]{1,0:T(8,128)(2,1)}, u32[]{:S(2)}, u32[]{:S(2)}) collective-permute-start(bf16[64,2048]{1,0:T(8,128)(2,1)} %get-tuple-element.100), channel_id=1, source_target_pairs={{0,6},{1,7},{2,4},{3,5},{4,2},{5,3},{6,0},{7,1},{8,14},{9,15},{10,... | collective-permute-start | bytes 786440 | tf_op jit(solution)/shard_map/ppermute | solution.py:372
  417.7 29.3 %collective-permute-start.116 = (bf16[64,2048]{1,0:T(8,128)(2,1)}, bf16[64,2048]{1,0:T(8,128)(2,1)}, u32[]{:S(2)}, u32[]{:S(2)}) collective-permute-start(bf16[64,2048]{1,0:T(8,128)(2,1)} %get-tuple-element.99), channel_id=1, source_target_pairs={{0,4},{1,5},{2,6},{3,7},{4,0},{5,1},{6,2},{7,3},{8,12},{9,13},{10,... | collective-permute-start | bytes 786440 | tf_op jit(solution)/shard_map/ppermute | solution.py:372
  418.8 28.3 %collective-permute-start.113 = (bf16[64,2048]{1,0:T(8,128)(2,1)}, bf16[64,2048]{1,0:T(8,128)(2,1)}, u32[]{:S(2)}, u32[]{:S(2)}) collective-permute-start(bf16[64,2048]{1,0:T(8,128)(2,1)} %fusion.30), channel_id=1, source_target_pairs={{0,2},{1,3},{2,0},{3,1},{4,6},{5,7},{6,4},{7,5},{8,10},{9,11},{10,... | collective-permute-start | bytes 786440 | tf_op jit(solution)/shard_map/ppermute | solution.py:372
  446.9 19.3 %collective-permute-start.124 = (bf16[128,1024]{1,0:T(8,128)(2,1)S(1)}, bf16[128,1024]{1,0:T(8,128)(2,1)S(1)}, u32[]{:S(2)}, u32[]{:S(2)}) collective-permute-start(bf16[128,1024]{1,0:T(8,128)(2,1)S(1)} %copy-done.57), channel_id=1, source_target_pairs={{0,4},{1,5},{2,6},{3,7},{4,0},{5,1},{6,2},{7,3},{8,12},{9,13},{10,... | collective-permute-start | bytes 786440 | tf_op jit(solution)/shard_map/ppermute | solution.py:372
  447.0 20.1 %collective-permute-start.121 = (bf16[128,1024]{1,0:T(8,128)(2,1)S(1)}, bf16[128,1024]{1,0:T(8,128)(2,1)S(1)}, u32[]{:S(2)}, u32[]{:S(2)}) collective-permute-start(bf16[128,1024]{1,0:T(8,128)(2,1)S(1)} %copy-done.56), channel_id=1, source_target_pairs={{0,2},{1,3},{2,0},{3,1},{4,6},{5,7},{6,4},{7,5},{8,10},{9,11},{10,... | collective-permute-start | bytes 786440 | tf_op jit(solution)/shard_map/ppermute | solution.py:372
  451.1 34.1 %collective-permute-start.88 = (bf16[256,1024]{1,0:T(8,128)(2,1)}, bf16[256,1024]{1,0:T(8,128)(2,1)S(1)}, u32[]{:S(2)}, u32[]{:S(2)}) collective-permute-start(bf16[256,1024]{1,0:T(8,128)(2,1)} %slice.786), channel_id=1, source_target_pairs={{0,1},{1,0},{2,3},{3,2},{4,5},{5,4},{6,7},{7,6},{8,9},{9,8},{10,11... | collective-permute-start | bytes 1572872 | tf_op jit(solution)/shard_map/ppermute | solution.py:372
  452.2 59.0 %collective-permute-start.94 = (bf16[4,64,1536]{2,1,0:T(8,128)(2,1)}, bf16[4,64,1536]{2,1,0:T(8,128)(2,1)}, u32[]{:S(2)}, u32[]{:S(2)}) collective-permute-start(bf16[4,64,1536]{2,1,0:T(8,128)(2,1)} %get-tuple-element.54), channel_id=1, source_target_pairs={{0,16},{1,17},{2,18},{3,19},{4,20},{5,21},{6,22},{7,23},{8,24},{9,... | collective-permute-start | bytes 2359304 | tf_op jit(solution)/shard_map/ppermute | solution.py:372
  456.4 21.3 %collective-permute-start.104 = (bf16[2,64,512]{2,1,0:T(8,128)(2,1)S(1)}, bf16[2,64,512]{2,1,0:T(8,128)(2,1)S(1)}, u32[]{:S(2)}, u32[]{:S(2)}) collective-permute-start(bf16[2,64,512]{2,1,0:T(8,128)(2,1)S(1)} %add_convert_fusion.17), channel_id=1, source_target_pairs={{0,8},{1,9},{2,10},{3,11},{4,12},{5,13},{6,14},{7,15},{8,0},{9,1},... | collective-permute-start | bytes 393224 | tf_op jit(solution)/shard_map/ppermute | solution.py:372
  482.6 27.4 %collective-permute-start.97 = (bf16[4,64,1536]{2,1,0:T(8,128)(2,1)}, bf16[4,64,1536]{2,1,0:T(8,128)(2,1)S(1)}, u32[]{:S(2)}, u32[]{:S(2)}) collective-permute-start(bf16[4,64,1536]{2,1,0:T(8,128)(2,1)} %get-tuple-element.56), channel_id=1, source_target_pairs={{0,8},{1,9},{2,10},{3,11},{4,12},{5,13},{6,14},{7,15},{8,0},{9,1},... | collective-permute-start | bytes 2359304 | tf_op jit(solution)/shard_map/ppermute | solution.py:372
  489.3 17.1 %collective-permute-start.110 = (f32[32,512]{1,0:T(8,128)S(1)}, f32[32,512]{1,0:T(8,128)S(1)}, u32[]{:S(2)}, u32[]{:S(2)}) collective-permute-start(f32[32,512]{1,0:T(8,128)S(1)} %get-tuple-element.116), channel_id=1, source_target_pairs={{0,1},{1,0},{2,3},{3,2},{4,5},{5,4},{6,7},{7,6},{8,9},{9,8},{10,11... | collective-permute-start | bytes 196616 | tf_op jit(solution)/shard_map/ppermute | solution.py:372
  (182 other events, 2439.2 us)

commit v2 on v1

--- a/solution.py
+++ b/solution.py
@@ -3,6 +3,7 @@
 from jax import lax
 from jax.experimental import pallas as pl
 from jax.experimental.pallas import tpu as pltpu
+from jax.sharding import Mesh
 from jax.sharding import PartitionSpec as P
 
 D = 1024
@@ -358,7 +359,8 @@
     return (result.astype(jnp.bfloat16)[None], input_gradient[None]) + tuple(gradient_sums)
 
 
-ALL = ("dp", "sp")
+ALL = ("dp", "z", "core")
+CHIPS = ("dp", "z")
 CORE_BIT = 1
 Z_BITS = (0, 2, 4, 6)
 X_BIT = 8
@@ -368,82 +370,78 @@
 
 
 def swapped(value, mask):
-    count = lax.axis_size("dp") * lax.axis_size("sp")
+    count = lax.axis_size(ALL)
     return lax.ppermute(value, ALL, [(source, source ^ mask) for source in range(count)])
 
 
 def placed_kernel(slot_ref, *refs, col_blocks):
-    pieces, out_ref, sem = refs[:16], refs[16], refs[17]
-    width = pieces[0].shape[1] // col_blocks
+    pieces, out_ref, sem = refs[:-2], refs[-2], refs[-1]
+    width = out_ref.shape[2] // col_blocks
     copies = []
-    for at in range(16):
-        row = slot_ref[at]
-        for col in range(col_blocks):
-            if col_blocks == 1:
-                target = out_ref.at[row]
-                source = pieces[at]
-            else:
-                source = pieces[at].at[:, pl.ds(col * width, width)]
-                to = pl.multiple_of(slot_ref[16 + col] * width, 128)
-                target = out_ref.at[row, :, pl.ds(to, width)]
-            copy = pltpu.make_async_copy(source, target, sem.at[at * col_blocks + col])
-            copy.start()
-            copies.append(copy)
+    for piece in pieces:
+        for within in range(piece.shape[0]):
+            row = slot_ref[len(copies) // col_blocks]
+            for col in range(col_blocks):
+                if col_blocks == 1:
+                    source, target = piece.at[within], out_ref.at[row]
+                else:
+                    source = piece.at[within, :, pl.ds(col * width, width)]
+                    to = pl.multiple_of(slot_ref[16 + col] * width, 128)
+                    target = out_ref.at[row, :, pl.ds(to, width)]
+                copy = pltpu.make_async_copy(source, target, sem.at[len(copies)])
+                copy.start()
+                copies.append(copy)
     for copy in copies:
         copy.wait()
 
 
 def placed(pieces, slots, col_blocks=1):
-    rows, cols = pieces[0].shape
+    rows, cols = pieces[0].shape[1:]
     return pl.pallas_call(
         lambda *refs: placed_kernel(*refs, col_blocks=col_blocks),
         out_shape=jax.ShapeDtypeStruct((16, rows, cols), pieces[0].dtype),
-        in_specs=[pl.BlockSpec(memory_space=pltpu.SMEM)] + [pl.BlockSpec(memory_space=pl.ANY)] * 16,
+        in_specs=[pl.BlockSpec(memory_space=pltpu.SMEM)]
+        + [pl.BlockSpec(memory_space=pl.ANY)] * len(pieces),
         out_specs=pl.BlockSpec(memory_space=pltpu.VMEM),
         scratch_shapes=[pltpu.SemaphoreType.DMA((16 * col_blocks,))],
         name="placed",
     )(slots, *pieces)
 
 
-def spread_kernel(slot_ref, whole_ref, *refs, col_blocks):
-    outs, sem = refs[:4], refs[4]
+def spread_kernel(slot_ref, whole_ref, *refs, groups, col_blocks):
+    outs, sem = refs[:-1], refs[-1]
     width = whole_ref.shape[2] // col_blocks
     copies = []
-    for at in range(16):
-        row = slot_ref[at]
-        across, along = at // 4, at % 4
-        if along < 2:
-            group, place = (0, across * 2 + along) if across < 2 else (1, (across - 2) * 2 + along)
-        else:
-            group, place = (2 + across % 2, (across // 2) * 2 + along - 2)
-        for col in range(col_blocks):
-            if col_blocks == 1:
-                source, target = whole_ref.at[row], outs[group].at[place]
-            else:
-                to = pl.multiple_of(slot_ref[16 + col] * width, 128)
-                source = whole_ref.at[row, :, pl.ds(to, width)]
-                target = outs[group].at[place, :, pl.ds(col * width, width)]
-            copy = pltpu.make_async_copy(source, target, sem.at[at * col_blocks + col])
-            copy.start()
-            copies.append(copy)
+    for out_ref, members in zip(outs, groups):
+        for place, at in enumerate(members):
+            row = slot_ref[at]
+            for col in range(col_blocks):
+                if col_blocks == 1:
+                    source, target = whole_ref.at[row], out_ref.at[place]
+                else:
+                    to = pl.multiple_of(slot_ref[16 + col] * width, 128)
+                    source = whole_ref.at[row, :, pl.ds(to, width)]
+                    target = out_ref.at[place, :, pl.ds(col * width, width)]
+                copy = pltpu.make_async_copy(source, target, sem.at[len(copies)])
+                copy.start()
+                copies.append(copy)
     for copy in copies:
         copy.wait()
 
 
-def spread(whole, slots, col_blocks=1):
+def spread(whole, slots, groups, col_blocks=1):
     rows, cols = whole.shape[1:]
     return pl.pallas_call(
-        lambda *refs: spread_kernel(*refs, col_blocks=col_blocks),
-        out_shape=[jax.ShapeDtypeStruct((4, rows, cols), whole.dtype)] * 4,
+        lambda *refs: spread_kernel(*refs, groups=groups, col_blocks=col_blocks),
+        out_shape=[jax.ShapeDtypeStruct((len(group), rows, cols), whole.dtype) for group in groups],
         in_specs=[pl.BlockSpec(memory_space=pltpu.SMEM), pl.BlockSpec(memory_space=pl.ANY)],
-        out_specs=[pl.BlockSpec(memory_space=pltpu.VMEM)] * 4,
+        out_specs=[pl.BlockSpec(memory_space=pltpu.VMEM)] * len(groups),
         scratch_shapes=[pltpu.SemaphoreType.DMA((16 * col_blocks,))],
         name="spread",
     )(slots, whole)
 
 
-def collected(piece):
-    line = [piece] + [swapped(piece, bits) for bits in Z_BITS[1:]]
+def collected(line):
     found = {}
     for along in range(4):
         first, second = (X_BIT, Y_BIT) if along < 2 else (Y_BIT, X_BIT)
@@ -451,13 +449,26 @@
         found[first >> 3, along] = swapped(line[along], first)
         found[second >> 3, along] = swapped(line[along], second)
         found[3, along] = swapped(found[first >> 3, along], second)
-    return [found[across, along] for across in range(4) for along in range(4)]
-
-
-def summed(whole, slots, col_blocks=1):
-    low = jnp.bfloat16
-    full = jnp.float32
-    keep_a, send_a, keep_b, send_b = spread(whole, slots, col_blocks)
+    return [found[across, along][None] for across in range(4) for along in range(4)]
+
+
+def collected_small(line):
+    stacked = jnp.stack(line)
+    beside = swapped(stacked, X_BIT)
+    return [stacked, beside, swapped(stacked, Y_BIT), swapped(beside, Y_BIT)]
+
+
+def summed_along(parts):
+    total = parts[0]
+    for along in (1, 2, 3):
+        total = total + swapped(parts[along].astype(jnp.bfloat16), Z_BITS[along]).astype(jnp.float32)
+    return total
+
+
+def summed(whole, slots, col_blocks):
+    low, full = jnp.bfloat16, jnp.float32
+    groups = ((0, 1, 4, 5), (8, 9, 12, 13), (2, 3, 10, 11), (6, 7, 14, 15))
+    keep_a, send_a, keep_b, send_b = spread(whole, slots, groups, col_blocks)
     got_a = swapped(send_a, Y_BIT)
     got_b = swapped(send_b, X_BIT)
     onward_a = (keep_a[2:].astype(full) + got_a[2:].astype(full)).astype(low)
@@ -466,12 +477,16 @@
     here_b = keep_b[:2].astype(full) + got_b[:2].astype(full)
     here_a = here_a + swapped(onward_a, X_BIT).astype(full)
     here_b = here_b + swapped(onward_b, Y_BIT).astype(full)
-    return (
-        here_a[0]
-        + swapped(here_a[1].astype(low), Z_BITS[1]).astype(full)
-        + swapped(here_b[0].astype(low), Z_BITS[2]).astype(full)
-        + swapped(here_b[1].astype(low), Z_BITS[3]).astype(full)
-    )
+    return summed_along((here_a[0], here_a[1], here_b[0], here_b[1]))
+
+
+def summed_small(whole, slots):
+    low, full = jnp.bfloat16, jnp.float32
+    keep, send = spread(whole, slots, (tuple(range(8)), tuple(range(8, 16))))
+    got = swapped(send, Y_BIT)
+    onward = (keep[4:].astype(full) + got[4:].astype(full)).astype(low)
+    here = keep[:4].astype(full) + got[:4].astype(full)
+    return summed_along(here + swapped(onward, X_BIT).astype(full))
 
 
 def lanes_low(rows):
@@ -710,10 +725,9 @@
     cotangent,
 ):
     low, full = jnp.bfloat16, jnp.float32
-    position = lax.axis_index("sp")
     group = lax.axis_index("dp")
-    core = position % 2
-    depth = position // 2
+    core = lax.axis_index("core")
+    depth = lax.axis_index("z")
     even = core == 0
     own_rows = inputs.shape[1]
     share = joint_weight.shape[0]
@@ -743,27 +757,47 @@
         ((chip_ids // 4) ^ depth) * 4 + (((chip_ids // 2) % 2) ^ core) * 2 + chip_ids % 2
     ]
 
-    small = jnp.concatenate(
+    def line_of(piece):
+        return [piece] + [swapped(piece, bits) for bits in Z_BITS[1:]]
+
+    units = expand_weight.shape[1] // 2
+    joint_parts = joint_weight.reshape(share, 3, 2, 4, 128).transpose(2, 0, 3, 1, 4).reshape(2, share, 1536)
+    joint_line = line_of(cores_exchanged((joint_parts[0], joint_parts[1])))
+    joint_full = placed(collected(joint_line), joint_slots, 4).reshape(D, 1536)
+    expand_parts = expand_weight.reshape(share, 16, 2, 128)
+    expand_own = cores_exchanged(
+        (expand_parts[:, :, 0].reshape(share, units), expand_parts[:, :, 1].reshape(share, units))
+    )
+    hidden_own = jnp.concatenate([expand_own[:, : units // 2], expand_own[:, units // 2 :], reduce_weight])
+    hidden_full = lax.all_gather(hidden_own, CHIPS, axis=0, tiled=False)
+    expand_full = hidden_full[:, :128].reshape(16, 2, 64, D).transpose(0, 2, 1, 3).reshape(D, units)
+    reduce_full = hidden_full[:, 128:].reshape(units, D)
+
+    count = share
+    small = jnp.stack(
         [
-            first_gain,
-            first_shift,
-            query_bias,
-            value_bias,
-            mixer_bias,
-            second_gain,
-            second_shift,
-            reduce_bias,
-            expand_bias,
+            jnp.pad(item, (0, 128 - item.shape[0]))
+            for item in (
+                first_gain,
+                first_shift,
+                query_bias,
+                value_bias,
+                mixer_bias,
+                second_gain,
+                second_shift,
+                reduce_bias,
+                expand_bias,
+            )
         ]
-    ).reshape(1, -1)
-    small_line = chip_order(small, swapped(small, CORE_BIT))[None]
-    small_line = jnp.concatenate([small_line] + [swapped(small_line, bits) for bits in Z_BITS[1:]])
-    small_all = jnp.concatenate(
-        [small_line[None]] + [swapped(small_line, bits)[None] for bits in (X_BIT, Y_BIT, X_BIT + Y_BIT)]
+    )
+    small, _ = lax.optimization_barrier((small, joint_line[3]))
+    small_line = jnp.stack(line_of(chip_order(small[None], swapped(small, CORE_BIT)[None])))
+    small_all = jnp.stack(
+        [small_line] + [swapped(small_line, bits) for bits in (X_BIT, Y_BIT, X_BIT + Y_BIT)]
     ).reshape(16, -1)
     pick = (slots[None, :] == chip_ids[:, None]).astype(low)
-    small_all = product(pick, small_all).reshape(32, -1)
-    count = share
+    small_all = product(pick, small_all).reshape(32, 9, 128).transpose(1, 0, 2)
+    rows_of = small_all[:8, :, :count].reshape(8, 32 * count)
     (
         gain_one,
         shift_one,
@@ -773,28 +807,19 @@
         gain_two,
         shift_two,
         reduce_shift,
-    ) = [small_all[:, at * count : (at + 1) * count].reshape(-1) for at in range(8)]
-    expand_shift = small_all[:, 8 * count :].reshape(16, 2, 128)
+    ) = [rows_of[at] for at in range(8)]
+    expand_shift = small_all[8].reshape(16, 2, 128)
     expand_shift = jnp.where(even, expand_shift[:, 0], expand_shift[:, 1]).reshape(-1)
 
-    joint_parts = joint_weight.reshape(share, 3, 2, 4, 128).transpose(2, 0, 3, 1, 4).reshape(2, share, 1536)
-    joint_own = cores_exchanged((joint_parts[0], joint_parts[1]))
-    joint_full = placed(collected(joint_own), joint_slots, 4).reshape(D, 1536)
     mixer_own = cores_exchanged((mixer_weight[:, : D // 2], mixer_weight[:, D // 2 :]))
-    mixer_cols = placed(collected(mixer_own), mixer_slots).reshape(2, D // 2, D // 2)
+    mixer_own, joint_full = lax.optimization_barrier((mixer_own, joint_full))
+    mixer_cols = placed(collected_small(line_of(mixer_own)), mixer_slots).reshape(2, D // 2, D // 2)
     mixer_mine, mixer_theirs = mixer_cols[0], swapped(mixer_cols[1], CORE_BIT)
     mixer_full = jnp.where(
         even,
         jnp.concatenate([mixer_mine, mixer_theirs], axis=1),
         jnp.concatenate([mixer_theirs, mixer_mine], axis=1),
     )
-    units = expand_weight.shape[1] // 2
-    expand_parts = expand_weight.reshape(share, 16, 2, 128)
-    expand_own = cores_exchanged(
-        (expand_parts[:, :, 0].reshape(share, units), expand_parts[:, :, 1].reshape(share, units))
-    )
-    expand_full = placed(collected(expand_own), slots).reshape(D, units)
-    reduce_full = placed(collected(reduce_weight), slots).reshape(units, D)
 
     token_rows = own_first(inputs[0]).astype(full)
     upstream = own_first(cotangent[0])
@@ -833,10 +858,13 @@
     result = middle[:own_rows] + (own_sum(product(active, reduce_full)) + reduce_shift)
 
     reduce_gradient = inner_rows(active, upstream).astype(low).reshape(16, 128, D)
-    reduce_sum = summed(reduce_gradient, slots)
     grad_before = gelu_pull(inner_cols(upstream, reduce_full))[0].astype(low)
-    expand_gradient = inner_rows(second, grad_before).astype(low).reshape(16, 64, units)
-    expand_sum = summed(expand_gradient, slots)
+    expand_gradient = inner_rows(second, grad_before).astype(low)
+    expand_gradient = expand_gradient.reshape(16, 64, 2, D).transpose(0, 2, 1, 3).reshape(16, 128, D)
+    hidden_gradient = jnp.concatenate([expand_gradient, reduce_gradient], axis=1)
+    hidden_sum = lax.psum_scatter(hidden_gradient, CHIPS, scatter_dimension=0, tiled=False)
+    reduce_sum = hidden_sum[128:].astype(full)
+    expand_sum = jnp.concatenate([hidden_sum[:64], hidden_sum[64:128]], axis=1)
     expand_shift_gradient = jnp.sum(grad_before.astype(full), axis=0)
     grad_second = both_cores(inner_cols(grad_before, expand_full))
     upstream_full = upstream.astype(full)
@@ -849,7 +877,7 @@
     mixer_keep = jnp.where(even, mixer_gradient[:, : D // 2], mixer_gradient[:, D // 2 :])
     mixer_send = jnp.where(even, mixer_gradient[:, D // 2 :], mixer_gradient[:, : D // 2])
     mixer_whole = jnp.concatenate([mixer_keep, swapped(mixer_send, CORE_BIT)], axis=0)
-    mixer_sum = summed(mixer_whole.reshape(16, 64, D // 2), mixer_slots)
+    mixer_sum = summed_small(mixer_whole.reshape(16, 64, D // 2), mixer_slots)
     grad_out = head_backward(joint_sorted, mixed_sorted, totals_sorted, grad_pieces, places)
     grad_joint = jnp.concatenate(
         [grad_out[0]] + [swapped(grad_out[at], Z_BITS[at]) for at in (1, 2, 3)], axis=1
@@ -893,7 +921,7 @@
     )
     for mask in (CORE_BIT, Z_BITS[1], Z_BITS[2], X_BIT, Y_BIT):
         sums = sums + swapped(sums, mask)
-    own_sums = lax.dynamic_slice_in_dim(sums, group * 8 + position, 1, axis=0)[0]
+    own_sums = lax.dynamic_slice_in_dim(sums, group * 8 + depth * 2 + core, 1, axis=0)[0]
     vectors = [own_sums[at * count : (at + 1) * count] for at in range(8)] + [own_sums[8 * count :]]
 
     def finished(total):
@@ -903,7 +931,7 @@
 
     joint_out = finished(joint_sum).reshape(2, share, 4, 3, 128).transpose(1, 3, 0, 2, 4)
     mixer_out = finished(mixer_sum).transpose(1, 0, 2)
-    expand_out = finished(expand_sum).reshape(2, share, 16, 128).transpose(1, 2, 0, 3)
+    expand_out = finished(expand_sum).reshape(2, share, 16, 128).transpose(1, 2, 0, 3).astype(full)
     return (
         result.astype(low)[None],
         input_gradient[None],
@@ -924,41 +952,48 @@
 
 
 def solution(mesh):
+    dp_size, sp_size = mesh.shape["dp"], mesh.shape["sp"]
+    if dp_size == 4 and sp_size == 8:
+        mesh = Mesh(mesh.devices.reshape(dp_size, sp_size // 2, 2), ALL)
+        body, line = chip_body, ("z", "core")
+    else:
+        body, line = ring_body, ("sp",)
+    rows = P("dp", line, None)
+    vector = P(("dp",) + line)
+    matrix = P(("dp",) + line, None)
     in_specs = (
-        P("dp", "sp", None),
+        rows,
         P(),
-        P(("dp", "sp")),
-        P(("dp", "sp")),
-        P(("dp", "sp"), None),
-        P(("dp", "sp")),
-        P(("dp", "sp")),
-        P(("dp", "sp"), None),
-        P(("dp", "sp")),
-        P(("dp", "sp")),
-        P(("dp", "sp")),
-        P(("dp", "sp"), None),
-        P(("dp", "sp")),
-        P(("dp", "sp"), None),
-        P(("dp", "sp")),
-        P("dp", "sp", None),
+        vector,
+        vector,
+        matrix,
+        vector,
+        vector,
+        matrix,
+        vector,
+        vector,
+        vector,
+        matrix,
+        vector,
+        matrix,
+        vector,
+        rows,
     )
     out_specs = (
-        P("dp", "sp", None),
-        P("dp", "sp", None),
-        P(("dp", "sp")),
-        P(("dp", "sp")),
-        P(("dp", "sp"), None),
-        P(("dp", "sp")),
-        P(("dp", "sp")),
-        P(("dp", "sp"), None),
-        P(("dp", "sp")),
-        P(("dp", "sp")),
-        P(("dp", "sp")),
-        P(("dp", "sp"), None),
-        P(("dp", "sp")),
-        P(("dp", "sp"), None),
-        P(("dp", "sp")),
-    )
-    whole_pairs = mesh.shape["dp"] == 4 and mesh.shape["sp"] == 8
-    body = chip_body if whole_pairs else ring_body
+        rows,
+        rows,
+        vector,
+        vector,
+        matrix,
+        vector,
+        vector,
+        matrix,
+        vector,
+        vector,
+        vector,
+        matrix,
+        vector,
+        matrix,
+        vector,
+    )
     return jax.shard_map(body, mesh=mesh, in_specs=in_specs, out_specs=out_specs, check_vma=False)

time: 544 us -> 575 us (1.057)
  waiting for transfers between devices: 172 us -> 219 us
  starting transfers between devices: 159 us -> 120 us
  local copies, waits for them, and re-layouts: 41.8 us -> 75 us
  Pallas kernels: 67.7 us -> 48.1 us
  between operations: 2.45 us -> 15.7 us
    ppermute x126 -> x71, waiting for transfers between devices: 172 us -> 219 us  [swapped(): lax.ppermute(value, ALL, [(source, source ^ mask) for source in range(cou...]
    ppermute x126 -> x71, starting transfers between devices: 159 us -> 120 us  [swapped(): lax.ppermute(value, ALL, [(source, source ^ mask) for source in range(cou...]
    reshape x2 -> x3, local copies, waits for them, and re-layouts: 0.02 us -> 16.4 us  [the longest x1 16.4 us: chip_body(): expand_gradient.reshape(16, 64, 2, D).transpose(0, 2, 1, 3)]
    transpose x1 -> x2, local copies, waits for them, and re-layouts: 0.41 us -> 14.3 us  [the longest x1 8.55 us: chip_body(): hidden_full[:, :128].reshape(16, 2, 64, D).transpose(0, 2, 1, 3)]
    pallas_call x4 -> x2, Pallas kernels: 17.8 us -> 7.78 us  [placed(): pl.pallas_call(lambda *refs: placed_kernel(*refs, col_blocks=col_blocks),...]
    pallas_call x4 -> x2, Pallas kernels: 17.9 us -> 8.06 us  [spread(): pl.pallas_call(lambda *refs: spread_kernel(*refs, groups=groups, col_bloc...]
    concatenate x2, other arithmetic: 0.06 us -> 8.99 us  [the longest x1 8.16 us: chip_body(): jnp.concatenate([expand_gradient, reduce_gradient], axis=1)]
    unnamed x217 -> x157, local copies, waits for them, and re-layouts: 10.3 us -> 17.3 us
  transfers between devices with their start and end apart: 126 -> 73, of which waited for: 45 -> 33; matrix products, arithmetic and copies ran while one was open for 18% -> 18% of each run, Pallas kernels for 13% -> 8%
where the time goes in v2:
time: 575 us; the launch traced here: 567 us
  waiting for transfers between devices  219 us (38%)
  starting transfers between devices  120 us (21%)
  local copies, waits for them, and re-layouts  75 us (13%)
  Pallas kernels  48.1 us (8%)
  matrix products  44.9 us (8%)
  other arithmetic  44.2 us (8%)
  between operations  15.7 us (3%)
    ppermute x71, waiting for transfers between devices, swapped(): lax.ppermute(value, ALL, [(source, source ^ mask) for source in range(cou...  219 us
    ppermute x71, starting transfers between devices, swapped(): lax.ppermute(value, ALL, [(source, source ^ mask) for source in range(cou...  120 us
    pallas_call x1, Pallas kernels, head_backward(): pl.pallas_call(head_backward_kernel, out_shape=[jax.ShapeDtypeStruct((row...  20.5 us
    unnamed x157, local copies, waits for them, and re-layouts  17.3 us
    dot_general x4, matrix products, inner_cols(): lax.dot_general(left, right, (((1,), (1,)), ((), ())), preferred_element_...  16.4 us
    reshape x1, local copies, waits for them, and re-layouts, chip_body(): expand_gradient.reshape(16, 64, 2, D).transpose(0, 2, 1, 3)  16.4 us
    dot_general x4, matrix products, inner_rows(): lax.dot_general(left, right, (((0,), (0,)), ((), ())), preferred_element_...  15.6 us
    dot_general x7, matrix products, product(): return jnp.dot(left, right, preferred_element_type=jnp.float32)  13 us
  transfers between devices with their start and end apart: 73, of which 33 were waited for; matrix products, arithmetic and copies ran while one was open for 18% of the time, Pallas kernels for 8%

profile of v2, /device:TPU:0, one launch (start us, length us, event | category | flops | bytes accessed | tf_op | source)
XLA Modules:
  0.0 567.4 jit_solution(6123821789641272099)
XLA Ops:
  13.4 5.0 collective-permute-start.2
  19.2 4.5 collective-permute-done.2
  23.7 7.2 %collective-permute-start.11 = (bf16[64,1536]{1,0:T(8,128)(2,1)S(1)}, bf16[64,1536]{1,0:T(8,128)(2,1)S(1)}, u32[]{:S(2)}, u32[]{:S(2)}) collective-permute-start(bf16[64,1536]{1,0:T(8,128)(2,1)S(1)} %maximum_select_fusion.4), channel_id=1, source_target_pairs={{0,2},{1,3},{2,0},{3,1},{4,6},{5,7},{6,4},{7,5},{8,10},{9,11},{10,... | collective-permute-start | bytes 589832 | tf_op jit(solution)/shard_map/ppermute | solution.py:374
  31.0 4.4 collective-permute-start.6
  36.0 8.2 %collective-permute-done.6 = bf16[2,9,128]{2,1,0:T(8,128)(2,1)S(1)} collective-permute-done((bf16[2,9,128]{2,1,0:T(8,128)(2,1)S(1)}, bf16[2,9,128]{2,1,0:T(8,128)(2,1)S(1)}, u32[]{:S(2)}, u32[]{:S(2)}) %collective-permute-start.6) | collective-permute-done | bytes 4640 | tf_op jit(solution)/shard_map/ppermute | solution.py:374
  54.4 16.4 %collective-permute-done.12 = bf16[64,1536]{1,0:T(8,128)(2,1)S(1)} collective-permute-done((bf16[64,1536]{1,0:T(8,128)(2,1)S(1)}, bf16[64,1536]{1,0:T(8,128)(2,1)S(1)}, u32[]{:S(2)}, u32[]{:S(2)}) %collective-permute-start.12) | collective-permute-done | bytes 196640 | tf_op jit(solution)/shard_map/ppermute | solution.py:374
  75.7 6.8 %collective-permute-done.14 = bf16[64,1536]{1,0:T(8,128)(2,1)} collective-permute-done((bf16[64,1536]{1,0:T(8,128)(2,1)S(1)}, bf16[64,1536]{1,0:T(8,128)(2,1)}, u32[]{:S(2)}, u32[]{:S(2)}) %collective-permute-start.14) | collective-permute-done | bytes 196640 | tf_op jit(solution)/shard_map/ppermute | solution.py:374
  90.4 4.5 collective-permute-done.21
  94.9 7.1 %collective-permute-done.22 = bf16[64,1536]{1,0:T(8,128)(2,1)S(1)} collective-permute-done((bf16[64,1536]{1,0:T(8,128)(2,1)}, bf16[64,1536]{1,0:T(8,128)(2,1)S(1)}, u32[]{:S(2)}, u32[]{:S(2)}) %collective-permute-start.22) | collective-permute-done | bytes 196640 | tf_op jit(solution)/shard_map/ppermute | solution.py:374
  102.8 4.8 placed.2
  112.1 3.5 collective-permute-done.33
  115.6 6.3 %collective-permute-done.32 = bf16[64,512]{1,0:T(8,128)(2,1)S(1)} collective-permute-done((bf16[64,512]{1,0:T(8,128)(2,1)S(1)}, bf16[64,512]{1,0:T(8,128)(2,1)S(1)}, u32[]{:S(2)}, u32[]{:S(2)}) %collective-permute-start.32) | collective-permute-done | bytes 65568 | tf_op jit(solution)/shard_map/ppermute | solution.py:374
  122.0 3.8 fusion.7
  128.0 3.5 collective-permute-done.34.refs_2_
  145.0 20.2 %collective-permute-done.25.refs_1_ = bf16[512,384]{1,0:T(8,128)(2,1)} collective-permute-done((bf16[512,384]{1,0:T(8,128)(2,1)}, bf16[512,384]{1,0:T(8,128)(2,1)}, u32[]{:S(2)}, u32[]{:S(2)}) %collective-permute-start.25) | collective-permute-done | bytes 393248 | tf_op jit(solution)/shard_map/ppermute | solution.py:374
  165.2 10.1 %collective-permute-done.26.refs_2_ = bf16[512,384]{1,0:T(8,128)(2,1)} collective-permute-done((bf16[512,384]{1,0:T(8,128)(2,1)S(1)}, bf16[512,384]{1,0:T(8,128)(2,1)}, u32[]{:S(2)}, u32[]{:S(2)}) %collective-permute-start.26) | collective-permute-done | bytes 393248 | tf_op jit(solution)/shard_map/ppermute | solution.py:374
  175.3 11.8 %head_forward.1 = (bf16[512,128]{1,0:T(8,128)(2,1)}, bf16[512,128]{1,0:T(8,128)(2,1)}, bf16[512,128]{1,0:T(8,128)(2,1)}, bf16[512,128]{1,0:T(8,128)(2,1)}, bf16[...) custom-call(s32[16]{0:T(128)} %gather_fusion, bf16[512,384]{1,0:T(8,128)(2,1)} %get-tuple-element.83.refs_0_, ...), custom_call_target="tpu_custom_call" | custom-call | tf_op jit(solution)/shard_map/head_forward/pallas_call | solution.py:558
  187.1 8.1 %collective-permute-start.28 = (bf16[512,128]{1,0:T(8,128)(2,1)}, bf16[512,128]{1,0:T(8,128)(2,1)S(1)}, u32[]{:S(2)}, u32[]{:S(2)}) collective-permute-start(bf16[512,128]{1,0:T(8,128)(2,1)} %get-tuple-element.38), channel_id=1, source_target_pairs={{0,2},{1,3},{2,0},{3,1},{4,6},{5,7},{6,4},{7,5},{8,10},{9,11},{10,... | collective-permute-start | bytes 393224 | tf_op jit(solution)/shard_map/ppermute | solution.py:374
  199.5 7.7 %collective-permute-done.29 = bf16[512,128]{1,0:T(8,128)(2,1)S(1)} collective-permute-done((bf16[512,128]{1,0:T(8,128)(2,1)}, bf16[512,128]{1,0:T(8,128)(2,1)S(1)}, u32[]{:S(2)}, u32[]{:S(2)}) %collective-permute-start.29) | collective-permute-done | bytes 131104 | tf_op jit(solution)/shard_map/ppermute | solution.py:374
  207.3 3.5 fusion.87
  215.4 3.9 fusion.77
  221.3 6.3 %fusion.78 = (bf16[16,128,1024]{2,1,0:T(8,128)(2,1)}, bf16[16,128,1024]{2,1,0:T(8,128)(2,1)}) fusion(bf16[16,256,1024]{2,1,0:T(8,128)(2,1)} %bitcast.203), kind=kLoop, calls=%fused_computation.248 | loop fusion | bytes 16777216 | tf_op jit(solution)/shard_map/slice | solution.py:773
  227.6 8.6 %copy.46 = bf16[16,64,2,1024]{3,2,1,0:T(2,128)(2,1)} copy(bf16[16,64,2,1024]{3,1,2,0:T(8,128)(2,1)} %bitcast.201) | data formatting | bytes 8388608 | tf_op jit(solution)/shard_map/transpose | solution.py:773
  236.1 3.8 copy.56
  244.6 6.2 %convert_reduce_fusion = (f32[2048]{0:T(1024)S(1)}, bf16[512,2048]{1,0:T(8,128)(2,1)S(1)}) fusion(f32[512,2048]{1,0:T(8,128)S(1)} %fusion.22, f32[2048]{0:T(1024)S(1)} %bitcast.263, bf16[2048,1024]{1,0:T(8,128)(2,1)S(1)} %bitcast.213, bf16[256,1024]{1,0:T(8,128)(2,1)} %collective-permute-done.41, bf16[256,1024]{1,0:T(8,128)(2,1)} %bitcast.55), kind=kOutput, calls=%fused_computation.11 | convolution fusion | flops 2173696000 | bytes 11550720 | tf_op jit(solution)/shard_map/dot_general | solution.py:45
  252.1 4.5 convolution_convert_fusion.1
  256.6 16.4 %reshape.613 = bf16[16,64,2,1024]{3,2,1,0:T(2,128)(2,1)} reshape(bf16[1024,2048]{1,0:T(8,128)(2,1)} %convolution_convert_fusion.1) | data formatting | bytes 8388608 | tf_op jit(solution)/shard_map/reshape | solution.py:863
  273.0 5.8 %copy.49 = bf16[16,2,64,1024]{3,2,1,0:T(8,128)(2,1)} copy(bf16[16,2,64,1024]{3,1,2,0:T(2,128)(2,1)} %bitcast.200) | data formatting | bytes 8388608 | tf_op jit(solution)/shard_map/transpose | solution.py:863
  278.7 6.6 %convolution_convert_fusion = bf16[2048,1024]{1,0:T(8,128)(2,1)} fusion(bf16[256,1024]{1,0:T(8,128)(2,1)} %collective-permute-done.41, bf16[256,1024]{1,0:T(8,128)(2,1)} %bitcast.55, f32[512,2048]{1,0:T(8,128)S(1)} %copy-done.70, f32[2048]{0:T(1024)S(1)} %bitcast.264), kind=kOutput, calls=%fused_computation.13 | convolution fusion | flops 2162163712 | bytes 9445376 | tf_op jit(solution)/shard_map/dot_general | solution.py:39
  285.3 8.2 %pad_maximum_fusion = bf16[16,256,1024]{2,1,0:T(8,128)(2,1)} fusion(bf16[16,128,1024]{2,1,0:T(8,128)(2,1)} %bitcast.215, bf16[16,128,1024]{2,1,0:T(8,128)(2,1)} %bitcast.202), kind=kLoop, calls=%fused_computation.1 | loop fusion | flops 16777216 | bytes 16777216 | tf_op jit(solution)/shard_map/concatenate | solution.py:864
  295.8 5.7 %fusion.88 = (bf16[512,1024]{1,0:T(8,128)(2,1)S(1)}, f32[512,1024]{1,0:T(8,128)S(1)}) fusion(bf16[512,2048]{1,0:T(8,128)(2,1)} %copy-done.72, bf16[1024,2048]{1,0:T(8,128)(2,1)} %bitcast.211), kind=kOutput, calls=%fused_computation.258 | convolution fusion | flops 2148007936 | bytes 9437184 | tf_op jit(solution)/shard_map/dot_general | solution.py:45
  309.2 4.1 fusion.76
  323.2 7.4 %collective-permute-done.43.refs_1_ = bf16[512,128]{1,0:T(8,128)(2,1)S(1)} collective-permute-done((bf16[512,128]{1,0:T(8,128)(2,1)S(1)}, bf16[512,128]{1,0:T(8,128)(2,1)S(1)}, u32[]{:S(2)}, u32[]{:S(2)}) %collective-permute-start.43) | collective-permute-done | bytes 131104 | tf_op jit(solution)/shard_map/ppermute | solution.py:374
  330.6 7.5 %collective-permute-done.44.refs_2_ = bf16[512,128]{1,0:T(8,128)(2,1)S(1)} collective-permute-done((bf16[512,128]{1,0:T(8,128)(2,1)S(1)}, bf16[512,128]{1,0:T(8,128)(2,1)S(1)}, u32[]{:S(2)}, u32[]{:S(2)}) %collective-permute-start.44) | collective-permute-done | bytes 131104 | tf_op jit(solution)/shard_map/ppermute | solution.py:374
  338.8 20.5 %head_backward.1 = (bf16[512,384]{1,0:T(8,128)(2,1)}, bf16[512,384]{1,0:T(8,128)(2,1)}, bf16[512,384]{1,0:T(8,128)(2,1)}, bf16[512,384]{1,0:T(8,128)(2,1)}) custom-call(s32[16]{0:T(128)} %gather_fusion, bf16[2048,384]{1,0:T(8,128)(2,1)} %get-tuple-element.42.joint_ref, f32[2048,128]{1,0:T(8,128)} %get-tuple-element.43.mixed_ref, ...), custom_call_target="tpu_custom_call" | custom-call | tf_op jit(solution)/shard_map/head_backward/pallas_call | solution.py:675
  359.3 11.7 %collective-permute-start.46 = (bf16[512,384]{1,0:T(8,128)(2,1)}, bf16[512,384]{1,0:T(8,128)(2,1)}, u32[]{:S(2)}, u32[]{:S(2)}) collective-permute-start(bf16[512,384]{1,0:T(8,128)(2,1)} %get-tuple-element.46), channel_id=1, source_target_pairs={{0,2},{1,3},{2,0},{3,1},{4,6},{5,7},{6,4},{7,5},{8,10},{9,11},{10,... | collective-permute-start | bytes 1179656 | tf_op jit(solution)/shard_map/ppermute | solution.py:374
  379.8 25.9 %collective-permute-done.46 = bf16[512,384]{1,0:T(8,128)(2,1)} collective-permute-done((bf16[512,384]{1,0:T(8,128)(2,1)}, bf16[512,384]{1,0:T(8,128)(2,1)}, u32[]{:S(2)}, u32[]{:S(2)}) %collective-permute-start.46) | collective-permute-done | bytes 393248 | tf_op jit(solution)/shard_map/ppermute | solution.py:374
  406.7 7.9 %collective-permute-done.47 = bf16[512,384]{1,0:T(8,128)(2,1)} collective-permute-done((bf16[512,384]{1,0:T(8,128)(2,1)}, bf16[512,384]{1,0:T(8,128)(2,1)}, u32[]{:S(2)}, u32[]{:S(2)}) %collective-permute-start.47) | collective-permute-done | bytes 393248 | tf_op jit(solution)/shard_map/ppermute | solution.py:374
  415.7 8.5 %collective-permute-done.48 = bf16[512,384]{1,0:T(8,128)(2,1)} collective-permute-done((bf16[512,384]{1,0:T(8,128)(2,1)}, bf16[512,384]{1,0:T(8,128)(2,1)}, u32[]{:S(2)}, u32[]{:S(2)}) %collective-permute-start.48) | collective-permute-done | bytes 393248 | tf_op jit(solution)/shard_map/ppermute | solution.py:374
  432.3 3.1 spread.3
  441.1 27.8 %collective-permute-start.51 = (f32[32,384]{1,0:T(8,128)S(1)}, f32[32,384]{1,0:T(8,128)S(1)}, u32[]{:S(2)}, u32[]{:S(2)}) collective-permute-start(f32[32,384]{1,0:T(8,128)S(1)} %add.354), channel_id=1, source_target_pairs={{0,2},{1,3},{2,0},{3,1},{4,6},{5,7},{6,4},{7,5},{8,10},{9,11},{10,... | collective-permute-start | bytes 147464 | tf_op jit(solution)/shard_map/ppermute | solution.py:374
  468.9 3.8 convolution_convert_fusion.2
  472.7 4.9 spread.2
  481.3 7.1 %collective-permute-done.52 = f32[32,384]{1,0:T(8,128)S(1)} collective-permute-done((f32[32,384]{1,0:T(8,128)S(1)}, f32[32,384]{1,0:T(8,128)S(1)}, u32[]{:S(2)}, u32[]{:S(2)}) %collective-permute-start.52) | collective-permute-done | bytes 49184 | tf_op jit(solution)/shard_map/ppermute | solution.py:374
  488.9 30.2 %collective-permute-done.53 = f32[32,384]{1,0:T(8,128)S(1)} collective-permute-done((f32[32,384]{1,0:T(8,128)S(1)}, f32[32,384]{1,0:T(8,128)S(1)}, u32[]{:S(2)}, u32[]{:S(2)}) %collective-permute-start.53) | collective-permute-done | bytes 49184 | tf_op jit(solution)/shard_map/ppermute | solution.py:374
  526.2 3.1 collective-permute-start.68
  540.5 3.9 collective-permute-done.61
  544.4 7.8 %collective-permute-done.60 = bf16[64,1536]{1,0:T(8,128)(2,1)S(1)} collective-permute-done((bf16[64,1536]{1,0:T(8,128)(2,1)S(1)}, bf16[64,1536]{1,0:T(8,128)(2,1)S(1)}, u32[]{:S(2)}, u32[]{:S(2)}) %collective-permute-start.60) | collective-permute-done | bytes 196640 | tf_op jit(solution)/shard_map/ppermute | solution.py:374
  (419 shorter events, 143.2 us)
Async XLA Ops:
  7.2 214.1 %all-gather.3.cloned.1.call-start = ((), (), s32[]{:S(2)}) async-start(), calls=%async_computation.2 | async-start | bytes 8912896 | tf_op jit(solution)/shard_map/all_gather | solution.py:772
  11.4 543.7 %reduce-scatter.2.cloned.1.call-start = ((), (), s32[]{:S(2)}) async-start(), calls=%async_computation.1 | async-start | bytes 8912896 | tf_op jit(solution)/shard_map/reduce_scatter | solution.py:865
  12.4 11.3 %collective-permute-start.10 = (bf16[32,512]{1,0:T(8,128)(2,1)S(1)}, bf16[32,512]{1,0:T(8,128)(2,1)S(1)}, u32[]{:S(2)}, u32[]{:S(2)}) collective-permute-start(bf16[32,512]{1,0:T(8,128)(2,1)S(1)} %get-tuple-element.119), channel_id=1, source_target_pairs={{0,1},{1,0},{2,3},{3,2},{4,5},{5,4},{6,7},{7,6},{8,9},{9,8},{10,11... | collective-permute-start | bytes 98312 | tf_op jit(solution)/shard_map/ppermute | solution.py:374
  12.6 61.8 %collective-permute-start = (bf16[256,1024]{1,0:T(8,128)(2,1)S(1)}, bf16[256,1024]{1,0:T(8,128)(2,1)S(1)}, u32[]{:S(2)}, u32[]{:S(2)}) collective-permute-start(bf16[256,1024]{1,0:T(8,128)(2,1)S(1)} %bitcast.204), channel_id=1, source_target_pairs={{0,1},{1,0},{2,3},{3,2},{4,5},{5,4},{6,7},{7,6},{8,9},{9,8},{10,11... | collective-permute-start | bytes 1572872 | tf_op jit(solution)/shard_map/ppermute | solution.py:374
  13.4 10.3 %collective-permute-start.2 = (bf16[64,1536]{1,0:T(8,128)(2,1)S(1)}, bf16[64,1536]{1,0:T(8,128)(2,1)S(1)}, u32[]{:S(2)}, u32[]{:S(2)}) collective-permute-start(bf16[64,1536]{1,0:T(8,128)(2,1)S(1)} %maximum_select_fusion.4), channel_id=1, source_target_pairs={{0,6},{1,7},{2,4},{3,5},{4,2},{5,3},{6,0},{7,1},{8,14},{9,15},{10,... | collective-permute-start | bytes 589832 | tf_op jit(solution)/shard_map/ppermute | solution.py:374
  23.7 30.1 %collective-permute-start.11 = (bf16[64,1536]{1,0:T(8,128)(2,1)S(1)}, bf16[64,1536]{1,0:T(8,128)(2,1)S(1)}, u32[]{:S(2)}, u32[]{:S(2)}) collective-permute-start(bf16[64,1536]{1,0:T(8,128)(2,1)S(1)} %maximum_select_fusion.4), channel_id=1, source_target_pairs={{0,2},{1,3},{2,0},{3,1},{4,6},{5,7},{6,4},{7,5},{8,10},{9,11},{10,... | collective-permute-start | bytes 589832 | tf_op jit(solution)/shard_map/ppermute | solution.py:374
  31.0 13.3 %collective-permute-start.6 = (bf16[2,9,128]{2,1,0:T(8,128)(2,1)S(1)}, bf16[2,9,128]{2,1,0:T(8,128)(2,1)S(1)}, u32[]{:S(2)}, u32[]{:S(2)}) collective-permute-start(bf16[2,9,128]{2,1,0:T(8,128)(2,1)S(1)} %maximum_select_fusion.11), channel_id=1, source_target_pairs={{0,6},{1,7},{2,4},{3,5},{4,2},{5,3},{6,0},{7,1},{8,14},{9,15},{10,... | collective-permute-start | bytes 13832 | tf_op jit(solution)/shard_map/ppermute | solution.py:374
  49.2 21.7 %collective-permute-start.12 = (bf16[64,1536]{1,0:T(8,128)(2,1)S(1)}, bf16[64,1536]{1,0:T(8,128)(2,1)S(1)}, u32[]{:S(2)}, u32[]{:S(2)}) collective-permute-start(bf16[64,1536]{1,0:T(8,128)(2,1)S(1)} %maximum_select_fusion.4), channel_id=1, source_target_pairs={{0,4},{1,5},{2,6},{3,7},{4,0},{5,1},{6,2},{7,3},{8,12},{9,13},{10,... | collective-permute-start | bytes 589832 | tf_op jit(solution)/shard_map/ppermute | solution.py:374
  51.3 21.1 %collective-permute-start.13 = (bf16[64,1536]{1,0:T(8,128)(2,1)S(1)}, bf16[64,1536]{1,0:T(8,128)(2,1)S(1)}, u32[]{:S(2)}, u32[]{:S(2)}) collective-permute-start(bf16[64,1536]{1,0:T(8,128)(2,1)S(1)} %maximum_select_fusion.4), channel_id=1, source_target_pairs={{0,8},{1,9},{2,10},{3,11},{4,12},{5,13},{6,14},{7,15},{8,0},{9,1},... | collective-permute-start | bytes 589832 | tf_op jit(solution)/shard_map/ppermute | solution.py:374
  51.6 22.5 %collective-permute-start.17 = (bf16[64,1536]{1,0:T(8,128)(2,1)S(1)}, bf16[64,1536]{1,0:T(8,128)(2,1)S(1)}, u32[]{:S(2)}, u32[]{:S(2)}) collective-permute-start(bf16[64,1536]{1,0:T(8,128)(2,1)S(1)} %maximum_select_fusion.4), channel_id=1, source_target_pairs={{0,16},{1,17},{2,18},{3,19},{4,20},{5,21},{6,22},{7,23},{8,24},{9,... | collective-permute-start | bytes 589832 | tf_op jit(solution)/shard_map/ppermute | solution.py:374
  53.9 30.7 %collective-permute-start.16 = (bf16[64,1536]{1,0:T(8,128)(2,1)S(1)}, bf16[64,1536]{1,0:T(8,128)(2,1)S(1)}, u32[]{:S(2)}, u32[]{:S(2)}) collective-permute-start(bf16[64,1536]{1,0:T(8,128)(2,1)S(1)} %collective-permute-done.2), channel_id=1, source_target_pairs={{0,8},{1,9},{2,10},{3,11},{4,12},{5,13},{6,14},{7,15},{8,0},{9,1},... | collective-permute-start | bytes 589832 | tf_op jit(solution)/shard_map/ppermute | solution.py:374
  70.8 13.2 %collective-permute-start.15 = (bf16[64,1536]{1,0:T(8,128)(2,1)S(1)}, bf16[64,1536]{1,0:T(8,128)(2,1)S(1)}, u32[]{:S(2)}, u32[]{:S(2)}) collective-permute-start(bf16[64,1536]{1,0:T(8,128)(2,1)S(1)} %collective-permute-done.12), channel_id=1, source_target_pairs={{0,8},{1,9},{2,10},{3,11},{4,12},{5,13},{6,14},{7,15},{8,0},{9,1},... | collective-permute-start | bytes 589832 | tf_op jit(solution)/shard_map/ppermute | solution.py:374
  72.4 13.7 %collective-permute-start.19 = (bf16[64,1536]{1,0:T(8,128)(2,1)S(1)}, bf16[64,1536]{1,0:T(8,128)(2,1)S(1)}, u32[]{:S(2)}, u32[]{:S(2)}) collective-permute-start(bf16[64,1536]{1,0:T(8,128)(2,1)S(1)} %collective-permute-done.12), channel_id=1, source_target_pairs={{0,16},{1,17},{2,18},{3,19},{4,20},{5,21},{6,22},{7,23},{8,24},{9,... | collective-permute-start | bytes 589832 | tf_op jit(solution)/shard_map/ppermute | solution.py:374
  74.0 12.7 %collective-permute-start.20 = (bf16[64,1536]{1,0:T(8,128)(2,1)S(1)}, bf16[64,1536]{1,0:T(8,128)(2,1)S(1)}, u32[]{:S(2)}, u32[]{:S(2)}) collective-permute-start(bf16[64,1536]{1,0:T(8,128)(2,1)S(1)} %collective-permute-done.2), channel_id=1, source_target_pairs={{0,16},{1,17},{2,18},{3,19},{4,20},{5,21},{6,22},{7,23},{8,24},{9,... | collective-permute-start | bytes 589832 | tf_op jit(solution)/shard_map/ppermute | solution.py:374
  84.0 10.9 %collective-permute-start.21 = (bf16[64,1536]{1,0:T(8,128)(2,1)S(1)}, bf16[64,1536]{1,0:T(8,128)(2,1)S(1)}, u32[]{:S(2)}, u32[]{:S(2)}) collective-permute-start(bf16[64,1536]{1,0:T(8,128)(2,1)S(1)} %collective-permute-done.13), channel_id=1, source_target_pairs={{0,16},{1,17},{2,18},{3,19},{4,20},{5,21},{6,22},{7,23},{8,24},{9,... | collective-permute-start | bytes 589832 | tf_op jit(solution)/shard_map/ppermute | solution.py:374
  84.6 17.4 %collective-permute-start.22 = (bf16[64,1536]{1,0:T(8,128)(2,1)}, bf16[64,1536]{1,0:T(8,128)(2,1)S(1)}, u32[]{:S(2)}, u32[]{:S(2)}) collective-permute-start(bf16[64,1536]{1,0:T(8,128)(2,1)} %collective-permute-done.14), channel_id=1, source_target_pairs={{0,16},{1,17},{2,18},{3,19},{4,20},{5,21},{6,22},{7,23},{8,24},{9,... | collective-permute-start | bytes 589832 | tf_op jit(solution)/shard_map/ppermute | solution.py:374
  86.1 15.9 %collective-permute-start.23 = (bf16[64,1536]{1,0:T(8,128)(2,1)S(1)}, bf16[64,1536]{1,0:T(8,128)(2,1)S(1)}, u32[]{:S(2)}, u32[]{:S(2)}) collective-permute-start(bf16[64,1536]{1,0:T(8,128)(2,1)S(1)} %collective-permute-done.19), channel_id=1, source_target_pairs={{0,8},{1,9},{2,10},{3,11},{4,12},{5,13},{6,14},{7,15},{8,0},{9,1},... | collective-permute-start | bytes 589832 | tf_op jit(solution)/shard_map/ppermute | solution.py:374
  86.8 15.2 %collective-permute-start.24 = (bf16[64,1536]{1,0:T(8,128)(2,1)S(1)}, bf16[64,1536]{1,0:T(8,128)(2,1)S(1)}, u32[]{:S(2)}, u32[]{:S(2)}) collective-permute-start(bf16[64,1536]{1,0:T(8,128)(2,1)S(1)} %collective-permute-done.20), channel_id=1, source_target_pairs={{0,8},{1,9},{2,10},{3,11},{4,12},{5,13},{6,14},{7,15},{8,0},{9,1},... | collective-permute-start | bytes 589832 | tf_op jit(solution)/shard_map/ppermute | solution.py:374
  110.0 11.9 %collective-permute-start.32 = (bf16[64,512]{1,0:T(8,128)(2,1)S(1)}, bf16[64,512]{1,0:T(8,128)(2,1)S(1)}, u32[]{:S(2)}, u32[]{:S(2)}) collective-permute-start(bf16[64,512]{1,0:T(8,128)(2,1)S(1)} %maximum_select_fusion.9), channel_id=1, source_target_pairs={{0,4},{1,5},{2,6},{3,7},{4,0},{5,1},{6,2},{7,3},{8,12},{9,13},{10,... | collective-permute-start | bytes 196616 | tf_op jit(solution)/shard_map/ppermute | solution.py:374
  110.1 11.8 %collective-permute-start.31 = (bf16[64,512]{1,0:T(8,128)(2,1)S(1)}, bf16[64,512]{1,0:T(8,128)(2,1)S(1)}, u32[]{:S(2)}, u32[]{:S(2)}) collective-permute-start(bf16[64,512]{1,0:T(8,128)(2,1)S(1)} %maximum_select_fusion.9), channel_id=1, source_target_pairs={{0,2},{1,3},{2,0},{3,1},{4,6},{5,7},{6,4},{7,5},{8,10},{9,11},{10,... | collective-permute-start | bytes 196616 | tf_op jit(solution)/shard_map/ppermute | solution.py:374
  125.9 12.1 %collective-permute-start.35 = (bf16[4,64,512]{2,1,0:T(8,128)(2,1)S(1)}, bf16[4,64,512]{2,1,0:T(8,128)(2,1)S(1)}, u32[]{:S(2)}, u32[]{:S(2)}) collective-permute-start(bf16[4,64,512]{2,1,0:T(8,128)(2,1)S(1)} %pad_maximum_fusion.7.refs_1_), channel_id=1, source_target_pairs={{0,16},{1,17},{2,18},{3,19},{4,20},{5,21},{6,22},{7,23},{8,24},{9,... | collective-permute-start | bytes 786440 | tf_op jit(solution)/shard_map/ppermute | solution.py:374
  133.1 32.1 %collective-permute-start.25 = (bf16[512,384]{1,0:T(8,128)(2,1)}, bf16[512,384]{1,0:T(8,128)(2,1)}, u32[]{:S(2)}, u32[]{:S(2)}) collective-permute-start(bf16[512,384]{1,0:T(8,128)(2,1)} %get-tuple-element.82), channel_id=1, source_target_pairs={{0,2},{1,3},{2,0},{3,1},{4,6},{5,7},{6,4},{7,5},{8,10},{9,11},{10,... | collective-permute-start | bytes 1179656 | tf_op jit(solution)/shard_map/ppermute | solution.py:374
  134.4 40.9 %collective-permute-start.26 = (bf16[512,384]{1,0:T(8,128)(2,1)S(1)}, bf16[512,384]{1,0:T(8,128)(2,1)}, u32[]{:S(2)}, u32[]{:S(2)}) collective-permute-start(bf16[512,384]{1,0:T(8,128)(2,1)S(1)} %get-tuple-element.81), channel_id=1, source_target_pairs={{0,4},{1,5},{2,6},{3,7},{4,0},{5,1},{6,2},{7,3},{8,12},{9,13},{10,... | collective-permute-start | bytes 1179656 | tf_op jit(solution)/shard_map/ppermute | solution.py:374
  136.4 38.9 %collective-permute-start.27 = (bf16[512,384]{1,0:T(8,128)(2,1)S(1)}, bf16[512,384]{1,0:T(8,128)(2,1)}, u32[]{:S(2)}, u32[]{:S(2)}) collective-permute-start(bf16[512,384]{1,0:T(8,128)(2,1)S(1)} %get-tuple-element.80), channel_id=1, source_target_pairs={{0,6},{1,7},{2,4},{3,5},{4,2},{5,3},{6,0},{7,1},{8,14},{9,15},{10,... | collective-permute-start | bytes 1179656 | tf_op jit(solution)/shard_map/ppermute | solution.py:374
  143.7 63.6 %collective-permute-start.37 = (bf16[512,512]{1,0:T(8,128)(2,1)S(1)}, bf16[512,512]{1,0:T(8,128)(2,1)}, u32[]{:S(2)}, u32[]{:S(2)}) collective-permute-start(bf16[512,512]{1,0:T(8,128)(2,1)S(1)} %bitcast.230), channel_id=1, source_target_pairs={{0,1},{1,0},{2,3},{3,2},{4,5},{5,4},{6,7},{7,6},{8,9},{9,8},{10,11... | collective-permute-start | bytes 1572872 | tf_op jit(solution)/shard_map/ppermute | solution.py:374
  187.1 12.4 %collective-permute-start.28 = (bf16[512,128]{1,0:T(8,128)(2,1)}, bf16[512,128]{1,0:T(8,128)(2,1)S(1)}, u32[]{:S(2)}, u32[]{:S(2)}) collective-permute-start(bf16[512,128]{1,0:T(8,128)(2,1)} %get-tuple-element.38), channel_id=1, source_target_pairs={{0,2},{1,3},{2,0},{3,1},{4,6},{5,7},{6,4},{7,5},{8,10},{9,11},{10,... | collective-permute-start | bytes 393224 | tf_op jit(solution)/shard_map/ppermute | solution.py:374
  195.2 12.0 %collective-permute-start.29 = (bf16[512,128]{1,0:T(8,128)(2,1)}, bf16[512,128]{1,0:T(8,128)(2,1)S(1)}, u32[]{:S(2)}, u32[]{:S(2)}) collective-permute-start(bf16[512,128]{1,0:T(8,128)(2,1)} %get-tuple-element.39), channel_id=1, source_target_pairs={{0,4},{1,5},{2,6},{3,7},{4,0},{5,1},{6,2},{7,3},{8,12},{9,13},{10,... | collective-permute-start | bytes 393224 | tf_op jit(solution)/shard_map/ppermute | solution.py:374
  196.1 11.1 %collective-permute-start.30 = (bf16[512,128]{1,0:T(8,128)(2,1)}, bf16[512,128]{1,0:T(8,128)(2,1)S(1)}, u32[]{:S(2)}, u32[]{:S(2)}) collective-permute-start(bf16[512,128]{1,0:T(8,128)(2,1)} %get-tuple-element.40), channel_id=1, source_target_pairs={{0,6},{1,7},{2,4},{3,5},{4,2},{5,3},{6,0},{7,1},{8,14},{9,15},{10,... | collective-permute-start | bytes 393224 | tf_op jit(solution)/shard_map/ppermute | solution.py:374
  211.0 31.3 %collective-permute-start.41 = (bf16[256,1024]{1,0:T(8,128)(2,1)}, bf16[256,1024]{1,0:T(8,128)(2,1)}, u32[]{:S(2)}, u32[]{:S(2)}) collective-permute-start(bf16[256,1024]{1,0:T(8,128)(2,1)} %bitcast.55), channel_id=1, source_target_pairs={{0,1},{1,0},{2,3},{3,2},{4,5},{5,4},{6,7},{7,6},{8,9},{9,8},{10,11... | collective-permute-start | bytes 1572872 | tf_op jit(solution)/shard_map/ppermute | solution.py:374
  307.5 131.1 %collective-permute-start.40 = (bf16[256,1024]{1,0:T(8,128)(2,1)}, bf16[256,1024]{1,0:T(8,128)(2,1)}, u32[]{:S(2)}, u32[]{:S(2)}) collective-permute-start(bf16[256,1024]{1,0:T(8,128)(2,1)} %slice.683), channel_id=1, source_target_pairs={{0,1},{1,0},{2,3},{3,2},{4,5},{5,4},{6,7},{7,6},{8,9},{9,8},{10,11... | collective-permute-start | bytes 1572872 | tf_op jit(solution)/shard_map/ppermute | solution.py:374
  316.6 14.0 %collective-permute-start.43 = (bf16[512,128]{1,0:T(8,128)(2,1)S(1)}, bf16[512,128]{1,0:T(8,128)(2,1)S(1)}, u32[]{:S(2)}, u32[]{:S(2)}) collective-permute-start(bf16[512,128]{1,0:T(8,128)(2,1)S(1)} %get-tuple-element.97), channel_id=1, source_target_pairs={{0,2},{1,3},{2,0},{3,1},{4,6},{5,7},{6,4},{7,5},{8,10},{9,11},{10,... | collective-permute-start | bytes 393224 | tf_op jit(solution)/shard_map/ppermute | solution.py:374
  319.0 19.1 %collective-permute-start.44 = (bf16[512,128]{1,0:T(8,128)(2,1)S(1)}, bf16[512,128]{1,0:T(8,128)(2,1)S(1)}, u32[]{:S(2)}, u32[]{:S(2)}) collective-permute-start(bf16[512,128]{1,0:T(8,128)(2,1)S(1)} %get-tuple-element.96), channel_id=1, source_target_pairs={{0,4},{1,5},{2,6},{3,7},{4,0},{5,1},{6,2},{7,3},{8,12},{9,13},{10,... | collective-permute-start | bytes 393224 | tf_op jit(solution)/shard_map/ppermute | solution.py:374
  319.0 19.2 %collective-permute-start.45 = (bf16[512,128]{1,0:T(8,128)(2,1)S(1)}, bf16[512,128]{1,0:T(8,128)(2,1)S(1)}, u32[]{:S(2)}, u32[]{:S(2)}) collective-permute-start(bf16[512,128]{1,0:T(8,128)(2,1)S(1)} %get-tuple-element.95), channel_id=1, source_target_pairs={{0,6},{1,7},{2,4},{3,5},{4,2},{5,3},{6,0},{7,1},{8,14},{9,15},{10,... | collective-permute-start | bytes 393224 | tf_op jit(solution)/shard_map/ppermute | solution.py:374
  359.3 46.4 %collective-permute-start.46 = (bf16[512,384]{1,0:T(8,128)(2,1)}, bf16[512,384]{1,0:T(8,128)(2,1)}, u32[]{:S(2)}, u32[]{:S(2)}) collective-permute-start(bf16[512,384]{1,0:T(8,128)(2,1)} %get-tuple-element.46), channel_id=1, source_target_pairs={{0,2},{1,3},{2,0},{3,1},{4,6},{5,7},{6,4},{7,5},{8,10},{9,11},{10,... | collective-permute-start | bytes 1179656 | tf_op jit(solution)/shard_map/ppermute | solution.py:374
  371.0 43.6 %collective-permute-start.47 = (bf16[512,384]{1,0:T(8,128)(2,1)}, bf16[512,384]{1,0:T(8,128)(2,1)}, u32[]{:S(2)}, u32[]{:S(2)}) collective-permute-start(bf16[512,384]{1,0:T(8,128)(2,1)} %get-tuple-element.47), channel_id=1, source_target_pairs={{0,4},{1,5},{2,6},{3,7},{4,0},{5,1},{6,2},{7,3},{8,12},{9,13},{10,... | collective-permute-start | bytes 1179656 | tf_op jit(solution)/shard_map/ppermute | solution.py:374
  373.3 50.9 %collective-permute-start.48 = (bf16[512,384]{1,0:T(8,128)(2,1)}, bf16[512,384]{1,0:T(8,128)(2,1)}, u32[]{:S(2)}, u32[]{:S(2)}) collective-permute-start(bf16[512,384]{1,0:T(8,128)(2,1)} %get-tuple-element.48), channel_id=1, source_target_pairs={{0,6},{1,7},{2,4},{3,5},{4,2},{5,3},{6,0},{7,1},{8,14},{9,15},{10,... | collective-permute-start | bytes 1179656 | tf_op jit(solution)/shard_map/ppermute | solution.py:374
  379.8 50.2 %collective-permute-start.63 = (bf16[512,512]{1,0:T(8,128)(2,1)}, bf16[512,512]{1,0:T(8,128)(2,1)}, u32[]{:S(2)}, u32[]{:S(2)}) collective-permute-start(bf16[512,512]{1,0:T(8,128)(2,1)} %get-tuple-element.85), channel_id=1, source_target_pairs={{0,1},{1,0},{2,3},{3,2},{4,5},{5,4},{6,7},{7,6},{8,9},{9,8},{10,11... | collective-permute-start | bytes 1572872 | tf_op jit(solution)/shard_map/ppermute | solution.py:374
  435.5 43.6 %collective-permute-start.64 = (bf16[8,64,512]{2,1,0:T(8,128)(2,1)}, bf16[8,64,512]{2,1,0:T(8,128)(2,1)}, u32[]{:S(2)}, u32[]{:S(2)}) collective-permute-start(bf16[8,64,512]{2,1,0:T(8,128)(2,1)} %get-tuple-element.54), channel_id=1, source_target_pairs={{0,16},{1,17},{2,18},{3,19},{4,20},{5,21},{6,22},{7,23},{8,24},{9,... | collective-permute-start | bytes 1572872 | tf_op jit(solution)/shard_map/ppermute | solution.py:374
  441.1 37.9 %collective-permute-start.51 = (f32[32,384]{1,0:T(8,128)S(1)}, f32[32,384]{1,0:T(8,128)S(1)}, u32[]{:S(2)}, u32[]{:S(2)}) collective-permute-start(f32[32,384]{1,0:T(8,128)S(1)} %add.354), channel_id=1, source_target_pairs={{0,2},{1,3},{2,0},{3,1},{4,6},{5,7},{6,4},{7,5},{8,10},{9,11},{10,... | collective-permute-start | bytes 147464 | tf_op jit(solution)/shard_map/ppermute | solution.py:374
  477.6 53.0 %collective-permute-start.55 = (bf16[4,64,1536]{2,1,0:T(8,128)(2,1)}, bf16[4,64,1536]{2,1,0:T(8,128)(2,1)S(1)}, u32[]{:S(2)}, u32[]{:S(2)}) collective-permute-start(bf16[4,64,1536]{2,1,0:T(8,128)(2,1)} %get-tuple-element.50), channel_id=1, source_target_pairs={{0,16},{1,17},{2,18},{3,19},{4,20},{5,21},{6,22},{7,23},{8,24},{9,... | collective-permute-start | bytes 2359304 | tf_op jit(solution)/shard_map/ppermute | solution.py:374
  478.1 45.8 %collective-permute-start.58 = (bf16[4,64,1536]{2,1,0:T(8,128)(2,1)}, bf16[4,64,1536]{2,1,0:T(8,128)(2,1)S(1)}, u32[]{:S(2)}, u32[]{:S(2)}) collective-permute-start(bf16[4,64,1536]{2,1,0:T(8,128)(2,1)} %get-tuple-element.52), channel_id=1, source_target_pairs={{0,8},{1,9},{2,10},{3,11},{4,12},{5,13},{6,14},{7,15},{8,0},{9,1},... | collective-permute-start | bytes 2359304 | tf_op jit(solution)/shard_map/ppermute | solution.py:374
  480.2 44.9 %collective-permute-start.65 = (bf16[4,64,512]{2,1,0:T(8,128)(2,1)S(1)}, bf16[4,64,512]{2,1,0:T(8,128)(2,1)S(1)}, u32[]{:S(2)}, u32[]{:S(2)}) collective-permute-start(bf16[4,64,512]{2,1,0:T(8,128)(2,1)S(1)} %add_convert_fusion.5), channel_id=1, source_target_pairs={{0,8},{1,9},{2,10},{3,11},{4,12},{5,13},{6,14},{7,15},{8,0},{9,1},... | collective-permute-start | bytes 786440 | tf_op jit(solution)/shard_map/ppermute | solution.py:374
  488.5 30.6 %collective-permute-start.53 = (f32[32,384]{1,0:T(8,128)S(1)}, f32[32,384]{1,0:T(8,128)S(1)}, u32[]{:S(2)}, u32[]{:S(2)}) collective-permute-start(f32[32,384]{1,0:T(8,128)S(1)} %add.356), channel_id=1, source_target_pairs={{0,8},{1,9},{2,10},{3,11},{4,12},{5,13},{6,14},{7,15},{8,0},{9,1},... | collective-permute-start | bytes 147464 | tf_op jit(solution)/shard_map/ppermute | solution.py:374
  524.0 10.4 %collective-permute-start.59 = (bf16[2,64,1536]{2,1,0:T(8,128)(2,1)S(1)}, bf16[2,64,1536]{2,1,0:T(8,128)(2,1)S(1)}, u32[]{:S(2)}, u32[]{:S(2)}) collective-permute-start(bf16[2,64,1536]{2,1,0:T(8,128)(2,1)S(1)} %add_convert_fusion.3), channel_id=1, source_target_pairs={{0,16},{1,17},{2,18},{3,19},{4,20},{5,21},{6,22},{7,23},{8,24},{9,... | collective-permute-start | bytes 1179656 | tf_op jit(solution)/shard_map/ppermute | solution.py:374
  534.7 9.7 %collective-permute-start.61 = (bf16[64,1536]{1,0:T(8,128)(2,1)S(1)}, bf16[64,1536]{1,0:T(8,128)(2,1)S(1)}, u32[]{:S(2)}, u32[]{:S(2)}) collective-permute-start(bf16[64,1536]{1,0:T(8,128)(2,1)S(1)} %get-tuple-element.104), channel_id=1, source_target_pairs={{0,6},{1,7},{2,4},{3,5},{4,2},{5,3},{6,0},{7,1},{8,14},{9,15},{10,... | collective-permute-start | bytes 589832 | tf_op jit(solution)/shard_map/ppermute | solution.py:374
  537.6 14.7 %collective-permute-start.60 = (bf16[64,1536]{1,0:T(8,128)(2,1)S(1)}, bf16[64,1536]{1,0:T(8,128)(2,1)S(1)}, u32[]{:S(2)}, u32[]{:S(2)}) collective-permute-start(bf16[64,1536]{1,0:T(8,128)(2,1)S(1)} %get-tuple-element.103), channel_id=1, source_target_pairs={{0,4},{1,5},{2,6},{3,7},{4,0},{5,1},{6,2},{7,3},{8,12},{9,13},{10,... | collective-permute-start | bytes 589832 | tf_op jit(solution)/shard_map/ppermute | solution.py:374
  539.7 12.5 %collective-permute-start.57 = (bf16[64,1536]{1,0:T(8,128)(2,1)S(1)}, bf16[64,1536]{1,0:T(8,128)(2,1)S(1)}, u32[]{:S(2)}, u32[]{:S(2)}) collective-permute-start(bf16[64,1536]{1,0:T(8,128)(2,1)S(1)} %fusion.24), channel_id=1, source_target_pairs={{0,2},{1,3},{2,0},{3,1},{4,6},{5,7},{6,4},{7,5},{8,10},{9,11},{10,... | collective-permute-start | bytes 589832 | tf_op jit(solution)/shard_map/ppermute | solution.py:374
  540.4 12.5 %collective-permute-start.69 = (f32[32,512]{1,0:T(8,128)S(1)}, f32[32,512]{1,0:T(8,128)S(1)}, u32[]{:S(2)}, u32[]{:S(2)}) collective-permute-start(f32[32,512]{1,0:T(8,128)S(1)} %get-tuple-element.117), channel_id=1, source_target_pairs={{0,1},{1,0},{2,3},{3,2},{4,5},{5,4},{6,7},{7,6},{8,9},{9,8},{10,11... | collective-permute-start | bytes 196616 | tf_op jit(solution)/shard_map/ppermute | solution.py:374
  (99 other events, 1387.1 us)
Sparse Core Ops, SparseCore 0:
  11.6 152.5 all-gather.2
  293.6 221.3 reduce-scatter.1

commit v3 on v2

--- a/solution.py
+++ b/solution.py
@@ -374,71 +374,59 @@
     return lax.ppermute(value, ALL, [(source, source ^ mask) for source in range(count)])
 
 
-def placed_kernel(slot_ref, *refs, col_blocks):
-    pieces, out_ref, sem = refs[:-2], refs[-2], refs[-1]
-    width = out_ref.shape[2] // col_blocks
+def moved_kernel(table_ref, *refs, plan, source_count):
+    sources, targets, sem = refs[:source_count], refs[source_count:-1], refs[-1]
     copies = []
-    for piece in pieces:
-        for within in range(piece.shape[0]):
-            row = slot_ref[len(copies) // col_blocks]
-            for col in range(col_blocks):
-                if col_blocks == 1:
-                    source, target = piece.at[within], out_ref.at[row]
-                else:
-                    source = piece.at[within, :, pl.ds(col * width, width)]
-                    to = pl.multiple_of(slot_ref[16 + col] * width, 128)
-                    target = out_ref.at[row, :, pl.ds(to, width)]
-                copy = pltpu.make_async_copy(source, target, sem.at[len(copies)])
-                copy.start()
-                copies.append(copy)
+    for source, source_at, target, target_at in plan:
+        copy = pltpu.make_async_copy(
+            sources[source].at[source_at(table_ref)],
+            targets[target].at[target_at(table_ref)],
+            sem.at[len(copies)],
+        )
+        copy.start()
+        copies.append(copy)
     for copy in copies:
         copy.wait()
 
 
-def placed(pieces, slots, col_blocks=1):
-    rows, cols = pieces[0].shape[1:]
+def moved(table, sources, plan, shapes):
     return pl.pallas_call(
-        lambda *refs: placed_kernel(*refs, col_blocks=col_blocks),
-        out_shape=jax.ShapeDtypeStruct((16, rows, cols), pieces[0].dtype),
+        lambda *refs: moved_kernel(*refs, plan=plan, source_count=len(sources)),
+        out_shape=[jax.ShapeDtypeStruct(shape, jnp.bfloat16) for shape in shapes],
         in_specs=[pl.BlockSpec(memory_space=pltpu.SMEM)]
-        + [pl.BlockSpec(memory_space=pl.ANY)] * len(pieces),
-        out_specs=pl.BlockSpec(memory_space=pltpu.VMEM),
-        scratch_shapes=[pltpu.SemaphoreType.DMA((16 * col_blocks,))],
-        name="placed",
-    )(slots, *pieces)
-
-
-def spread_kernel(slot_ref, whole_ref, *refs, groups, col_blocks):
-    outs, sem = refs[:-1], refs[-1]
-    width = whole_ref.shape[2] // col_blocks
-    copies = []
-    for out_ref, members in zip(outs, groups):
-        for place, at in enumerate(members):
-            row = slot_ref[at]
-            for col in range(col_blocks):
-                if col_blocks == 1:
-                    source, target = whole_ref.at[row], out_ref.at[place]
-                else:
-                    to = pl.multiple_of(slot_ref[16 + col] * width, 128)
-                    source = whole_ref.at[row, :, pl.ds(to, width)]
-                    target = out_ref.at[place, :, pl.ds(col * width, width)]
-                copy = pltpu.make_async_copy(source, target, sem.at[len(copies)])
-                copy.start()
-                copies.append(copy)
-    for copy in copies:
-        copy.wait()
-
-
-def spread(whole, slots, groups, col_blocks=1):
-    rows, cols = whole.shape[1:]
-    return pl.pallas_call(
-        lambda *refs: spread_kernel(*refs, groups=groups, col_blocks=col_blocks),
-        out_shape=[jax.ShapeDtypeStruct((len(group), rows, cols), whole.dtype) for group in groups],
-        in_specs=[pl.BlockSpec(memory_space=pltpu.SMEM), pl.BlockSpec(memory_space=pl.ANY)],
-        out_specs=[pl.BlockSpec(memory_space=pltpu.VMEM)] * len(groups),
-        scratch_shapes=[pltpu.SemaphoreType.DMA((16 * col_blocks,))],
-        name="spread",
-    )(slots, whole)
+        + [pl.BlockSpec(memory_space=pl.ANY)] * len(sources),
+        out_specs=[pl.BlockSpec(memory_space=pltpu.VMEM)] * len(shapes),
+        scratch_shapes=[pltpu.SemaphoreType.DMA((len(plan),))],
+        name="moved",
+    )(table, *sources)
+
+
+def slot(at):
+    return lambda table: (table[at],)
+
+
+def slot_rows(at, start, count):
+    return lambda table: (table[at], pl.ds(start, count))
+
+
+def slot_part(at, start, count, left, width):
+    return lambda table: (table[at], pl.ds(start, count), pl.ds(left, width))
+
+
+def looked(entry, count, column_at, width):
+    return lambda table: (
+        entry,
+        pl.ds(0, count),
+        pl.ds(pl.multiple_of(table[column_at] * width, 128), width),
+    )
+
+
+def fixed(*index):
+    return lambda table: index
+
+
+def line_of(piece):
+    return [piece] + [swapped(piece, bits) for bits in Z_BITS[1:]]
 
 
 def collected(line):
@@ -449,26 +437,40 @@
         found[first >> 3, along] = swapped(line[along], first)
         found[second >> 3, along] = swapped(line[along], second)
         found[3, along] = swapped(found[first >> 3, along], second)
-    return [found[across, along][None] for across in range(4) for along in range(4)]
+    arrays = [found[across, along][None] for across in range(4) for along in range(4)]
+    return arrays, [(at, 0) for at in range(16)]
+
+
+def collected_pairs(line):
+    near, far = jnp.stack(line[:2]), jnp.stack(line[2:])
+    near_x, far_y = swapped(near, X_BIT), swapped(far, Y_BIT)
+    arrays = [
+        near,
+        near_x,
+        swapped(near, Y_BIT),
+        swapped(near_x, Y_BIT),
+        far,
+        swapped(far, X_BIT),
+        far_y,
+        swapped(far_y, X_BIT),
+    ]
+    return arrays, [((at % 4 // 2) * 4 + at // 4, at % 2) for at in range(16)]
 
 
 def collected_small(line):
     stacked = jnp.stack(line)
     beside = swapped(stacked, X_BIT)
-    return [stacked, beside, swapped(stacked, Y_BIT), swapped(beside, Y_BIT)]
-
-
-def summed_along(parts):
-    total = parts[0]
-    for along in (1, 2, 3):
-        total = total + swapped(parts[along].astype(jnp.bfloat16), Z_BITS[along]).astype(jnp.float32)
-    return total
-
-
-def summed(whole, slots, col_blocks):
+    arrays = [stacked, beside, swapped(stacked, Y_BIT), swapped(beside, Y_BIT)]
+    return arrays, [(at // 4, at % 4) for at in range(16)]
+
+
+GROUPS = ((0, 1, 4, 5), (8, 9, 12, 13), (2, 3, 10, 11), (6, 7, 14, 15))
+GROUP_OF = {at: (group, place) for group, held in enumerate(GROUPS) for place, at in enumerate(held)}
+
+
+def summed(grouped):
     low, full = jnp.bfloat16, jnp.float32
-    groups = ((0, 1, 4, 5), (8, 9, 12, 13), (2, 3, 10, 11), (6, 7, 14, 15))
-    keep_a, send_a, keep_b, send_b = spread(whole, slots, groups, col_blocks)
+    keep_a, send_a, keep_b, send_b = grouped
     got_a = swapped(send_a, Y_BIT)
     got_b = swapped(send_b, X_BIT)
     onward_a = (keep_a[2:].astype(full) + got_a[2:].astype(full)).astype(low)
@@ -477,16 +479,10 @@
     here_b = keep_b[:2].astype(full) + got_b[:2].astype(full)
     here_a = here_a + swapped(onward_a, X_BIT).astype(full)
     here_b = here_b + swapped(onward_b, Y_BIT).astype(full)
-    return summed_along((here_a[0], here_a[1], here_b[0], here_b[1]))
-
-
-def summed_small(whole, slots):
-    low, full = jnp.bfloat16, jnp.float32
-    keep, send = spread(whole, slots, (tuple(range(8)), tuple(range(8, 16))))
-    got = swapped(send, Y_BIT)
-    onward = (keep[4:].astype(full) + got[4:].astype(full)).astype(low)
-    here = keep[:4].astype(full) + got[:4].astype(full)
-    return summed_along(here + swapped(onward, X_BIT).astype(full))
+    total = here_a[0]
+    for along, part in ((1, here_a[1]), (2, here_b[0]), (3, here_b[1])):
+        total = total + swapped(part.astype(low), Z_BITS[along]).astype(full)
+    return total
 
 
 def lanes_low(rows):
@@ -732,9 +728,6 @@
     own_rows = inputs.shape[1]
     share = joint_weight.shape[0]
 
-    def own_first(value):
-        return jnp.concatenate([value, swapped(value, CORE_BIT)], axis=0)
-
     def chip_order(mine, theirs):
         return jnp.where(
             even,
@@ -747,57 +740,77 @@
         theirs = jnp.where(even, parts[1], parts[0])
         return chip_order(mine, swapped(theirs, CORE_BIT))
 
+    def by_depth(value):
+        value = jnp.where(depth % 2 == 0, value, value.reshape((2, 2) + value.shape[1:])[:, ::-1].reshape(value.shape))
+        return jnp.where(depth < 2, value, jnp.concatenate([value[2:], value[:2]], axis=0))
+
     chip_ids = jnp.arange(16, dtype=jnp.int32)
     across, along = chip_ids // 4, chip_ids % 4
     slots = (across ^ group) * 4 + (along ^ depth)
     col_slots = jnp.arange(4, dtype=jnp.int32) ^ depth
-    joint_slots = jnp.concatenate([slots, col_slots])
     mixer_slots = ((slots // 8) ^ core) * 8 + (((slots // 2) % 4) ^ depth) * 2 + slots % 2
+    table = jnp.concatenate([slots, col_slots, mixer_slots])
     places = block_order[
         ((chip_ids // 4) ^ depth) * 4 + (((chip_ids // 2) % 2) ^ core) * 2 + chip_ids % 2
     ]
 
-    def line_of(piece):
-        return [piece] + [swapped(piece, bits) for bits in Z_BITS[1:]]
+    tokens = inputs[0]
+    pair = jnp.concatenate([tokens, cotangent[0]], axis=0)
+    pair_got = swapped(pair, CORE_BIT)
 
     units = expand_weight.shape[1] // 2
+    small = jnp.concatenate(
+        [
+            jnp.concatenate(
+                [
+                    first_gain,
+                    first_shift,
+                    query_bias,
+                    value_bias,
+                    mixer_bias,
+                    second_gain,
+                    second_shift,
+                    reduce_bias,
+                ]
+            ),
+            expand_bias,
+        ]
+    ).reshape(1, 384)
     joint_parts = joint_weight.reshape(share, 3, 2, 4, 128).transpose(2, 0, 3, 1, 4).reshape(2, share, 1536)
-    joint_line = line_of(cores_exchanged((joint_parts[0], joint_parts[1])))
-    joint_full = placed(collected(joint_line), joint_slots, 4).reshape(D, 1536)
-    expand_parts = expand_weight.reshape(share, 16, 2, 128)
-    expand_own = cores_exchanged(
-        (expand_parts[:, :, 0].reshape(share, units), expand_parts[:, :, 1].reshape(share, units))
-    )
-    hidden_own = jnp.concatenate([expand_own[:, : units // 2], expand_own[:, units // 2 :], reduce_weight])
-    hidden_full = lax.all_gather(hidden_own, CHIPS, axis=0, tiled=False)
-    expand_full = hidden_full[:, :128].reshape(16, 2, 64, D).transpose(0, 2, 1, 3).reshape(D, units)
-    reduce_full = hidden_full[:, 128:].reshape(units, D)
-
+    small_rows = jnp.pad(small, ((0, 7), (0, 1536 - 384)))
+    joint_mine = jnp.where(even, joint_parts[0], joint_parts[1])
+    joint_theirs = jnp.where(even, joint_parts[1], joint_parts[0])
+    joint_got = swapped(jnp.concatenate([joint_theirs, small_rows]), CORE_BIT)
+    small_got = joint_got[share:, :384]
+    small_pair = jnp.concatenate(
+        [
+            jnp.where(even, small_rows[:, :384], small_got),
+            jnp.where(even, small_got, small_rows[:, :384]),
+            jnp.zeros((8, 768), low),
+        ],
+        axis=1,
+    )
+    joint_own = jnp.concatenate([chip_order(joint_mine, joint_got[:share]), small_pair])
+    joint_line = line_of(joint_own)
+    joint_arrays, joint_at = collected(joint_line)
+    joint_plan = []
+    for at, (array, entry) in enumerate(joint_at):
+        for col in range(4):
+            source_at = looked(entry, 64, 16 + col, 384)
+            joint_plan.append((array, source_at, col, slot(at)))
+            joint_plan.append((array, source_at, 4, slot_part(at, 0, 64, col * 384, 384)))
+        joint_plan.append((array, fixed(entry, pl.ds(64, 8), pl.ds(0, 768)), 5, slot(at)))
+    joint_done = moved(
+        table,
+        joint_arrays,
+        joint_plan,
+        [(16, 64, 384)] * 4 + [(16, 64, 1536), (16, 8, 768)],
+    )
+    joint_columns = [part.reshape(D, 384) for part in joint_done[:4]]
+    joint_full = joint_done[4].reshape(D, 1536)
+    small_all = joint_done[5][:, 0].reshape(32, 384)
     count = share
-    small = jnp.stack(
-        [
-            jnp.pad(item, (0, 128 - item.shape[0]))
-            for item in (
-                first_gain,
-                first_shift,
-                query_bias,
-                value_bias,
-                mixer_bias,
-                second_gain,
-                second_shift,
-                reduce_bias,
-                expand_bias,
-            )
-        ]
-    )
-    small, _ = lax.optimization_barrier((small, joint_line[3]))
-    small_line = jnp.stack(line_of(chip_order(small[None], swapped(small, CORE_BIT)[None])))
-    small_all = jnp.stack(
-        [small_line] + [swapped(small_line, bits) for bits in (X_BIT, Y_BIT, X_BIT + Y_BIT)]
-    ).reshape(16, -1)
-    pick = (slots[None, :] == chip_ids[:, None]).astype(low)
-    small_all = product(pick, small_all).reshape(32, 9, 128).transpose(1, 0, 2)
-    rows_of = small_all[:8, :, :count].reshape(8, 32 * count)
+    rows_of = small_all[:, : 8 * count].reshape(32, 8, count).transpose(1, 0, 2).reshape(8, 32 * count)
     (
         gain_one,
         shift_one,
@@ -808,33 +821,49 @@
         shift_two,
         reduce_shift,
     ) = [rows_of[at] for at in range(8)]
-    expand_shift = small_all[8].reshape(16, 2, 128)
+    expand_shift = small_all[:, 8 * count :].reshape(16, 2, 128)
     expand_shift = jnp.where(even, expand_shift[:, 0], expand_shift[:, 1]).reshape(-1)
 
+    expand_parts = expand_weight.reshape(share, 16, 2, 128)
+    expand_own = cores_exchanged(
+        (expand_parts[:, :, 0].reshape(share, units), expand_parts[:, :, 1].reshape(share, units))
+    )
     mixer_own = cores_exchanged((mixer_weight[:, : D // 2], mixer_weight[:, D // 2 :]))
-    mixer_own, joint_full = lax.optimization_barrier((mixer_own, joint_full))
-    mixer_cols = placed(collected_small(line_of(mixer_own)), mixer_slots).reshape(2, D // 2, D // 2)
+    hidden_own = jnp.concatenate([expand_own[:, :D], expand_own[:, D:], reduce_weight])
+    mixer_own, hidden_own, _ = lax.optimization_barrier((mixer_own, hidden_own, joint_line[1:]))
+    mixer_arrays, mixer_at = collected_small(line_of(mixer_own))
+    hidden_arrays, hidden_at = collected_pairs(line_of(hidden_own))
+    mixer_cols = moved(
+        table,
+        mixer_arrays,
+        [(array, fixed(entry), 0, slot(20 + at)) for at, (array, entry) in enumerate(mixer_at)],
+        [(16, 64, D // 2)],
+    )[0].reshape(2, D // 2, D // 2)
     mixer_mine, mixer_theirs = mixer_cols[0], swapped(mixer_cols[1], CORE_BIT)
     mixer_full = jnp.where(
         even,
         jnp.concatenate([mixer_mine, mixer_theirs], axis=1),
         jnp.concatenate([mixer_theirs, mixer_mine], axis=1),
     )
-
-    token_rows = own_first(inputs[0]).astype(full)
-    upstream = own_first(cotangent[0])
+    hidden_plan = []
+    for at, (array, entry) in enumerate(hidden_at):
+        hidden_plan.append((array, fixed(entry, pl.ds(0, 64)), 0, slot_part(at, 0, 64, 0, D)))
+        hidden_plan.append((array, fixed(entry, pl.ds(64, 64)), 0, slot_part(at, 0, 64, D, D)))
+        hidden_plan.append((array, fixed(entry, pl.ds(128, 128)), 1, slot(at)))
+    expand_full, reduce_full = moved(table, hidden_arrays, hidden_plan, [(16, 64, units), (16, 128, D)])
+    expand_full, reduce_full = expand_full.reshape(D, units), reduce_full.reshape(units, D)
+
+    token_rows = jnp.concatenate([tokens, pair_got[:own_rows]], axis=0).astype(full)
+    upstream = jnp.concatenate([cotangent[0], pair_got[own_rows:]], axis=0)
     scaled_one, inverse_one = norm_parts(token_rows)
     normed = (scaled_one * gain_one + shift_one).astype(low)
     halves_of = [
         jnp.where(even, item[: D // 2], item[D // 2 :]).reshape(4, 1, 128)
         for item in (query_shift, value_shift)
     ]
-    joint_shift = jnp.concatenate([halves_of[0], jnp.zeros_like(halves_of[0]), halves_of[1]], axis=1)
-    joint_shift = product(
-        (col_slots[:, None] == jnp.arange(4)[None, :]).astype(low), joint_shift.reshape(4, 384).astype(low)
-    ).reshape(-1)
-    joint_rows = (product(normed, joint_full) + joint_shift).astype(low)
-    head_pieces = [joint_rows[:, at * 384 : (at + 1) * 384] for at in range(4)]
+    joint_shift = by_depth(jnp.concatenate([halves_of[0], jnp.zeros_like(halves_of[0]), halves_of[1]], axis=1))
+    joint_shift = joint_shift.reshape(4, 384)
+    head_pieces = [(product(normed, joint_columns[at]) + joint_shift[at]).astype(low) for at in range(4)]
     head_pieces = [head_pieces[0]] + [swapped(head_pieces[at], Z_BITS[at]) for at in (1, 2, 3)]
     forward = head_forward(head_pieces, places)
     mixed_out, (joint_sorted, mixed_sorted, totals_sorted) = forward[:4], forward[4:]
@@ -859,12 +888,7 @@
 
     reduce_gradient = inner_rows(active, upstream).astype(low).reshape(16, 128, D)
     grad_before = gelu_pull(inner_cols(upstream, reduce_full))[0].astype(low)
-    expand_gradient = inner_rows(second, grad_before).astype(low)
-    expand_gradient = expand_gradient.reshape(16, 64, 2, D).transpose(0, 2, 1, 3).reshape(16, 128, D)
-    hidden_gradient = jnp.concatenate([expand_gradient, reduce_gradient], axis=1)
-    hidden_sum = lax.psum_scatter(hidden_gradient, CHIPS, scatter_dimension=0, tiled=False)
-    reduce_sum = hidden_sum[128:].astype(full)
-    expand_sum = jnp.concatenate([hidden_sum[:64], hidden_sum[64:128]], axis=1)
+    expand_gradient = inner_rows(second, grad_before).astype(low).reshape(16, 64, units)
     expand_shift_gradient = jnp.sum(grad_before.astype(full), axis=0)
     grad_second = both_cores(inner_cols(grad_before, expand_full))
     upstream_full = upstream.astype(full)
@@ -876,77 +900,126 @@
     grad_pieces = [grad_pieces[0]] + [swapped(grad_pieces[at], Z_BITS[at]) for at in (1, 2, 3)]
     mixer_keep = jnp.where(even, mixer_gradient[:, : D // 2], mixer_gradient[:, D // 2 :])
     mixer_send = jnp.where(even, mixer_gradient[:, D // 2 :], mixer_gradient[:, : D // 2])
-    mixer_whole = jnp.concatenate([mixer_keep, swapped(mixer_send, CORE_BIT)], axis=0)
-    mixer_sum = summed_small(mixer_whole.reshape(16, 64, D // 2), mixer_slots)
+    mixer_got = swapped(mixer_send, CORE_BIT)
+    hidden_plan = []
+    for at in range(16):
+        to, place = GROUP_OF[at]
+        hidden_plan.append((0, slot_part(at, 0, 64, 0, D), to, fixed(place, pl.ds(0, 64))))
+        hidden_plan.append((0, slot_part(at, 0, 64, D, D), to, fixed(place, pl.ds(64, 64))))
+        hidden_plan.append((1, slot(at), to, fixed(place, pl.ds(128, 128))))
+        for half in range(2):
+            hidden_plan.append(
+                (
+                    2,
+                    slot_rows(20 + at, half * 32, 32),
+                    to,
+                    fixed(place, pl.ds(256, 32), pl.ds(half * (D // 2), D // 2)),
+                )
+            )
+    mixer_whole = jnp.concatenate([mixer_keep, mixer_got], axis=0).reshape(16, 64, D // 2)
+    hidden_sum = summed(
+        moved(table, (expand_gradient, reduce_gradient, mixer_whole), hidden_plan, [(4, 288, D)] * 4)
+    )
     grad_out = head_backward(joint_sorted, mixed_sorted, totals_sorted, grad_pieces, places)
     grad_joint = jnp.concatenate(
         [grad_out[0]] + [swapped(grad_out[at], Z_BITS[at]) for at in (1, 2, 3)], axis=1
     )
     joint_gradient = inner_rows(normed, grad_joint).astype(low).reshape(16, 64, 1536)
-    joint_sum = summed(joint_gradient, joint_slots, 4)
-    joint_sums = product(
-        (col_slots[:, None] == jnp.arange(4)[None, :]).astype(full),
-        jnp.sum(grad_joint.astype(full), axis=0).reshape(4, 384),
-    ).reshape(4, 3, 128)
-    grad_normed = own_sum(inner_cols(grad_joint, joint_full))
-    own_scaled = scaled_one[:own_rows]
-    input_gradient = (
-        grad_middle[:own_rows] + norm_pull(grad_normed, own_scaled, inverse_one[:own_rows], gain_one)
-    ).astype(low)
+    grad_normed_part = inner_cols(grad_joint, joint_full)
+    joint_sums = by_depth(jnp.sum(grad_joint.astype(full), axis=0).reshape(4, 3, 128))
 
     def one_core(values):
         values = values.reshape(1, -1)
         nothing = jnp.zeros_like(values)
         return jnp.where(
-            even, jnp.concatenate([values, nothing]), jnp.concatenate([nothing, values])
-        )
-
-    expand_rows = one_core(expand_shift_gradient).reshape(2, 16, 128).transpose(1, 0, 2)
-    sums = jnp.concatenate(
+            even, jnp.concatenate([values, nothing], axis=1), jnp.concatenate([nothing, values], axis=1)
+        )[0]
+
+    expand_rows = expand_shift_gradient.reshape(16, 1, 128)
+    expand_rows = jnp.where(
+        even,
+        jnp.concatenate([expand_rows, jnp.zeros_like(expand_rows)], axis=1),
+        jnp.concatenate([jnp.zeros_like(expand_rows), expand_rows], axis=1),
+    ).reshape(32, 128)
+    sums = jnp.stack(
         [
-            item.reshape(32, -1)
-            for item in (
-                jnp.sum(grad_normed * own_scaled, axis=0),
-                jnp.sum(grad_normed, axis=0),
-                one_core(joint_sums[:, 0]),
-                one_core(joint_sums[:, 2]),
-                jnp.sum(grad_branch[:own_rows].astype(full), axis=0),
-                jnp.sum(grad_second[:own_rows] * scaled_two[:own_rows], axis=0),
-                jnp.sum(grad_second[:own_rows], axis=0),
-                jnp.sum(upstream_full[:own_rows], axis=0),
-                expand_rows,
-            )
-        ],
-        axis=1,
-    )
-    for mask in (CORE_BIT, Z_BITS[1], Z_BITS[2], X_BIT, Y_BIT):
-        sums = sums + swapped(sums, mask)
-    own_sums = lax.dynamic_slice_in_dim(sums, group * 8 + depth * 2 + core, 1, axis=0)[0]
+            jnp.sum(grad_normed_part * scaled_one, axis=0),
+            jnp.sum(grad_normed_part, axis=0),
+            one_core(joint_sums[:, 0]),
+            one_core(joint_sums[:, 2]),
+            jnp.sum(grad_branch[:own_rows].astype(full), axis=0),
+            jnp.sum(grad_second[:own_rows] * scaled_two[:own_rows], axis=0),
+            jnp.sum(grad_second[:own_rows], axis=0),
+            jnp.sum(upstream_full[:own_rows], axis=0),
+        ]
+    )
+    sums = sums.astype(low).reshape(8, 32, count).transpose(1, 0, 2).reshape(32, 8 * count)
+    sums = jnp.concatenate([sums, expand_rows.astype(low)], axis=1).reshape(16, 1, 768)
+    sums = jnp.pad(sums, ((0, 0), (0, 7), (0, 0)))
+    joint_plan = []
+    for at in range(16):
+        to, place = GROUP_OF[at]
+        for col in range(4):
+            left = looked(place, 64, 16 + col, 384)
+            joint_plan.append((0, slot_part(at, 0, 64, col * 384, 384), to, left))
+        joint_plan.append((1, slot(at), to, fixed(place, pl.ds(64, 8), pl.ds(0, 768))))
+    joint_sum = summed(moved(table, (joint_gradient, sums), joint_plan, [(4, 72, 1536)] * 4))
+    grad_normed = own_sum(grad_normed_part)
+    input_gradient = (
+        grad_middle[:own_rows]
+        + norm_pull(grad_normed, scaled_one[:own_rows], inverse_one[:own_rows], gain_one)
+    ).astype(low)
+
+    def paired(first_core, second_core):
+        mine = jnp.where(even, first_core, second_core)
+        got = swapped(jnp.where(even, second_core, first_core), CORE_BIT)
+        return mine, got
+
+    mixer_mine, mixer_got = paired(hidden_sum[256:, : D // 2], hidden_sum[256:, D // 2 :])
+    mixer_out = jnp.where(
+        even,
+        jnp.concatenate([mixer_mine, mixer_got], axis=1),
+        jnp.concatenate([mixer_got, mixer_mine], axis=1),
+    )
+    expand_pairs = hidden_sum[:128].reshape(2, 2, share, 8, 128)
+    expand_mine, expand_got = paired(expand_pairs[:, 0], expand_pairs[:, 1])
+    expand_out = jnp.where(
+        even, jnp.stack([expand_mine, expand_got], axis=3), jnp.stack([expand_got, expand_mine], axis=3)
+    )
+    expand_out = expand_out.transpose(1, 0, 2, 3, 4).reshape(share, 2 * units)
+    joint_mine = jnp.where(even, joint_sum[:share], joint_sum[share : 2 * share])
+    joint_got = swapped(
+        jnp.concatenate(
+            [jnp.where(even, joint_sum[share : 2 * share], joint_sum[:share]), joint_sum[2 * share :]]
+        ),
+        CORE_BIT,
+    )
+    joint_mine_parts = joint_mine.reshape(share, 4, 3, 128)
+    joint_got_parts = joint_got[:share].reshape(share, 4, 3, 128)
+    joint_out = jnp.where(
+        even,
+        jnp.stack([joint_mine_parts, joint_got_parts], axis=1),
+        jnp.stack([joint_got_parts, joint_mine_parts], axis=1),
+    )
+    joint_out = joint_out.transpose(0, 3, 1, 2, 4).reshape(share, 3 * D)
+    own_sums = joint_sum[2 * share, :768] + joint_got[share, :768]
+    own_sums = jnp.where(even, own_sums[:384], own_sums[384:])
     vectors = [own_sums[at * count : (at + 1) * count] for at in range(8)] + [own_sums[8 * count :]]
-
-    def finished(total):
-        mine = jnp.where(even, total[:share], total[share:])
-        theirs = swapped(jnp.where(even, total[share:], total[:share]), CORE_BIT)
-        return jnp.where(even, jnp.stack([mine, theirs], axis=0), jnp.stack([theirs, mine], axis=0))
-
-    joint_out = finished(joint_sum).reshape(2, share, 4, 3, 128).transpose(1, 3, 0, 2, 4)
-    mixer_out = finished(mixer_sum).transpose(1, 0, 2)
-    expand_out = finished(expand_sum).reshape(2, share, 16, 128).transpose(1, 2, 0, 3).astype(full)
     return (
         result.astype(low)[None],
         input_gradient[None],
         vectors[0],
         vectors[1],
-        joint_out.reshape(share, 3 * D),
+        joint_out,
         vectors[2],
         vectors[3],
-        mixer_out.reshape(share, D),
+        mixer_out,
         vectors[4],
         vectors[5],
         vectors[6],
-        expand_out.reshape(share, 2 * units),
+        expand_out,
         vectors[8],
-        reduce_sum,
+        hidden_sum[128:256],
         vectors[7],
     )
 

time: 575 us -> 594 us (1.033)
  waiting for transfers between devices: 219 us -> 284 us
  local copies, waits for them, and re-layouts: 75 us -> 38.9 us
  starting transfers between devices: 120 us -> 92.4 us
  Pallas kernels: 48.1 us -> 65.1 us
  between operations: 15.7 us -> 2.46 us
  matrix products: 44.9 us -> 56.9 us
    ppermute x71 -> x69, waiting for transfers between devices: 219 us -> 284 us  [swapped(): lax.ppermute(value, ALL, [(source, source ^ mask) for source in range(cou...]
    ppermute x71 -> x69, starting transfers between devices: 120 us -> 92.4 us  [swapped(): lax.ppermute(value, ALL, [(source, source ^ mask) for source in range(cou...]
    reshape x16 -> x8, local copies, waits for them, and re-layouts: 24 us -> 3.36 us  [the longest x1 1.9 us: chip_body(): joint_out = joint_out.transpose(0, 3, 1, 2, 4).reshape(share, 3 * D)]
    pallas_call x4 -> x5, Pallas kernels: 15.8 us -> 32.7 us  [moved(): pl.pallas_call(lambda *refs: moved_kernel(*refs, plan=plan, source_count=...]
    transpose x3, local copies, waits for them, and re-layouts: 14.4 us -> 1.28 us  [the longest x1 0.85 us: chip_body(): joint_out = joint_out.transpose(0, 3, 1, 2, 4).reshape(share, 3 * D)]
    dot_general x4, matrix products: 16.4 us -> 25.8 us  [inner_cols(): lax.dot_general(left, right, (((1,), (1,)), ((), ())), preferred_element_...]
    concatenate x4 -> x8, other arithmetic: 11.9 us -> 4.55 us  [the longest x1 2.07 us: chip_body(): jnp.concatenate([mixer_keep, mixer_got], axis=0).reshape(16, 64, D // 2)]
    unnamed x157 -> x196, local copies, waits for them, and re-layouts: 17.3 us -> 12.4 us
  transfers between devices with their start and end apart: 73 -> 69, of which waited for: 33 -> 29; matrix products, arithmetic and copies ran while one was open for 18% -> 18% of each run, Pallas kernels for 8% -> 10%
where the time goes in v3:
time: 594 us; the launch traced here: 586 us
  waiting for transfers between devices  284 us (48%)
  starting transfers between devices  92.4 us (16%)
  Pallas kernels  65.1 us (11%)
  matrix products  56.9 us (10%)
  other arithmetic  45.8 us (8%)
  local copies, waits for them, and re-layouts  38.9 us (7%)
    ppermute x69, waiting for transfers between devices, swapped(): lax.ppermute(value, ALL, [(source, source ^ mask) for source in range(cou...  284 us
    ppermute x69, starting transfers between devices, swapped(): lax.ppermute(value, ALL, [(source, source ^ mask) for source in range(cou...  92.4 us
    pallas_call x5, Pallas kernels, moved(): pl.pallas_call(lambda *refs: moved_kernel(*refs, plan=plan, source_count=...  32.7 us
    dot_general x4, matrix products, inner_cols(): lax.dot_general(left, right, (((1,), (1,)), ((), ())), preferred_element_...  25.8 us
    pallas_call x1, Pallas kernels, head_backward(): pl.pallas_call(head_backward_kernel, out_shape=[jax.ShapeDtypeStruct((row...  20.7 us
    dot_general x4, matrix products, inner_rows(): lax.dot_general(left, right, (((0,), (0,)), ((), ())), preferred_element_...  15.9 us
    dot_general x7, matrix products, product(): return jnp.dot(left, right, preferred_element_type=jnp.float32)  15.2 us
    unnamed x196, local copies, waits for them, and re-layouts  12.4 us
  transfers between devices with their start and end apart: 69, of which 29 were waited for; matrix products, arithmetic and copies ran while one was open for 18% of the time, Pallas kernels for 10%

profile of v3, /device:TPU:0, one launch (start us, length us, event | category | flops | bytes accessed | tf_op | source)
XLA Modules:
  0.0 585.7 jit_solution(10853408858435994724)
XLA Ops:
  6.8 2.9 collective-permute-start.2
  9.8 2.6 collective-permute-start.3
  15.7 4.0 collective-permute-done.2
  21.4 7.1 %collective-permute-done.3 = bf16[72,1536]{1,0:T(8,128)(2,1)S(1)} collective-permute-done((bf16[72,1536]{1,0:T(8,128)(2,1)S(1)}, bf16[72,1536]{1,0:T(8,128)(2,1)S(1)}, u32[]{:S(2)}, u32[]{:S(2)}) %collective-permute-start.3) | collective-permute-done | bytes 221216 | tf_op jit(solution)/shard_map/ppermute | solution.py:374
  28.5 2.5 collective-permute-start.27
  31.0 3.9 collective-permute-start.26
  53.2 3.2 collective-permute-done.12
  62.1 3.4 collective-permute-start.38
  67.8 7.7 %moved.5 = (bf16[16,64,384]{2,1,0:T(8,128)(2,1)}, bf16[16,64,384]{2,1,0:T(8,128)(2,1)}, bf16[16,64,384]{2,1,0:T(8,128)(2,1)}, bf16[16,64,384]{2,1,0:T(8,128)(2,1...) custom-call(s32[36]{0:T(128)} %pad_add_fusion.refs_0_, bf16[1,72,1536]{2,1,0:T(8,128)(2,1)} %get-tuple-element.123.refs_1_, ...), custom_call_target="tpu_custom_call" | custom-call | tf_op jit(solution)/shard_map/moved/pallas_call | solution.py:393
  82.0 3.0 moved.6
  96.8 8.3 %collective-permute-done.17.refs_1_ = bf16[512,384]{1,0:T(8,128)(2,1)S(1)} collective-permute-done((bf16[512,384]{1,0:T(8,128)(2,1)S(1)}, bf16[512,384]{1,0:T(8,128)(2,1)S(1)}, u32[]{:S(2)}, u32[]{:S(2)}) %collective-permute-start.17) | collective-permute-done | bytes 393248 | tf_op jit(solution)/shard_map/ppermute | solution.py:374
  106.6 28.8 %collective-permute-done.18.refs_2_ = bf16[512,384]{1,0:T(8,128)(2,1)} collective-permute-done((bf16[512,384]{1,0:T(8,128)(2,1)S(1)}, bf16[512,384]{1,0:T(8,128)(2,1)}, u32[]{:S(2)}, u32[]{:S(2)}) %collective-permute-start.18) | collective-permute-done | bytes 393248 | tf_op jit(solution)/shard_map/ppermute | solution.py:374
  135.4 11.8 %head_forward.1 = (bf16[512,128]{1,0:T(8,128)(2,1)}, bf16[512,128]{1,0:T(8,128)(2,1)}, bf16[512,128]{1,0:T(8,128)(2,1)}, bf16[512,128]{1,0:T(8,128)(2,1)}, bf16[...) custom-call(s32[16]{0:T(128)} %gather_fusion, bf16[512,384]{1,0:T(8,128)(2,1)} %fusion.10.refs_0_, ...), custom_call_target="tpu_custom_call" | custom-call | tf_op jit(solution)/shard_map/head_forward/pallas_call | solution.py:554
  147.2 8.9 %collective-permute-start.20 = (bf16[512,128]{1,0:T(8,128)(2,1)}, bf16[512,128]{1,0:T(8,128)(2,1)S(1)}, u32[]{:S(2)}, u32[]{:S(2)}) collective-permute-start(bf16[512,128]{1,0:T(8,128)(2,1)} %get-tuple-element.50), channel_id=1, source_target_pairs={{0,2},{1,3},{2,0},{3,1},{4,6},{5,7},{6,4},{7,5},{8,10},{9,11},{10,... | collective-permute-start | bytes 393224 | tf_op jit(solution)/shard_map/ppermute | solution.py:374
  162.8 8.4 %collective-permute-done.21 = bf16[512,128]{1,0:T(8,128)(2,1)S(1)} collective-permute-done((bf16[512,128]{1,0:T(8,128)(2,1)S(1)}, bf16[512,128]{1,0:T(8,128)(2,1)S(1)}, u32[]{:S(2)}, u32[]{:S(2)}) %collective-permute-start.21) | collective-permute-done | bytes 131104 | tf_op jit(solution)/shard_map/ppermute | solution.py:374
  171.3 3.5 fusion.82
  180.9 3.9 collective-permute-done.40.refs_7_
  187.3 2.4 fusion.70
  191.6 15.7 %collective-permute-done.35.refs_3_ = bf16[2,256,1024]{2,1,0:T(8,128)(2,1)} collective-permute-done((bf16[2,256,1024]{2,1,0:T(8,128)(2,1)}, bf16[2,256,1024]{2,1,0:T(8,128)(2,1)}, u32[]{:S(2)}, u32[]{:S(2)}) %collective-permute-start.35) | collective-permute-done | bytes 1048608 | tf_op jit(solution)/shard_map/ppermute | solution.py:374
  207.3 21.2 %collective-permute-done.36.refs_4_ = bf16[2,256,1024]{2,1,0:T(8,128)(2,1)} collective-permute-done((bf16[2,256,1024]{2,1,0:T(8,128)(2,1)}, bf16[2,256,1024]{2,1,0:T(8,128)(2,1)}, u32[]{:S(2)}, u32[]{:S(2)}) %collective-permute-start.36) | collective-permute-done | bytes 1048608 | tf_op jit(solution)/shard_map/ppermute | solution.py:374
  228.5 7.8 %moved.7 = (bf16[16,64,2048]{2,1,0:T(8,128)(2,1)}, bf16[16,128,1024]{2,1,0:T(8,128)(2,1)}) custom-call(s32[36]{0:T(128)} %pad_add_fusion.refs_0_, bf16[2,256,1024]{2,1,0:T(8,128)(2,1)} %pad_maximum_fusion.3.refs_1_, bf16[2,256,1024]{2,1,0:T(8,128)(2,1)} %collective-permute-done.34.refs_2_, bf16[2,256,1024]{2,1,0:T(8,128)(2,1)} %collective-permute-done.35.refs_3_, ...), custom_call_target="tpu_custom_call" | custom-call | tf_op jit(solution)/shard_map/moved/pallas_call | solution.py:393
  236.3 5.3 fusion.31
  241.7 2.9 fusion.67
  244.6 15.9 %convert_reduce_fusion = (f32[2048]{0:T(1024)S(1)}, bf16[512,2048]{1,0:T(8,128)(2,1)S(1)}) fusion(f32[512,2048]{1,0:T(8,128)S(1)} %fusion.31, f32[2048]{0:T(1024)S(1)} %bitcast.222, bf16[2048,1024]{1,0:T(8,128)(2,1)S(1)} %bitcast.234, bf16[256,1024]{1,0:T(8,128)(2,1)S(1)} %copy-done.9, bf16[256,1024]{1,0:T(8,128)(2,1)S(1)} %bitcast.180), kind=kOutput, calls=%fused_computation.10 | convolution fusion | flops 2173696000 | bytes 11550720 | tf_op jit(solution)/shard_map/dot_general | solution.py:45
  260.5 2.4 fusion.83
  264.4 4.5 convolution_convert_fusion.1
  270.4 5.3 convolution_convert_fusion
  283.4 2.4 collective-permute-start.45
  288.4 2.7 collective-permute-done.44.refs_1_
  291.2 5.1 collective-permute-done.45.refs_2_
  297.0 20.7 %head_backward.1 = (bf16[512,384]{1,0:T(8,128)(2,1)}, bf16[512,384]{1,0:T(8,128)(2,1)}, bf16[512,384]{1,0:T(8,128)(2,1)}, bf16[512,384]{1,0:T(8,128)(2,1)}) custom-call(s32[16]{0:T(128)} %gather_fusion, bf16[2048,384]{1,0:T(8,128)(2,1)} %get-tuple-element.57.joint_ref, f32[2048,128]{1,0:T(8,128)} %get-tuple-element.58.mixed_ref, ...), custom_call_target="tpu_custom_call" | custom-call | tf_op jit(solution)/shard_map/head_backward/pallas_call | solution.py:671
  317.6 2.7 collective-permute-start.47
  329.4 7.2 %collective-permute-done.47 = bf16[512,384]{1,0:T(8,128)(2,1)} collective-permute-done((bf16[512,384]{1,0:T(8,128)(2,1)}, bf16[512,384]{1,0:T(8,128)(2,1)}, u32[]{:S(2)}, u32[]{:S(2)}) %collective-permute-start.47) | collective-permute-done | bytes 393248 | tf_op jit(solution)/shard_map/ppermute | solution.py:374
  338.4 12.0 %collective-permute-done.48 = bf16[512,384]{1,0:T(8,128)(2,1)} collective-permute-done((bf16[512,384]{1,0:T(8,128)(2,1)}, bf16[512,384]{1,0:T(8,128)(2,1)}, u32[]{:S(2)}, u32[]{:S(2)}) %collective-permute-start.48) | collective-permute-done | bytes 393248 | tf_op jit(solution)/shard_map/ppermute | solution.py:374
  355.8 5.6 fusion.68
  364.2 5.3 convolution_convert_fusion.2
  370.5 5.2 moved.8
  377.2 2.5 fusion.24
  381.8 8.9 %moved.9 = (bf16[4,288,1024]{2,1,0:T(8,128)(2,1)}, bf16[4,288,1024]{2,1,0:T(8,128)(2,1)}, bf16[4,288,1024]{2,1,0:T(8,128)(2,1)}, bf16[4,288,1024]{2,1,0:T(8,128)(2,1)}) custom-call(s32[36]{0:T(128)} %pad_add_fusion.refs_0_, bf16[16,64,2048]{2,1,0:T(8,128)(2,1)} %bitcast.183, bf16[16,128,1024]{2,1,0:T(8,128)(2,1)} %bitcast.184, bf16[16,64,512]{2,1,0:T(8,128)(2,1)} %bitcast.185), custom_call_target="tpu_custom_call" | custom-call | tf_op jit(solution)/shard_map/moved/pallas_call | solution.py:393
  394.9 3.6 collective-permute-done.54
  401.2 62.8 %collective-permute-done.51 = bf16[4,72,1536]{2,1,0:T(8,128)(2,1)S(1)} collective-permute-done((bf16[4,72,1536]{2,1,0:T(8,128)(2,1)}, bf16[4,72,1536]{2,1,0:T(8,128)(2,1)S(1)}, u32[]{:S(2)}, u32[]{:S(2)}) %collective-permute-start.51) | collective-permute-done | bytes 884768 | tf_op jit(solution)/shard_map/ppermute | solution.py:374
  464.7 8.1 %collective-permute-done.55 = bf16[2,72,1536]{2,1,0:T(8,128)(2,1)S(1)} collective-permute-done((bf16[2,72,1536]{2,1,0:T(8,128)(2,1)S(1)}, bf16[2,72,1536]{2,1,0:T(8,128)(2,1)S(1)}, u32[]{:S(2)}, u32[]{:S(2)}) %collective-permute-start.55) | collective-permute-done | bytes 442400 | tf_op jit(solution)/shard_map/ppermute | solution.py:374
  476.2 4.6 collective-permute-start.56
  482.7 14.1 %collective-permute-done.56 = bf16[72,1536]{1,0:T(8,128)(2,1)S(1)} collective-permute-done((bf16[72,1536]{1,0:T(8,128)(2,1)S(1)}, bf16[72,1536]{1,0:T(8,128)(2,1)S(1)}, u32[]{:S(2)}, u32[]{:S(2)}) %collective-permute-start.56) | collective-permute-done | bytes 221216 | tf_op jit(solution)/shard_map/ppermute | solution.py:374
  511.9 14.8 %collective-permute-done.64 = bf16[2,288,1024]{2,1,0:T(8,128)(2,1)} collective-permute-done((bf16[2,288,1024]{2,1,0:T(8,128)(2,1)}, bf16[2,288,1024]{2,1,0:T(8,128)(2,1)}, u32[]{:S(2)}, u32[]{:S(2)}) %collective-permute-start.64) | collective-permute-done | bytes 1179680 | tf_op jit(solution)/shard_map/ppermute | solution.py:374
  526.7 2.5 add_convert_fusion
  536.8 10.7 %collective-permute-done.66 = bf16[288,1024]{1,0:T(8,128)(2,1)S(1)} collective-permute-done((bf16[288,1024]{1,0:T(8,128)(2,1)S(1)}, bf16[288,1024]{1,0:T(8,128)(2,1)S(1)}, u32[]{:S(2)}, u32[]{:S(2)}) %collective-permute-start.66) | collective-permute-done | bytes 589856 | tf_op jit(solution)/shard_map/ppermute | solution.py:374
  547.5 33.0 %collective-permute-done.65 = bf16[288,1024]{1,0:T(8,128)(2,1)S(1)} collective-permute-done((bf16[288,1024]{1,0:T(8,128)(2,1)S(1)}, bf16[288,1024]{1,0:T(8,128)(2,1)S(1)}, u32[]{:S(2)}, u32[]{:S(2)}) %collective-permute-start.65) | collective-permute-done | bytes 589856 | tf_op jit(solution)/shard_map/ppermute | solution.py:374
  (466 shorter events, 151.6 us)
Async XLA Ops:
  6.8 12.8 %collective-permute-start.2 = (bf16[72,1536]{1,0:T(8,128)(2,1)S(1)}, bf16[72,1536]{1,0:T(8,128)(2,1)S(1)}, u32[]{:S(2)}, u32[]{:S(2)}) collective-permute-start(bf16[72,1536]{1,0:T(8,128)(2,1)S(1)} %get-tuple-element.124), channel_id=1, source_target_pairs={{0,2},{1,3},{2,0},{3,1},{4,6},{5,7},{6,4},{7,5},{8,10},{9,11},{10,... | collective-permute-start | bytes 663560 | tf_op jit(solution)/shard_map/ppermute | solution.py:374
  9.8 18.7 %collective-permute-start.3 = (bf16[72,1536]{1,0:T(8,128)(2,1)S(1)}, bf16[72,1536]{1,0:T(8,128)(2,1)S(1)}, u32[]{:S(2)}, u32[]{:S(2)}) collective-permute-start(bf16[72,1536]{1,0:T(8,128)(2,1)S(1)} %get-tuple-element.124), channel_id=1, source_target_pairs={{0,4},{1,5},{2,6},{3,7},{4,0},{5,1},{6,2},{7,3},{8,12},{9,13},{10,... | collective-permute-start | bytes 663560 | tf_op jit(solution)/shard_map/ppermute | solution.py:374
  12.4 16.1 %collective-permute-start.4 = (bf16[72,1536]{1,0:T(8,128)(2,1)S(1)}, bf16[72,1536]{1,0:T(8,128)(2,1)S(1)}, u32[]{:S(2)}, u32[]{:S(2)}) collective-permute-start(bf16[72,1536]{1,0:T(8,128)(2,1)S(1)} %get-tuple-element.124), channel_id=1, source_target_pairs={{0,6},{1,7},{2,4},{3,5},{4,2},{5,3},{6,0},{7,1},{8,14},{9,15},{10,... | collective-permute-start | bytes 663560 | tf_op jit(solution)/shard_map/ppermute | solution.py:374
  12.4 22.5 %collective-permute-start.5 = (bf16[72,1536]{1,0:T(8,128)(2,1)S(1)}, bf16[72,1536]{1,0:T(8,128)(2,1)S(1)}, u32[]{:S(2)}, u32[]{:S(2)}) collective-permute-start(bf16[72,1536]{1,0:T(8,128)(2,1)S(1)} %get-tuple-element.124), channel_id=1, source_target_pairs={{0,8},{1,9},{2,10},{3,11},{4,12},{5,13},{6,14},{7,15},{8,0},{9,1},... | collective-permute-start | bytes 663560 | tf_op jit(solution)/shard_map/ppermute | solution.py:374
  14.1 21.0 %collective-permute-start.9 = (bf16[72,1536]{1,0:T(8,128)(2,1)S(1)}, bf16[72,1536]{1,0:T(8,128)(2,1)S(1)}, u32[]{:S(2)}, u32[]{:S(2)}) collective-permute-start(bf16[72,1536]{1,0:T(8,128)(2,1)S(1)} %get-tuple-element.124), channel_id=1, source_target_pairs={{0,16},{1,17},{2,18},{3,19},{4,20},{5,21},{6,22},{7,23},{8,24},{9,... | collective-permute-start | bytes 663560 | tf_op jit(solution)/shard_map/ppermute | solution.py:374
  19.7 21.1 %collective-permute-start.6 = (bf16[72,1536]{1,0:T(8,128)(2,1)S(1)}, bf16[72,1536]{1,0:T(8,128)(2,1)S(1)}, u32[]{:S(2)}, u32[]{:S(2)}) collective-permute-start(bf16[72,1536]{1,0:T(8,128)(2,1)S(1)} %collective-permute-done.2), channel_id=1, source_target_pairs={{0,8},{1,9},{2,10},{3,11},{4,12},{5,13},{6,14},{7,15},{8,0},{9,1},... | collective-permute-start | bytes 663560 | tf_op jit(solution)/shard_map/ppermute | solution.py:374
  40.7 15.7 %collective-permute-start.12 = (bf16[72,1536]{1,0:T(8,128)(2,1)S(1)}, bf16[72,1536]{1,0:T(8,128)(2,1)}, u32[]{:S(2)}, u32[]{:S(2)}) collective-permute-start(bf16[72,1536]{1,0:T(8,128)(2,1)S(1)} %collective-permute-done.4), channel_id=1, source_target_pairs={{0,16},{1,17},{2,18},{3,19},{4,20},{5,21},{6,22},{7,23},{8,24},{9,... | collective-permute-start | bytes 663560 | tf_op jit(solution)/shard_map/ppermute | solution.py:374
  43.4 16.3 %collective-permute-start.28 = (bf16[4,64,512]{2,1,0:T(8,128)(2,1)S(1)}, bf16[4,64,512]{2,1,0:T(8,128)(2,1)S(1)}, u32[]{:S(2)}, u32[]{:S(2)}) collective-permute-start(bf16[4,64,512]{2,1,0:T(8,128)(2,1)S(1)} %pad_maximum_fusion.9.refs_1_), channel_id=1, source_target_pairs={{0,8},{1,9},{2,10},{3,11},{4,12},{5,13},{6,14},{7,15},{8,0},{9,1},... | collective-permute-start | bytes 786440 | tf_op jit(solution)/shard_map/ppermute | solution.py:374
  49.7 12.4 %collective-permute-start.14 = (bf16[72,1536]{1,0:T(8,128)(2,1)}, bf16[72,1536]{1,0:T(8,128)(2,1)S(1)}, u32[]{:S(2)}, u32[]{:S(2)}) collective-permute-start(bf16[72,1536]{1,0:T(8,128)(2,1)} %copy-done.43), channel_id=1, source_target_pairs={{0,16},{1,17},{2,18},{3,19},{4,20},{5,21},{6,22},{7,23},{8,24},{9,... | collective-permute-start | bytes 663560 | tf_op jit(solution)/shard_map/ppermute | solution.py:374
  51.7 13.8 %collective-permute-start.15 = (bf16[72,1536]{1,0:T(8,128)(2,1)}, bf16[72,1536]{1,0:T(8,128)(2,1)S(1)}, u32[]{:S(2)}, u32[]{:S(2)}) collective-permute-start(bf16[72,1536]{1,0:T(8,128)(2,1)} %collective-permute-done.11), channel_id=1, source_target_pairs={{0,8},{1,9},{2,10},{3,11},{4,12},{5,13},{6,14},{7,15},{8,0},{9,1},... | collective-permute-start | bytes 663560 | tf_op jit(solution)/shard_map/ppermute | solution.py:374
  59.8 25.3 %collective-permute-start = (bf16[512,1024]{1,0:T(8,128)(2,1)}, bf16[512,1024]{1,0:T(8,128)(2,1)}, u32[]{:S(2)}, u32[]{:S(2)}) collective-permute-start(bf16[512,1024]{1,0:T(8,128)(2,1)} %pad_maximum_fusion), channel_id=1, source_target_pairs={{0,1},{1,0},{2,3},{3,2},{4,5},{5,4},{6,7},{7,6},{8,9},{9,8},{10,11... | collective-permute-start | bytes 3145736 | tf_op jit(solution)/shard_map/ppermute | solution.py:374
  59.8 19.6 %collective-permute-start.33 = (bf16[256,1024]{1,0:T(8,128)(2,1)S(1)}, bf16[256,1024]{1,0:T(8,128)(2,1)S(1)}, u32[]{:S(2)}, u32[]{:S(2)}) collective-permute-start(bf16[256,1024]{1,0:T(8,128)(2,1)S(1)} %pad_maximum_fusion.8), channel_id=1, source_target_pairs={{0,2},{1,3},{2,0},{3,1},{4,6},{5,7},{6,4},{7,5},{8,10},{9,11},{10,... | collective-permute-start | bytes 1572872 | tf_op jit(solution)/shard_map/ppermute | solution.py:374
  62.1 94.0 %collective-permute-start.38 = (bf16[256,1024]{1,0:T(8,128)(2,1)S(1)}, bf16[256,1024]{1,0:T(8,128)(2,1)}, u32[]{:S(2)}, u32[]{:S(2)}) collective-permute-start(bf16[256,1024]{1,0:T(8,128)(2,1)S(1)} %pad_maximum_fusion.8), channel_id=1, source_target_pairs={{0,6},{1,7},{2,4},{3,5},{4,2},{5,3},{6,0},{7,1},{8,14},{9,15},{10,... | collective-permute-start | bytes 1572872 | tf_op jit(solution)/shard_map/ppermute | solution.py:374
  65.6 15.1 %collective-permute-start.29 = (bf16[4,64,512]{2,1,0:T(8,128)(2,1)S(1)}, bf16[4,64,512]{2,1,0:T(8,128)(2,1)S(1)}, u32[]{:S(2)}, u32[]{:S(2)}) collective-permute-start(bf16[4,64,512]{2,1,0:T(8,128)(2,1)S(1)} %pad_maximum_fusion.9.refs_1_), channel_id=1, source_target_pairs={{0,16},{1,17},{2,18},{3,19},{4,20},{5,21},{6,22},{7,23},{8,24},{9,... | collective-permute-start | bytes 786440 | tf_op jit(solution)/shard_map/ppermute | solution.py:374
  67.2 13.5 %collective-permute-start.30 = (bf16[4,64,512]{2,1,0:T(8,128)(2,1)S(1)}, bf16[4,64,512]{2,1,0:T(8,128)(2,1)S(1)}, u32[]{:S(2)}, u32[]{:S(2)}) collective-permute-start(bf16[4,64,512]{2,1,0:T(8,128)(2,1)S(1)} %collective-permute-done.28.refs_2_), channel_id=1, source_target_pairs={{0,16},{1,17},{2,18},{3,19},{4,20},{5,21},{6,22},{7,23},{8,24},{9,... | collective-permute-start | bytes 786440 | tf_op jit(solution)/shard_map/ppermute | solution.py:374
  79.4 76.7 %collective-permute-start.37 = (bf16[256,1024]{1,0:T(8,128)(2,1)S(1)}, bf16[256,1024]{1,0:T(8,128)(2,1)}, u32[]{:S(2)}, u32[]{:S(2)}) collective-permute-start(bf16[256,1024]{1,0:T(8,128)(2,1)S(1)} %pad_maximum_fusion.8), channel_id=1, source_target_pairs={{0,4},{1,5},{2,6},{3,7},{4,0},{5,1},{6,2},{7,3},{8,12},{9,13},{10,... | collective-permute-start | bytes 1572872 | tf_op jit(solution)/shard_map/ppermute | solution.py:374
  88.4 16.7 %collective-permute-start.17 = (bf16[512,384]{1,0:T(8,128)(2,1)S(1)}, bf16[512,384]{1,0:T(8,128)(2,1)S(1)}, u32[]{:S(2)}, u32[]{:S(2)}) collective-permute-start(bf16[512,384]{1,0:T(8,128)(2,1)S(1)} %fusion.11), channel_id=1, source_target_pairs={{0,2},{1,3},{2,0},{3,1},{4,6},{5,7},{6,4},{7,5},{8,10},{9,11},{10,... | collective-permute-start | bytes 1179656 | tf_op jit(solution)/shard_map/ppermute | solution.py:374
  90.1 45.3 %collective-permute-start.18 = (bf16[512,384]{1,0:T(8,128)(2,1)S(1)}, bf16[512,384]{1,0:T(8,128)(2,1)}, u32[]{:S(2)}, u32[]{:S(2)}) collective-permute-start(bf16[512,384]{1,0:T(8,128)(2,1)S(1)} %fusion.12), channel_id=1, source_target_pairs={{0,4},{1,5},{2,6},{3,7},{4,0},{5,1},{6,2},{7,3},{8,12},{9,13},{10,... | collective-permute-start | bytes 1179656 | tf_op jit(solution)/shard_map/ppermute | solution.py:374
  92.9 42.5 %collective-permute-start.19 = (bf16[512,384]{1,0:T(8,128)(2,1)S(1)}, bf16[512,384]{1,0:T(8,128)(2,1)}, u32[]{:S(2)}, u32[]{:S(2)}) collective-permute-start(bf16[512,384]{1,0:T(8,128)(2,1)S(1)} %fusion.13), channel_id=1, source_target_pairs={{0,6},{1,7},{2,4},{3,5},{4,2},{5,3},{6,0},{7,1},{8,14},{9,15},{10,... | collective-permute-start | bytes 1179656 | tf_op jit(solution)/shard_map/ppermute | solution.py:374
  105.1 74.5 %collective-permute-start.34 = (bf16[2,256,1024]{2,1,0:T(8,128)(2,1)}, bf16[2,256,1024]{2,1,0:T(8,128)(2,1)}, u32[]{:S(2)}, u32[]{:S(2)}) collective-permute-start(bf16[2,256,1024]{2,1,0:T(8,128)(2,1)} %pad_maximum_fusion.3.refs_1_), channel_id=1, source_target_pairs={{0,8},{1,9},{2,10},{3,11},{4,12},{5,13},{6,14},{7,15},{8,0},{9,1},... | collective-permute-start | bytes 3145736 | tf_op jit(solution)/shard_map/ppermute | solution.py:374
  135.4 36.0 %collective-permute-start.31 = (bf16[512,512]{1,0:T(8,128)(2,1)}, bf16[512,512]{1,0:T(8,128)(2,1)}, u32[]{:S(2)}, u32[]{:S(2)}) collective-permute-start(bf16[512,512]{1,0:T(8,128)(2,1)} %bitcast.31), channel_id=1, source_target_pairs={{0,1},{1,0},{2,3},{3,2},{4,5},{5,4},{6,7},{7,6},{8,9},{9,8},{10,11... | collective-permute-start | bytes 1572872 | tf_op jit(solution)/shard_map/ppermute | solution.py:374
  147.2 14.1 %collective-permute-start.20 = (bf16[512,128]{1,0:T(8,128)(2,1)}, bf16[512,128]{1,0:T(8,128)(2,1)S(1)}, u32[]{:S(2)}, u32[]{:S(2)}) collective-permute-start(bf16[512,128]{1,0:T(8,128)(2,1)} %get-tuple-element.50), channel_id=1, source_target_pairs={{0,2},{1,3},{2,0},{3,1},{4,6},{5,7},{6,4},{7,5},{8,10},{9,11},{10,... | collective-permute-start | bytes 393224 | tf_op jit(solution)/shard_map/ppermute | solution.py:374
  158.4 26.4 %collective-permute-start.40 = (bf16[2,256,1024]{2,1,0:T(8,128)(2,1)}, bf16[2,256,1024]{2,1,0:T(8,128)(2,1)}, u32[]{:S(2)}, u32[]{:S(2)}) collective-permute-start(bf16[2,256,1024]{2,1,0:T(8,128)(2,1)} %pad_maximum_fusion.4.refs_5_), channel_id=1, source_target_pairs={{0,16},{1,17},{2,18},{3,19},{4,20},{5,21},{6,22},{7,23},{8,24},{9,... | collective-permute-start | bytes 3145736 | tf_op jit(solution)/shard_map/ppermute | solution.py:374
  176.9 30.4 %collective-permute-start.35 = (bf16[2,256,1024]{2,1,0:T(8,128)(2,1)}, bf16[2,256,1024]{2,1,0:T(8,128)(2,1)}, u32[]{:S(2)}, u32[]{:S(2)}) collective-permute-start(bf16[2,256,1024]{2,1,0:T(8,128)(2,1)} %pad_maximum_fusion.3.refs_1_), channel_id=1, source_target_pairs={{0,16},{1,17},{2,18},{3,19},{4,20},{5,21},{6,22},{7,23},{8,24},{9,... | collective-permute-start | bytes 3145736 | tf_op jit(solution)/shard_map/ppermute | solution.py:374
  177.7 29.6 %collective-permute-start.39 = (bf16[2,256,1024]{2,1,0:T(8,128)(2,1)}, bf16[2,256,1024]{2,1,0:T(8,128)(2,1)}, u32[]{:S(2)}, u32[]{:S(2)}) collective-permute-start(bf16[2,256,1024]{2,1,0:T(8,128)(2,1)} %pad_maximum_fusion.4.refs_5_), channel_id=1, source_target_pairs={{0,8},{1,9},{2,10},{3,11},{4,12},{5,13},{6,14},{7,15},{8,0},{9,1},... | collective-permute-start | bytes 3145736 | tf_op jit(solution)/shard_map/ppermute | solution.py:374
  179.6 48.9 %collective-permute-start.36 = (bf16[2,256,1024]{2,1,0:T(8,128)(2,1)}, bf16[2,256,1024]{2,1,0:T(8,128)(2,1)}, u32[]{:S(2)}, u32[]{:S(2)}) collective-permute-start(bf16[2,256,1024]{2,1,0:T(8,128)(2,1)} %collective-permute-done.34.refs_2_), channel_id=1, source_target_pairs={{0,16},{1,17},{2,18},{3,19},{4,20},{5,21},{6,22},{7,23},{8,24},{9,... | collective-permute-start | bytes 3145736 | tf_op jit(solution)/shard_map/ppermute | solution.py:374
  184.8 43.7 %collective-permute-start.41 = (bf16[2,256,1024]{2,1,0:T(8,128)(2,1)}, bf16[2,256,1024]{2,1,0:T(8,128)(2,1)}, u32[]{:S(2)}, u32[]{:S(2)}) collective-permute-start(bf16[2,256,1024]{2,1,0:T(8,128)(2,1)} %collective-permute-done.40.refs_7_), channel_id=1, source_target_pairs={{0,8},{1,9},{2,10},{3,11},{4,12},{5,13},{6,14},{7,15},{8,0},{9,1},... | collective-permute-start | bytes 3145736 | tf_op jit(solution)/shard_map/ppermute | solution.py:374
  263.0 12.7 %collective-permute-start.43 = (bf16[512,1024]{1,0:T(8,128)(2,1)S(1)}, bf16[512,1024]{1,0:T(8,128)(2,1)S(1)}, u32[]{:S(2)}, u32[]{:S(2)}) collective-permute-start(bf16[512,1024]{1,0:T(8,128)(2,1)S(1)} %pad_maximum_fusion.6), channel_id=1, source_target_pairs={{0,1},{1,0},{2,3},{3,2},{4,5},{5,4},{6,7},{7,6},{8,9},{9,8},{10,11... | collective-permute-start | bytes 3145736 | tf_op jit(solution)/shard_map/ppermute | solution.py:374
  269.8 107.4 %collective-permute-start.42 = (bf16[256,1024]{1,0:T(8,128)(2,1)}, bf16[256,1024]{1,0:T(8,128)(2,1)}, u32[]{:S(2)}, u32[]{:S(2)}) collective-permute-start(bf16[256,1024]{1,0:T(8,128)(2,1)} %slice.769), channel_id=1, source_target_pairs={{0,1},{1,0},{2,3},{3,2},{4,5},{5,4},{6,7},{7,6},{8,9},{9,8},{10,11... | collective-permute-start | bytes 1572872 | tf_op jit(solution)/shard_map/ppermute | solution.py:374
  283.4 12.9 %collective-permute-start.45 = (bf16[512,128]{1,0:T(8,128)(2,1)S(1)}, bf16[512,128]{1,0:T(8,128)(2,1)S(1)}, u32[]{:S(2)}, u32[]{:S(2)}) collective-permute-start(bf16[512,128]{1,0:T(8,128)(2,1)S(1)} %get-tuple-element.108), channel_id=1, source_target_pairs={{0,4},{1,5},{2,6},{3,7},{4,0},{5,1},{6,2},{7,3},{8,12},{9,13},{10,... | collective-permute-start | bytes 393224 | tf_op jit(solution)/shard_map/ppermute | solution.py:374
  317.6 19.0 %collective-permute-start.47 = (bf16[512,384]{1,0:T(8,128)(2,1)}, bf16[512,384]{1,0:T(8,128)(2,1)}, u32[]{:S(2)}, u32[]{:S(2)}) collective-permute-start(bf16[512,384]{1,0:T(8,128)(2,1)} %get-tuple-element.61), channel_id=1, source_target_pairs={{0,2},{1,3},{2,0},{3,1},{4,6},{5,7},{6,4},{7,5},{8,10},{9,11},{10,... | collective-permute-start | bytes 1179656 | tf_op jit(solution)/shard_map/ppermute | solution.py:374
  320.3 30.1 %collective-permute-start.48 = (bf16[512,384]{1,0:T(8,128)(2,1)}, bf16[512,384]{1,0:T(8,128)(2,1)}, u32[]{:S(2)}, u32[]{:S(2)}) collective-permute-start(bf16[512,384]{1,0:T(8,128)(2,1)} %get-tuple-element.62), channel_id=1, source_target_pairs={{0,4},{1,5},{2,6},{3,7},{4,0},{5,1},{6,2},{7,3},{8,12},{9,13},{10,... | collective-permute-start | bytes 1179656 | tf_op jit(solution)/shard_map/ppermute | solution.py:374
  323.4 28.8 %collective-permute-start.49 = (bf16[512,384]{1,0:T(8,128)(2,1)}, bf16[512,384]{1,0:T(8,128)(2,1)}, u32[]{:S(2)}, u32[]{:S(2)}) collective-permute-start(bf16[512,384]{1,0:T(8,128)(2,1)} %get-tuple-element.63), channel_id=1, source_target_pairs={{0,6},{1,7},{2,4},{3,5},{4,2},{5,3},{6,0},{7,1},{8,14},{9,15},{10,... | collective-permute-start | bytes 1179656 | tf_op jit(solution)/shard_map/ppermute | solution.py:374
  328.6 51.1 %collective-permute-start.59 = (bf16[512,512]{1,0:T(8,128)(2,1)}, bf16[512,512]{1,0:T(8,128)(2,1)}, u32[]{:S(2)}, u32[]{:S(2)}) collective-permute-start(bf16[512,512]{1,0:T(8,128)(2,1)} %get-tuple-element.98), channel_id=1, source_target_pairs={{0,1},{1,0},{2,3},{3,2},{4,5},{5,4},{6,7},{7,6},{8,9},{9,8},{10,11... | collective-permute-start | bytes 1572872 | tf_op jit(solution)/shard_map/ppermute | solution.py:374
  363.7 29.6 %collective-permute-start.50 = (bf16[256,1024]{1,0:T(8,128)(2,1)}, bf16[256,1024]{1,0:T(8,128)(2,1)S(1)}, u32[]{:S(2)}, u32[]{:S(2)}) collective-permute-start(bf16[256,1024]{1,0:T(8,128)(2,1)} %slice.768), channel_id=1, source_target_pairs={{0,1},{1,0},{2,3},{3,2},{4,5},{5,4},{6,7},{7,6},{8,9},{9,8},{10,11... | collective-permute-start | bytes 1572872 | tf_op jit(solution)/shard_map/ppermute | solution.py:374
  375.7 22.8 %collective-permute-start.54 = (bf16[4,72,1536]{2,1,0:T(8,128)(2,1)}, bf16[4,72,1536]{2,1,0:T(8,128)(2,1)}, u32[]{:S(2)}, u32[]{:S(2)}) collective-permute-start(bf16[4,72,1536]{2,1,0:T(8,128)(2,1)} %get-tuple-element.68), channel_id=1, source_target_pairs={{0,8},{1,9},{2,10},{3,11},{4,12},{5,13},{6,14},{7,15},{8,0},{9,1},... | collective-permute-start | bytes 2654216 | tf_op jit(solution)/shard_map/ppermute | solution.py:374
  390.7 110.1 %collective-permute-start.60 = (bf16[4,288,1024]{2,1,0:T(8,128)(2,1)}, bf16[4,288,1024]{2,1,0:T(8,128)(2,1)S(1)}, u32[]{:S(2)}, u32[]{:S(2)}) collective-permute-start(bf16[4,288,1024]{2,1,0:T(8,128)(2,1)} %get-tuple-element.70), channel_id=1, source_target_pairs={{0,16},{1,17},{2,18},{3,19},{4,20},{5,21},{6,22},{7,23},{8,24},{9,... | collective-permute-start | bytes 7077896 | tf_op jit(solution)/shard_map/ppermute | solution.py:374
  392.2 104.7 %collective-permute-start.63 = (bf16[4,288,1024]{2,1,0:T(8,128)(2,1)}, bf16[4,288,1024]{2,1,0:T(8,128)(2,1)S(1)}, u32[]{:S(2)}, u32[]{:S(2)}) collective-permute-start(bf16[4,288,1024]{2,1,0:T(8,128)(2,1)} %get-tuple-element.72), channel_id=1, source_target_pairs={{0,8},{1,9},{2,10},{3,11},{4,12},{5,13},{6,14},{7,15},{8,0},{9,1},... | collective-permute-start | bytes 7077896 | tf_op jit(solution)/shard_map/ppermute | solution.py:374
  392.8 71.2 %collective-permute-start.51 = (bf16[4,72,1536]{2,1,0:T(8,128)(2,1)}, bf16[4,72,1536]{2,1,0:T(8,128)(2,1)S(1)}, u32[]{:S(2)}, u32[]{:S(2)}) collective-permute-start(bf16[4,72,1536]{2,1,0:T(8,128)(2,1)} %get-tuple-element.66), channel_id=1, source_target_pairs={{0,16},{1,17},{2,18},{3,19},{4,20},{5,21},{6,22},{7,23},{8,24},{9,... | collective-permute-start | bytes 2654216 | tf_op jit(solution)/shard_map/ppermute | solution.py:374
  399.6 73.2 %collective-permute-start.55 = (bf16[2,72,1536]{2,1,0:T(8,128)(2,1)S(1)}, bf16[2,72,1536]{2,1,0:T(8,128)(2,1)S(1)}, u32[]{:S(2)}, u32[]{:S(2)}) collective-permute-start(bf16[2,72,1536]{2,1,0:T(8,128)(2,1)S(1)} %add_convert_fusion.6), channel_id=1, source_target_pairs={{0,16},{1,17},{2,18},{3,19},{4,20},{5,21},{6,22},{7,23},{8,24},{9,... | collective-permute-start | bytes 1327112 | tf_op jit(solution)/shard_map/ppermute | solution.py:374
  464.1 16.7 %collective-permute-start.52 = (bf16[2,72,1536]{2,1,0:T(8,128)(2,1)S(1)}, bf16[2,72,1536]{2,1,0:T(8,128)(2,1)S(1)}, u32[]{:S(2)}, u32[]{:S(2)}) collective-permute-start(bf16[2,72,1536]{2,1,0:T(8,128)(2,1)S(1)} %add_convert_fusion.7), channel_id=1, source_target_pairs={{0,8},{1,9},{2,10},{3,11},{4,12},{5,13},{6,14},{7,15},{8,0},{9,1},... | collective-permute-start | bytes 1327112 | tf_op jit(solution)/shard_map/ppermute | solution.py:374
  476.2 20.6 %collective-permute-start.56 = (bf16[72,1536]{1,0:T(8,128)(2,1)S(1)}, bf16[72,1536]{1,0:T(8,128)(2,1)S(1)}, u32[]{:S(2)}, u32[]{:S(2)}) collective-permute-start(bf16[72,1536]{1,0:T(8,128)(2,1)S(1)} %get-tuple-element.115), channel_id=1, source_target_pairs={{0,4},{1,5},{2,6},{3,7},{4,0},{5,1},{6,2},{7,3},{8,12},{9,13},{10,... | collective-permute-start | bytes 663560 | tf_op jit(solution)/shard_map/ppermute | solution.py:374
  481.0 15.8 %collective-permute-start.53 = (bf16[72,1536]{1,0:T(8,128)(2,1)S(1)}, bf16[72,1536]{1,0:T(8,128)(2,1)S(1)}, u32[]{:S(2)}, u32[]{:S(2)}) collective-permute-start(bf16[72,1536]{1,0:T(8,128)(2,1)S(1)} %fusion.33), channel_id=1, source_target_pairs={{0,2},{1,3},{2,0},{3,1},{4,6},{5,7},{6,4},{7,5},{8,10},{9,11},{10,... | collective-permute-start | bytes 663560 | tf_op jit(solution)/shard_map/ppermute | solution.py:374
  498.5 28.2 %collective-permute-start.64 = (bf16[2,288,1024]{2,1,0:T(8,128)(2,1)}, bf16[2,288,1024]{2,1,0:T(8,128)(2,1)}, u32[]{:S(2)}, u32[]{:S(2)}) collective-permute-start(bf16[2,288,1024]{2,1,0:T(8,128)(2,1)} %add_convert_fusion.1), channel_id=1, source_target_pairs={{0,16},{1,17},{2,18},{3,19},{4,20},{5,21},{6,22},{7,23},{8,24},{9,... | collective-permute-start | bytes 3538952 | tf_op jit(solution)/shard_map/ppermute | solution.py:374
  502.6 29.0 %collective-permute-start.61 = (bf16[2,288,1024]{2,1,0:T(8,128)(2,1)}, bf16[2,288,1024]{2,1,0:T(8,128)(2,1)}, u32[]{:S(2)}, u32[]{:S(2)}) collective-permute-start(bf16[2,288,1024]{2,1,0:T(8,128)(2,1)} %add_convert_fusion.2), channel_id=1, source_target_pairs={{0,8},{1,9},{2,10},{3,11},{4,12},{5,13},{6,14},{7,15},{8,0},{9,1},... | collective-permute-start | bytes 3538952 | tf_op jit(solution)/shard_map/ppermute | solution.py:374
  529.3 18.2 %collective-permute-start.66 = (bf16[288,1024]{1,0:T(8,128)(2,1)S(1)}, bf16[288,1024]{1,0:T(8,128)(2,1)S(1)}, u32[]{:S(2)}, u32[]{:S(2)}) collective-permute-start(bf16[288,1024]{1,0:T(8,128)(2,1)S(1)} %get-tuple-element.95), channel_id=1, source_target_pairs={{0,6},{1,7},{2,4},{3,5},{4,2},{5,3},{6,0},{7,1},{8,14},{9,15},{10,... | collective-permute-start | bytes 1769480 | tf_op jit(solution)/shard_map/ppermute | solution.py:374
  531.6 48.9 %collective-permute-start.65 = (bf16[288,1024]{1,0:T(8,128)(2,1)S(1)}, bf16[288,1024]{1,0:T(8,128)(2,1)S(1)}, u32[]{:S(2)}, u32[]{:S(2)}) collective-permute-start(bf16[288,1024]{1,0:T(8,128)(2,1)S(1)} %get-tuple-element.94), channel_id=1, source_target_pairs={{0,4},{1,5},{2,6},{3,7},{4,0},{5,1},{6,2},{7,3},{8,12},{9,13},{10,... | collective-permute-start | bytes 1769480 | tf_op jit(solution)/shard_map/ppermute | solution.py:374
  533.4 47.1 %collective-permute-start.62 = (bf16[288,1024]{1,0:T(8,128)(2,1)S(1)}, bf16[288,1024]{1,0:T(8,128)(2,1)S(1)}, u32[]{:S(2)}, u32[]{:S(2)}) collective-permute-start(bf16[288,1024]{1,0:T(8,128)(2,1)S(1)} %fusion.23), channel_id=1, source_target_pairs={{0,2},{1,3},{2,0},{3,1},{4,6},{5,7},{6,4},{7,5},{8,10},{9,11},{10,... | collective-permute-start | bytes 1769480 | tf_op jit(solution)/shard_map/ppermute | solution.py:374
  (113 other events, 1335.2 us)

commit v4 on v3

--- a/solution.py
+++ b/solution.py
@@ -425,36 +425,20 @@
     return lambda table: index
 
 
+def after(value, *others):
+    return lax.optimization_barrier((value, others))[0]
+
+
 def line_of(piece):
     return [piece] + [swapped(piece, bits) for bits in Z_BITS[1:]]
 
 
 def collected(line):
-    found = {}
-    for along in range(4):
-        first, second = (X_BIT, Y_BIT) if along < 2 else (Y_BIT, X_BIT)
-        found[0, along] = line[along]
-        found[first >> 3, along] = swapped(line[along], first)
-        found[second >> 3, along] = swapped(line[along], second)
-        found[3, along] = swapped(found[first >> 3, along], second)
-    arrays = [found[across, along][None] for across in range(4) for along in range(4)]
-    return arrays, [(at, 0) for at in range(16)]
-
-
-def collected_pairs(line):
-    near, far = jnp.stack(line[:2]), jnp.stack(line[2:])
-    near_x, far_y = swapped(near, X_BIT), swapped(far, Y_BIT)
-    arrays = [
-        near,
-        near_x,
-        swapped(near, Y_BIT),
-        swapped(near_x, Y_BIT),
-        far,
-        swapped(far, X_BIT),
-        far_y,
-        swapped(far_y, X_BIT),
-    ]
-    return arrays, [((at % 4 // 2) * 4 + at // 4, at % 2) for at in range(16)]
+    stacked = jnp.stack(line)
+    beside, above = swapped(stacked, X_BIT), swapped(stacked, Y_BIT)
+    arrays = [stacked, beside, above, swapped(beside[:2], Y_BIT), swapped(above[2:], X_BIT)]
+    held = [(at // 4, at % 4) for at in range(12)] + [(3, 0), (3, 1), (4, 0), (4, 1)]
+    return arrays, held
 
 
 def collected_small(line):
@@ -468,7 +452,7 @@
 GROUP_OF = {at: (group, place) for group, held in enumerate(GROUPS) for place, at in enumerate(held)}
 
 
-def summed(grouped):
+def summed_first(grouped):
     low, full = jnp.bfloat16, jnp.float32
     keep_a, send_a, keep_b, send_b = grouped
     got_a = swapped(send_a, Y_BIT)
@@ -477,11 +461,24 @@
     onward_b = (keep_b[2:].astype(full) + got_b[2:].astype(full)).astype(low)
     here_a = keep_a[:2].astype(full) + got_a[:2].astype(full)
     here_b = keep_b[:2].astype(full) + got_b[:2].astype(full)
+    return onward_a, onward_b, here_a, here_b
+
+
+def summed_second(state):
+    low, full = jnp.bfloat16, jnp.float32
+    onward_a, onward_b, here_a, here_b = state
     here_a = here_a + swapped(onward_a, X_BIT).astype(full)
     here_b = here_b + swapped(onward_b, Y_BIT).astype(full)
-    total = here_a[0]
-    for along, part in ((1, here_a[1]), (2, here_b[0]), (3, here_b[1])):
-        total = total + swapped(part.astype(low), Z_BITS[along]).astype(full)
+    return here_a[0], here_a[1].astype(low), here_b[0].astype(low), here_b[1].astype(low)
+
+
+def summed_third(state, *others):
+    got = [swapped(state[along], Z_BITS[along]) for along in (1, 2, 3)]
+    if others:
+        got = after(got, *others)
+    total = state[0]
+    for piece in got:
+        total = total + piece.astype(jnp.float32)
     return total
 
 
@@ -562,6 +559,11 @@
         in_specs=[pl.BlockSpec(memory_space=pltpu.SMEM)] + [vmem] * 4,
         out_specs=[vmem] * 7,
         scratch_shapes=[pltpu.VMEM((2, TILE, 2 * HD), jnp.float32)],
+        cost_estimate=pl.CostEstimate(
+            flops=12 * total_rows * total_rows * 2 * HD,
+            bytes_accessed=8 * total_rows * wide,
+            transcendentals=2 * total_rows * total_rows,
+        ),
         name="head_forward",
     )(places, *pieces)
 
@@ -681,6 +683,11 @@
             pltpu.VMEM((2, TILE, 2 * HD), jnp.float32),
             pltpu.VMEM((total_rows, wide), jnp.bfloat16),
         ],
+        cost_estimate=pl.CostEstimate(
+            flops=30 * total_rows * total_rows * 2 * HD,
+            bytes_accessed=8 * total_rows * wide,
+            transcendentals=2 * total_rows * total_rows,
+        ),
         name="head_backward",
     )(places, joint_sorted, mixed_sorted, totals_sorted, *pieces)
 
@@ -793,22 +800,34 @@
     joint_own = jnp.concatenate([chip_order(joint_mine, joint_got[:share]), small_pair])
     joint_line = line_of(joint_own)
     joint_arrays, joint_at = collected(joint_line)
+
+    expand_parts = expand_weight.reshape(share, 16, 2, 128)
+    expand_own = cores_exchanged(
+        (expand_parts[:, :, 0].reshape(share, units), expand_parts[:, :, 1].reshape(share, units))
+    )
+    mixer_own = cores_exchanged((mixer_weight[:, : D // 2], mixer_weight[:, D // 2 :]))
+    hidden_own = jnp.concatenate([expand_own[:, :D], expand_own[:, D:], reduce_weight])
+    mixer_line = line_of(after(mixer_own, *joint_line[1:]))
+    hidden_line = line_of(after(hidden_own, *mixer_line[1:]))
+    mixer_arrays, mixer_at = collected_small(after(mixer_line, *joint_arrays[1:3]))
+    token_rows = jnp.concatenate([tokens, pair_got[:own_rows]], axis=0).astype(full)
+    upstream = jnp.concatenate([cotangent[0], pair_got[own_rows:]], axis=0)
+    scaled_one, inverse_one = norm_parts(token_rows)
+    joint_arrays = after(joint_arrays, scaled_one)
     joint_plan = []
     for at, (array, entry) in enumerate(joint_at):
         for col in range(4):
             source_at = looked(entry, 64, 16 + col, 384)
-            joint_plan.append((array, source_at, col, slot(at)))
-            joint_plan.append((array, source_at, 4, slot_part(at, 0, 64, col * 384, 384)))
-        joint_plan.append((array, fixed(entry, pl.ds(64, 8), pl.ds(0, 768)), 5, slot(at)))
+            joint_plan.append((array, source_at, 0, slot_part(at, 0, 64, col * 384, 384)))
+        joint_plan.append((array, fixed(entry, pl.ds(64, 8), pl.ds(0, 768)), 1, slot(at)))
     joint_done = moved(
         table,
         joint_arrays,
         joint_plan,
-        [(16, 64, 384)] * 4 + [(16, 64, 1536), (16, 8, 768)],
-    )
-    joint_columns = [part.reshape(D, 384) for part in joint_done[:4]]
-    joint_full = joint_done[4].reshape(D, 1536)
-    small_all = joint_done[5][:, 0].reshape(32, 384)
+        [(16, 64, 1536), (16, 8, 768)],
+    )
+    joint_full = joint_done[0].reshape(D, 1536)
+    small_all = joint_done[1][:, 0].reshape(32, 384)
     count = share
     rows_of = small_all[:, : 8 * count].reshape(32, 8, count).transpose(1, 0, 2).reshape(8, 32 * count)
     (
@@ -824,15 +843,25 @@
     expand_shift = small_all[:, 8 * count :].reshape(16, 2, 128)
     expand_shift = jnp.where(even, expand_shift[:, 0], expand_shift[:, 1]).reshape(-1)
 
-    expand_parts = expand_weight.reshape(share, 16, 2, 128)
-    expand_own = cores_exchanged(
-        (expand_parts[:, :, 0].reshape(share, units), expand_parts[:, :, 1].reshape(share, units))
-    )
-    mixer_own = cores_exchanged((mixer_weight[:, : D // 2], mixer_weight[:, D // 2 :]))
-    hidden_own = jnp.concatenate([expand_own[:, :D], expand_own[:, D:], reduce_weight])
-    mixer_own, hidden_own, _ = lax.optimization_barrier((mixer_own, hidden_own, joint_line[1:]))
-    mixer_arrays, mixer_at = collected_small(line_of(mixer_own))
-    hidden_arrays, hidden_at = collected_pairs(line_of(hidden_own))
+    normed = (scaled_one * gain_one + shift_one).astype(low)
+    halves_of = [
+        jnp.where(even, item[: D // 2], item[D // 2 :]).reshape(4, 1, 128)
+        for item in (query_shift, value_shift)
+    ]
+    joint_shift = by_depth(jnp.concatenate([halves_of[0], jnp.zeros_like(halves_of[0]), halves_of[1]], axis=1))
+    joint_rows = (product(normed, joint_full) + joint_shift.reshape(1536)).astype(low)
+    hidden_line = after(hidden_line, joint_rows)
+    joint_rows = after(joint_rows, hidden_line[3], mixer_arrays)
+    hidden_arrays, hidden_at = collected(hidden_line)
+    head_pieces = [joint_rows[:, at * 384 : (at + 1) * 384] for at in range(4)]
+    head_pieces = [head_pieces[0]] + [swapped(head_pieces[at], Z_BITS[at]) for at in (1, 2, 3)]
+    hidden_plan = []
+    for at, (array, entry) in enumerate(hidden_at):
+        hidden_plan.append((array, fixed(entry, pl.ds(0, 64)), 0, slot_part(at, 0, 64, 0, D)))
+        hidden_plan.append((array, fixed(entry, pl.ds(64, 64)), 0, slot_part(at, 0, 64, D, D)))
+        hidden_plan.append((array, fixed(entry, pl.ds(128, 128)), 1, slot(at)))
+    expand_full, reduce_full = moved(table, hidden_arrays, hidden_plan, [(16, 64, units), (16, 128, D)])
+    expand_full, reduce_full = expand_full.reshape(D, units), reduce_full.reshape(units, D)
     mixer_cols = moved(
         table,
         mixer_arrays,
@@ -845,28 +874,9 @@
         jnp.concatenate([mixer_mine, mixer_theirs], axis=1),
         jnp.concatenate([mixer_theirs, mixer_mine], axis=1),
     )
-    hidden_plan = []
-    for at, (array, entry) in enumerate(hidden_at):
-        hidden_plan.append((array, fixed(entry, pl.ds(0, 64)), 0, slot_part(at, 0, 64, 0, D)))
-        hidden_plan.append((array, fixed(entry, pl.ds(64, 64)), 0, slot_part(at, 0, 64, D, D)))
-        hidden_plan.append((array, fixed(entry, pl.ds(128, 128)), 1, slot(at)))
-    expand_full, reduce_full = moved(table, hidden_arrays, hidden_plan, [(16, 64, units), (16, 128, D)])
-    expand_full, reduce_full = expand_full.reshape(D, units), reduce_full.reshape(units, D)
-
-    token_rows = jnp.concatenate([tokens, pair_got[:own_rows]], axis=0).astype(full)
-    upstream = jnp.concatenate([cotangent[0], pair_got[own_rows:]], axis=0)
-    scaled_one, inverse_one = norm_parts(token_rows)
-    normed = (scaled_one * gain_one + shift_one).astype(low)
-    halves_of = [
-        jnp.where(even, item[: D // 2], item[D // 2 :]).reshape(4, 1, 128)
-        for item in (query_shift, value_shift)
-    ]
-    joint_shift = by_depth(jnp.concatenate([halves_of[0], jnp.zeros_like(halves_of[0]), halves_of[1]], axis=1))
-    joint_shift = joint_shift.reshape(4, 384)
-    head_pieces = [(product(normed, joint_columns[at]) + joint_shift[at]).astype(low) for at in range(4)]
-    head_pieces = [head_pieces[0]] + [swapped(head_pieces[at], Z_BITS[at]) for at in (1, 2, 3)]
     forward = head_forward(head_pieces, places)
     mixed_out, (joint_sorted, mixed_sorted, totals_sorted) = forward[:4], forward[4:]
+    mixed_out = after(mixed_out, hidden_arrays[1], hidden_arrays[2])
     mixed_rows = jnp.concatenate(
         [mixed_out[0]] + [swapped(mixed_out[at], Z_BITS[at]) for at in (1, 2, 3)], axis=1
     )
@@ -901,6 +911,7 @@
     mixer_keep = jnp.where(even, mixer_gradient[:, : D // 2], mixer_gradient[:, D // 2 :])
     mixer_send = jnp.where(even, mixer_gradient[:, D // 2 :], mixer_gradient[:, : D // 2])
     mixer_got = swapped(mixer_send, CORE_BIT)
+    mixer_whole = jnp.concatenate([mixer_keep, mixer_got], axis=0).reshape(16, 64, D // 2)
     hidden_plan = []
     for at in range(16):
         to, place = GROUP_OF[at]
@@ -908,22 +919,18 @@
         hidden_plan.append((0, slot_part(at, 0, 64, D, D), to, fixed(place, pl.ds(64, 64))))
         hidden_plan.append((1, slot(at), to, fixed(place, pl.ds(128, 128))))
         for half in range(2):
-            hidden_plan.append(
-                (
-                    2,
-                    slot_rows(20 + at, half * 32, 32),
-                    to,
-                    fixed(place, pl.ds(256, 32), pl.ds(half * (D // 2), D // 2)),
-                )
-            )
-    mixer_whole = jnp.concatenate([mixer_keep, mixer_got], axis=0).reshape(16, 64, D // 2)
-    hidden_sum = summed(
-        moved(table, (expand_gradient, reduce_gradient, mixer_whole), hidden_plan, [(4, 288, D)] * 4)
-    )
+            left = fixed(place, pl.ds(256, 32), pl.ds(half * (D // 2), D // 2))
+            hidden_plan.append((2, slot_rows(20 + at, half * 32, 32), to, left))
+    grouped = moved(
+        table, (expand_gradient, reduce_gradient, mixer_whole), hidden_plan, [(4, 288, D)] * 4
+    )
+    hidden_state = summed_first(grouped)
+    grad_pieces = after(grad_pieces, grouped)
     grad_out = head_backward(joint_sorted, mixed_sorted, totals_sorted, grad_pieces, places)
-    grad_joint = jnp.concatenate(
-        [grad_out[0]] + [swapped(grad_out[at], Z_BITS[at]) for at in (1, 2, 3)], axis=1
-    )
+    grad_got = [swapped(grad_out[at], Z_BITS[at]) for at in (1, 2, 3)]
+    grad_got = after(grad_got, hidden_state)
+    hidden_state = summed_second(hidden_state)
+    grad_joint = jnp.concatenate([grad_out[0]] + grad_got, axis=1)
     joint_gradient = inner_rows(normed, grad_joint).astype(low).reshape(16, 64, 1536)
     grad_normed_part = inner_cols(grad_joint, joint_full)
     joint_sums = by_depth(jnp.sum(grad_joint.astype(full), axis=0).reshape(4, 3, 128))
@@ -956,6 +963,7 @@
     sums = sums.astype(low).reshape(8, 32, count).transpose(1, 0, 2).reshape(32, 8 * count)
     sums = jnp.concatenate([sums, expand_rows.astype(low)], axis=1).reshape(16, 1, 768)
     sums = jnp.pad(sums, ((0, 0), (0, 7), (0, 0)))
+    joint_gradient = after(joint_gradient, hidden_state)
     joint_plan = []
     for at in range(16):
         to, place = GROUP_OF[at]
@@ -963,7 +971,11 @@
             left = looked(place, 64, 16 + col, 384)
             joint_plan.append((0, slot_part(at, 0, 64, col * 384, 384), to, left))
         joint_plan.append((1, slot(at), to, fixed(place, pl.ds(64, 8), pl.ds(0, 768))))
-    joint_sum = summed(moved(table, (joint_gradient, sums), joint_plan, [(4, 72, 1536)] * 4))
+    joint_state = summed_second(
+        summed_first(moved(table, (joint_gradient, sums), joint_plan, [(4, 72, 1536)] * 4))
+    )
+    hidden_sum = summed_third(hidden_state, joint_state)
+    joint_sum = summed_third(joint_state)
     grad_normed = own_sum(grad_normed_part)
     input_gradient = (
         grad_middle[:own_rows]

time: 594 us -> 495 us (0.83)
  waiting for transfers between devices: 284 us -> 206 us
  matrix products: 56.9 us -> 41.2 us
    ppermute x69 -> x59, waiting for transfers between devices: 284 us -> 206 us  [swapped(): lax.ppermute(value, ALL, [(source, source ^ mask) for source in range(cou...]
    dot_general x4, matrix products: 25.8 us -> 12.9 us  [inner_cols(): lax.dot_general(left, right, (((1,), (1,)), ((), ())), preferred_element_...]
    concatenate x1, local copies, waits for them, and re-layouts: 0.1 us -> 6.09 us  [chip_body(): jnp.concatenate([jnp.concatenate([first_gain, first_shift, query_bias, va...]
    unnamed x196 -> x114, local copies, waits for them, and re-layouts: 12.4 us -> 8.43 us
    dot_general x7 -> x4, matrix products: 15.2 us -> 12.5 us  [product(): return jnp.dot(left, right, preferred_element_type=jnp.float32)]
    ppermute x69 -> x59, starting transfers between devices: 92.4 us -> 94.3 us  [swapped(): lax.ppermute(value, ALL, [(source, source ^ mask) for source in range(cou...]
  transfers between devices with their start and end apart: 69 -> 59, of which waited for: 29 -> 25; matrix products, arithmetic and copies ran while one was open for 18% -> 19% of each run, Pallas kernels for 10% -> 11%
where the time goes in v4:
time: 495 us; the launch traced here: 486 us
  waiting for transfers between devices  206 us (42%)
  starting transfers between devices  94.3 us (19%)
  Pallas kernels  62 us (13%)
  local copies, waits for them, and re-layouts  41.4 us (8%)
  matrix products  41.2 us (8%)
  other arithmetic  40.1 us (8%)
    ppermute x59, waiting for transfers between devices, swapped(): lax.ppermute(value, ALL, [(source, source ^ mask) for source in range(cou...  206 us
    ppermute x59, starting transfers between devices, swapped(): lax.ppermute(value, ALL, [(source, source ^ mask) for source in range(cou...  94.3 us
    pallas_call x5, Pallas kernels, moved(): pl.pallas_call(lambda *refs: moved_kernel(*refs, plan=plan, source_count=...  29.9 us
    pallas_call x1, Pallas kernels, head_backward(): pl.pallas_call(head_backward_kernel, out_shape=[jax.ShapeDtypeStruct((row...  20.5 us
    dot_general x4, matrix products, inner_rows(): lax.dot_general(left, right, (((0,), (0,)), ((), ())), preferred_element_...  15.7 us
    dot_general x4, matrix products, inner_cols(): lax.dot_general(left, right, (((1,), (1,)), ((), ())), preferred_element_...  12.9 us
    dot_general x4, matrix products, product(): return jnp.dot(left, right, preferred_element_type=jnp.float32)  12.5 us
    pallas_call x1, Pallas kernels, head_forward(): pl.pallas_call(head_forward_kernel, out_shape=[jax.ShapeDtypeStruct((rows...  11.6 us
  transfers between devices with their start and end apart: 59, of which 25 were waited for; matrix products, arithmetic and copies ran while one was open for 19% of the time, Pallas kernels for 11%

profile of v4, /device:TPU:0, one launch (start us, length us, event | category | flops | bytes accessed | tf_op | source)
XLA Modules:
  0.0 486.5 jit_solution(2623505817196137360)
XLA Ops:
  2.0 6.1 %concatenate.119 = bf16[384]{0:T(512)(128)(2,1)S(1)} concatenate(bf16[32]{0:T(256)(128)(2,1)} %param.18, bf16[32]{0:T(256)(128)(2,1)} %param.19, bf16[32]{0:T(256)(128)(2,1)} %param.21, bf16[32]{0:T(256)(128)(2,1)} %param.22, bf16[32]{0:T(256)(128)(2,1)} %param.24, bf16[32]{0:T(256)(128)(2,1)} %param.25, bf16[32]{0:T(256)(128)(2,1)} %param.26, bf16[32]{0:T(256)(128)(2,1)} %param.30, ...), dimensions={0} | concatenate | bytes 1536 | tf_op jit(solution)/shard_map/concatenate | solution.py:769
  12.9 4.1 collective-permute-start.3
  18.7 9.9 %collective-permute-done.3 = bf16[72,1536]{1,0:T(8,128)(2,1)S(1)} collective-permute-done((bf16[72,1536]{1,0:T(8,128)(2,1)S(1)}, bf16[72,1536]{1,0:T(8,128)(2,1)S(1)}, u32[]{:S(2)}, u32[]{:S(2)}) %collective-permute-start.3) | collective-permute-done | bytes 221216 | tf_op jit(solution)/shard_map/ppermute | solution.py:374
  28.5 4.8 collective-permute-done.4
  39.1 4.5 collective-permute-start.12
  43.5 3.6 collective-permute-start.11
  49.4 3.6 collective-permute-start.16
  60.3 4.7 collective-permute-done.8.refs_5_
  67.5 5.0 %moved.5 = (bf16[16,64,1536]{2,1,0:T(8,128)(2,1)}, bf16[16,8,768]{2,1,0:T(8,128)(2,1)}) custom-call(s32[36]{0:T(128)} %pad_add_fusion.refs_0_, bf16[4,72,1536]{2,1,0:T(8,128)(2,1)} %copy-done.13, bf16[4,72,1536]{2,1,0:T(8,128)(2,1)} %copy-done.21, bf16[4,72,1536]{2,1,0:T(8,128)(2,1)} %copy-done.20, bf16[2,72,1536]{2,1,0:T(8,128)(2,1)} %copy-done.28, ...), custom_call_target="tpu_custom_call" | custom-call | tf_op jit(solution)/shard_map/moved/pallas_call | solution.py:393
  74.6 3.8 fusion.7
  78.4 17.7 %collective-permute-done.15 = bf16[256,1024]{1,0:T(8,128)(2,1)} collective-permute-done((bf16[256,1024]{1,0:T(8,128)(2,1)}, bf16[256,1024]{1,0:T(8,128)(2,1)}, u32[]{:S(2)}, u32[]{:S(2)}) %collective-permute-start.15) | collective-permute-done | bytes 524320 | tf_op jit(solution)/shard_map/ppermute | solution.py:374
  96.2 3.1 pad_maximum_fusion.refs_1_
  103.4 47.9 %collective-permute-done.17.refs_2_ = bf16[4,64,512]{2,1,0:T(8,128)(2,1)S(1)} collective-permute-done((bf16[4,64,512]{2,1,0:T(8,128)(2,1)S(1)}, bf16[4,64,512]{2,1,0:T(8,128)(2,1)S(1)}, u32[]{:S(2)}, u32[]{:S(2)}) %collective-permute-start.17) | collective-permute-done | bytes 262176 | tf_op jit(solution)/shard_map/ppermute | solution.py:374
  153.8 4.0 collective-permute-done.19.refs_4_
  158.8 3.9 collective-permute-start.22
  164.5 3.0 moved.6
  169.7 3.5 collective-permute-done.22.refs_3_
  173.2 20.4 %collective-permute-done.21.refs_2_ = bf16[512,384]{1,0:T(8,128)(2,1)} collective-permute-done((bf16[512,384]{1,0:T(8,128)(2,1)S(1)}, bf16[512,384]{1,0:T(8,128)(2,1)}, u32[]{:S(2)}, u32[]{:S(2)}) %collective-permute-start.21) | collective-permute-done | bytes 393248 | tf_op jit(solution)/shard_map/ppermute | solution.py:374
  193.7 11.6 %head_forward.1 = (bf16[512,128]{1,0:T(8,128)(2,1)}, bf16[512,128]{1,0:T(8,128)(2,1)}, bf16[512,128]{1,0:T(8,128)(2,1)}, bf16[512,128]{1,0:T(8,128)(2,1)}, bf16[...) custom-call(s32[16]{0:T(128)} %gather_fusion, bf16[512,384]{1,0:T(8,128)(2,1)} %get-tuple-element.141.refs_0_, ...), custom_call_target="tpu_custom_call" | custom-call | flops 6442450944 | bytes 6291456 | tf_op jit(solution)/shard_map/head_forward/pallas_call | solution.py:551
  213.9 2.7 collective-permute-start.27
  216.7 6.5 %collective-permute-done.26 = bf16[512,128]{1,0:T(8,128)(2,1)S(1)} collective-permute-done((bf16[512,128]{1,0:T(8,128)(2,1)S(1)}, bf16[512,128]{1,0:T(8,128)(2,1)S(1)}, u32[]{:S(2)}, u32[]{:S(2)}) %collective-permute-start.26) | collective-permute-done | bytes 131104 | tf_op jit(solution)/shard_map/ppermute | solution.py:374
  223.3 3.5 fusion.72
  228.6 2.8 collective-permute-done.31.refs_5_
  233.9 7.8 %moved.7 = (bf16[16,64,2048]{2,1,0:T(8,128)(2,1)}, bf16[16,128,1024]{2,1,0:T(8,128)(2,1)}) custom-call(s32[36]{0:T(128)} %pad_add_fusion.refs_0_, bf16[4,256,1024]{2,1,0:T(8,128)(2,1)} %pad_maximum_fusion.refs_1_, bf16[4,256,1024]{2,1,0:T(8,128)(2,1)} %collective-permute-done.23.refs_2_, bf16[4,256,1024]{2,1,0:T(8,128)(2,1)} %collective-permute-done.24.refs_3_, ...), custom_call_target="tpu_custom_call" | custom-call | tf_op jit(solution)/shard_map/moved/pallas_call | solution.py:393
  244.8 2.7 copy-done.44
  249.8 2.9 fusion.54
  252.7 6.1 %convert_reduce_fusion = (f32[2048]{0:T(1024)S(1)}, bf16[512,2048]{1,0:T(8,128)(2,1)S(1)}) fusion(f32[512,2048]{1,0:T(8,128)S(1)} %fusion.22, f32[2048]{0:T(1024)S(1)} %bitcast.176, bf16[2048,1024]{1,0:T(8,128)(2,1)S(1)} %bitcast.184, bf16[256,1024]{1,0:T(8,128)(2,1)S(1)} %get-tuple-element.152, bf16[256,1024]{1,0:T(8,128)(2,1)S(1)} %bitcast.146), kind=kOutput, calls=%fused_computation.10 | convolution fusion | flops 2173696000 | bytes 11550720 | tf_op jit(solution)/shard_map/dot_general | solution.py:45
  262.0 4.5 convolution_convert_fusion.2
  266.5 5.3 %convolution_convert_fusion.1 = bf16[2048,1024]{1,0:T(8,128)(2,1)} fusion(bf16[256,1024]{1,0:T(8,128)(2,1)S(1)} %get-tuple-element.152, bf16[256,1024]{1,0:T(8,128)(2,1)S(1)} %bitcast.147, f32[512,2048]{1,0:T(8,128)S(1)} %fusion.22, f32[2048]{0:T(1024)S(1)} %bitcast.177), kind=kOutput, calls=%fused_computation.13 | convolution fusion | flops 2162163712 | bytes 9445376 | tf_op jit(solution)/shard_map/dot_general | solution.py:39
  281.8 8.7 %moved.8 = (bf16[4,288,1024]{2,1,0:T(8,128)(2,1)}, bf16[4,288,1024]{2,1,0:T(8,128)(2,1)}, bf16[4,288,1024]{2,1,0:T(8,128)(2,1)}, bf16[4,288,1024]{2,1,0:T(8,128)(2,1)}) custom-call(s32[36]{0:T(128)} %pad_add_fusion.refs_0_, bf16[16,64,2048]{2,1,0:T(8,128)(2,1)} %bitcast.149, bf16[16,128,1024]{2,1,0:T(8,128)(2,1)} %bitcast.150, bf16[16,64,512]{2,1,0:T(8,128)(2,1)} %bitcast.151), custom_call_target="tpu_custom_call" | custom-call | tf_op jit(solution)/shard_map/moved/pallas_call | solution.py:393
  305.1 6.6 %collective-permute-done.35.refs_2_ = bf16[512,128]{1,0:T(8,128)(2,1)} collective-permute-done((bf16[512,128]{1,0:T(8,128)(2,1)S(1)}, bf16[512,128]{1,0:T(8,128)(2,1)}, u32[]{:S(2)}, u32[]{:S(2)}) %collective-permute-start.35) | collective-permute-done | bytes 131104 | tf_op jit(solution)/shard_map/ppermute | solution.py:374
  311.7 20.5 %head_backward.1 = (bf16[512,384]{1,0:T(8,128)(2,1)}, bf16[512,384]{1,0:T(8,128)(2,1)}, bf16[512,384]{1,0:T(8,128)(2,1)}, bf16[512,384]{1,0:T(8,128)(2,1)}) custom-call(s32[16]{0:T(128)} %gather_fusion, bf16[2048,384]{1,0:T(8,128)(2,1)} %get-tuple-element.97.joint_ref, f32[2048,128]{1,0:T(8,128)} %get-tuple-element.98.mixed_ref, ...), custom_call_target="tpu_custom_call" | custom-call | flops 16106127360 | bytes 6291456 | tf_op jit(solution)/shard_map/head_backward/pallas_call | solution.py:673
  337.8 6.6 %collective-permute-done.41 = bf16[4,288,1024]{2,1,0:T(8,128)(2,1)} collective-permute-done((bf16[4,288,1024]{2,1,0:T(8,128)(2,1)}, bf16[4,288,1024]{2,1,0:T(8,128)(2,1)}, u32[]{:S(2)}, u32[]{:S(2)}) %collective-permute-start.41) | collective-permute-done | bytes 2359328 | tf_op jit(solution)/shard_map/ppermute | solution.py:374
  344.5 3.2 add_convert_fusion.2
  349.1 2.8 add_convert_fusion.1
  351.9 10.3 %collective-permute-done.39 = bf16[512,384]{1,0:T(8,128)(2,1)S(1)} collective-permute-done((bf16[512,384]{1,0:T(8,128)(2,1)}, bf16[512,384]{1,0:T(8,128)(2,1)S(1)}, u32[]{:S(2)}, u32[]{:S(2)}) %collective-permute-start.39) | collective-permute-done | bytes 393248 | tf_op jit(solution)/shard_map/ppermute | solution.py:374
  368.0 5.2 %convolution_convert_fusion = bf16[1024,1536]{1,0:T(8,128)(2,1)} fusion(bf16[512,1536]{1,0:T(8,128)(2,1)} %copy-done.15, f32[1024]{0:T(1024)S(1)} %copy-done.43, f32[1024]{0:T(1024)S(1)} %reshape.570, f32[512]{0:T(512)S(1)} %copy-done.41, f32[512]{0:T(512)S(1)} %broadcast_multiply_fusion.3, bf16[256,1024]{1,0:T(8,128)(2,1)S(1)} %get-tuple-element.153, ...), kind=kOutput, calls=%fused_computation.12 | convolution fusion | flops 1616904192 | bytes 5779456 | tf_op jit(solution)/shard_map/dot_general | solution.py:39
  377.8 12.1 %collective-permute-done.45 = bf16[2,288,1024]{2,1,0:T(8,128)(2,1)} collective-permute-done((bf16[2,288,1024]{2,1,0:T(8,128)(2,1)}, bf16[2,288,1024]{2,1,0:T(8,128)(2,1)}, u32[]{:S(2)}, u32[]{:S(2)}) %collective-permute-start.45) | collective-permute-done | bytes 1179680 | tf_op jit(solution)/shard_map/ppermute | solution.py:374
  393.3 5.3 %moved.9 = (bf16[4,72,1536]{2,1,0:T(8,128)(2,1)}, bf16[4,72,1536]{2,1,0:T(8,128)(2,1)}, bf16[4,72,1536]{2,1,0:T(8,128)(2,1)}, bf16[4,72,1536]{2,1,0:T(8,128)(2,1)}) custom-call(s32[36]{0:T(128)} %pad_add_fusion.refs_0_, bf16[16,64,1536]{2,1,0:T(8,128)(2,1)} %bitcast.152, bf16[16,8,768]{2,1,0:T(8,128)(2,1)} %pad.15.refs_2_), custom_call_target="tpu_custom_call" | custom-call | tf_op jit(solution)/shard_map/moved/pallas_call | solution.py:393
  402.0 2.7 fusion.19
  404.6 8.9 %collective-permute-start.54 = (bf16[288,1024]{1,0:T(8,128)(2,1)S(1)}, bf16[288,1024]{1,0:T(8,128)(2,1)S(1)}, u32[]{:S(2)}, u32[]{:S(2)}) collective-permute-start(bf16[288,1024]{1,0:T(8,128)(2,1)S(1)} %fusion.17), channel_id=1, source_target_pairs={{0,2},{1,3},{2,0},{3,1},{4,6},{5,7},{6,4},{7,5},{8,10},{9,11},{10,... | collective-permute-start | bytes 1769480 | tf_op jit(solution)/shard_map/ppermute | solution.py:374
  417.6 4.5 collective-permute-done.49
  423.1 5.2 %collective-permute-done.47 = bf16[2,72,1536]{2,1,0:T(8,128)(2,1)S(1)} collective-permute-done((bf16[2,72,1536]{2,1,0:T(8,128)(2,1)S(1)}, bf16[2,72,1536]{2,1,0:T(8,128)(2,1)S(1)}, u32[]{:S(2)}, u32[]{:S(2)}) %collective-permute-start.47) | collective-permute-done | bytes 442400 | tf_op jit(solution)/shard_map/ppermute | solution.py:374
  428.5 10.6 %collective-permute-start.48 = (bf16[72,1536]{1,0:T(8,128)(2,1)S(1)}, bf16[72,1536]{1,0:T(8,128)(2,1)S(1)}, u32[]{:S(2)}, u32[]{:S(2)}) collective-permute-start(bf16[72,1536]{1,0:T(8,128)(2,1)S(1)} %fusion.24), channel_id=1, source_target_pairs={{0,2},{1,3},{2,0},{3,1},{4,6},{5,7},{6,4},{7,5},{8,10},{9,11},{10,... | collective-permute-start | bytes 663560 | tf_op jit(solution)/shard_map/ppermute | solution.py:374
  439.3 3.5 collective-permute-done.56
  442.8 20.4 %collective-permute-done.55 = bf16[288,1024]{1,0:T(8,128)(2,1)S(1)} collective-permute-done((bf16[288,1024]{1,0:T(8,128)(2,1)S(1)}, bf16[288,1024]{1,0:T(8,128)(2,1)S(1)}, u32[]{:S(2)}, u32[]{:S(2)}) %collective-permute-start.55) | collective-permute-done | bytes 589856 | tf_op jit(solution)/shard_map/ppermute | solution.py:374
  464.4 10.2 %collective-permute-start.52 = (bf16[72,1536]{1,0:T(8,128)(2,1)S(1)}, bf16[72,1536]{1,0:T(8,128)(2,1)S(1)}, u32[]{:S(2)}, u32[]{:S(2)}) collective-permute-start(bf16[72,1536]{1,0:T(8,128)(2,1)S(1)} %get-tuple-element.167), channel_id=1, source_target_pairs={{0,6},{1,7},{2,4},{3,5},{4,2},{5,3},{6,0},{7,1},{8,14},{9,15},{10,... | collective-permute-start | bytes 663560 | tf_op jit(solution)/shard_map/ppermute | solution.py:374
  475.3 5.7 %collective-permute-done.52 = bf16[72,1536]{1,0:T(8,128)(2,1)S(1)} collective-permute-done((bf16[72,1536]{1,0:T(8,128)(2,1)S(1)}, bf16[72,1536]{1,0:T(8,128)(2,1)S(1)}, u32[]{:S(2)}, u32[]{:S(2)}) %collective-permute-start.52) | collective-permute-done | bytes 221216 | tf_op jit(solution)/shard_map/ppermute | solution.py:374
  (371 shorter events, 121.6 us)
Async XLA Ops:
  1.5 11.3 %collective-permute-start.10 = (bf16[32,512]{1,0:T(8,128)(2,1)S(1)}, bf16[32,512]{1,0:T(8,128)(2,1)S(1)}, u32[]{:S(2)}, u32[]{:S(2)}) collective-permute-start(bf16[32,512]{1,0:T(8,128)(2,1)S(1)} %get-tuple-element.187), channel_id=1, source_target_pairs={{0,1},{1,0},{2,3},{3,2},{4,5},{5,4},{6,7},{7,6},{8,9},{9,8},{10,11... | collective-permute-start | bytes 98312 | tf_op jit(solution)/shard_map/ppermute | solution.py:374
  11.9 42.1 %collective-permute-start = (bf16[512,1024]{1,0:T(8,128)(2,1)}, bf16[512,1024]{1,0:T(8,128)(2,1)}, u32[]{:S(2)}, u32[]{:S(2)}) collective-permute-start(bf16[512,1024]{1,0:T(8,128)(2,1)} %pad_maximum_fusion.1), channel_id=1, source_target_pairs={{0,1},{1,0},{2,3},{3,2},{4,5},{5,4},{6,7},{7,6},{8,9},{9,8},{10,11... | collective-permute-start | bytes 3145736 | tf_op jit(solution)/shard_map/ppermute | solution.py:374
  12.9 15.6 %collective-permute-start.3 = (bf16[72,1536]{1,0:T(8,128)(2,1)S(1)}, bf16[72,1536]{1,0:T(8,128)(2,1)S(1)}, u32[]{:S(2)}, u32[]{:S(2)}) collective-permute-start(bf16[72,1536]{1,0:T(8,128)(2,1)S(1)} %get-tuple-element.175), channel_id=1, source_target_pairs={{0,4},{1,5},{2,6},{3,7},{4,0},{5,1},{6,2},{7,3},{8,12},{9,13},{10,... | collective-permute-start | bytes 663560 | tf_op jit(solution)/shard_map/ppermute | solution.py:374
  17.0 11.5 %collective-permute-start.2 = (bf16[72,1536]{1,0:T(8,128)(2,1)S(1)}, bf16[72,1536]{1,0:T(8,128)(2,1)S(1)}, u32[]{:S(2)}, u32[]{:S(2)}) collective-permute-start(bf16[72,1536]{1,0:T(8,128)(2,1)S(1)} %get-tuple-element.175), channel_id=1, source_target_pairs={{0,2},{1,3},{2,0},{3,1},{4,6},{5,7},{6,4},{7,5},{8,10},{9,11},{10,... | collective-permute-start | bytes 663560 | tf_op jit(solution)/shard_map/ppermute | solution.py:374
  18.6 14.7 %collective-permute-start.4 = (bf16[72,1536]{1,0:T(8,128)(2,1)S(1)}, bf16[72,1536]{1,0:T(8,128)(2,1)S(1)}, u32[]{:S(2)}, u32[]{:S(2)}) collective-permute-start(bf16[72,1536]{1,0:T(8,128)(2,1)S(1)} %get-tuple-element.175), channel_id=1, source_target_pairs={{0,6},{1,7},{2,4},{3,5},{4,2},{5,3},{6,0},{7,1},{8,14},{9,15},{10,... | collective-permute-start | bytes 663560 | tf_op jit(solution)/shard_map/ppermute | solution.py:374
  33.5 23.0 %collective-permute-start.6 = (bf16[4,72,1536]{2,1,0:T(8,128)(2,1)S(1)}, bf16[4,72,1536]{2,1,0:T(8,128)(2,1)S(1)}, u32[]{:S(2)}, u32[]{:S(2)}) collective-permute-start(bf16[4,72,1536]{2,1,0:T(8,128)(2,1)S(1)} %pad_maximum_fusion.7.refs_1_), channel_id=1, source_target_pairs={{0,16},{1,17},{2,18},{3,19},{4,20},{5,21},{6,22},{7,23},{8,24},{9,... | collective-permute-start | bytes 2654216 | tf_op jit(solution)/shard_map/ppermute | solution.py:374
  35.1 21.8 %collective-permute-start.5 = (bf16[4,72,1536]{2,1,0:T(8,128)(2,1)S(1)}, bf16[4,72,1536]{2,1,0:T(8,128)(2,1)S(1)}, u32[]{:S(2)}, u32[]{:S(2)}) collective-permute-start(bf16[4,72,1536]{2,1,0:T(8,128)(2,1)S(1)} %pad_maximum_fusion.7.refs_1_), channel_id=1, source_target_pairs={{0,8},{1,9},{2,10},{3,11},{4,12},{5,13},{6,14},{7,15},{8,0},{9,1},... | collective-permute-start | bytes 2654216 | tf_op jit(solution)/shard_map/ppermute | solution.py:374
  39.1 8.9 %collective-permute-start.12 = (bf16[64,512]{1,0:T(8,128)(2,1)S(1)}, bf16[64,512]{1,0:T(8,128)(2,1)S(1)}, u32[]{:S(2)}, u32[]{:S(2)}) collective-permute-start(bf16[64,512]{1,0:T(8,128)(2,1)S(1)} %maximum_select_fusion.8), channel_id=1, source_target_pairs={{0,4},{1,5},{2,6},{3,7},{4,0},{5,1},{6,2},{7,3},{8,12},{9,13},{10,... | collective-permute-start | bytes 196616 | tf_op jit(solution)/shard_map/ppermute | solution.py:374
  49.4 29.1 %collective-permute-start.16 = (bf16[256,1024]{1,0:T(8,128)(2,1)}, bf16[256,1024]{1,0:T(8,128)(2,1)}, u32[]{:S(2)}, u32[]{:S(2)}) collective-permute-start(bf16[256,1024]{1,0:T(8,128)(2,1)} %pad_maximum_fusion.8), channel_id=1, source_target_pairs={{0,6},{1,7},{2,4},{3,5},{4,2},{5,3},{6,0},{7,1},{8,14},{9,15},{10,... | collective-permute-start | bytes 1572872 | tf_op jit(solution)/shard_map/ppermute | solution.py:374
  52.9 43.2 %collective-permute-start.15 = (bf16[256,1024]{1,0:T(8,128)(2,1)}, bf16[256,1024]{1,0:T(8,128)(2,1)}, u32[]{:S(2)}, u32[]{:S(2)}) collective-permute-start(bf16[256,1024]{1,0:T(8,128)(2,1)} %pad_maximum_fusion.8), channel_id=1, source_target_pairs={{0,4},{1,5},{2,6},{3,7},{4,0},{5,1},{6,2},{7,3},{8,12},{9,13},{10,... | collective-permute-start | bytes 1572872 | tf_op jit(solution)/shard_map/ppermute | solution.py:374
  54.0 42.2 %collective-permute-start.14 = (bf16[256,1024]{1,0:T(8,128)(2,1)}, bf16[256,1024]{1,0:T(8,128)(2,1)}, u32[]{:S(2)}, u32[]{:S(2)}) collective-permute-start(bf16[256,1024]{1,0:T(8,128)(2,1)} %pad_maximum_fusion.8), channel_id=1, source_target_pairs={{0,2},{1,3},{2,0},{3,1},{4,6},{5,7},{6,4},{7,5},{8,10},{9,11},{10,... | collective-permute-start | bytes 1572872 | tf_op jit(solution)/shard_map/ppermute | solution.py:374
  56.5 8.4 %collective-permute-start.8 = (bf16[2,72,1536]{2,1,0:T(8,128)(2,1)S(1)}, bf16[2,72,1536]{2,1,0:T(8,128)(2,1)S(1)}, u32[]{:S(2)}, u32[]{:S(2)}) collective-permute-start(bf16[2,72,1536]{2,1,0:T(8,128)(2,1)S(1)} %slice.541), channel_id=1, source_target_pairs={{0,8},{1,9},{2,10},{3,11},{4,12},{5,13},{6,14},{7,15},{8,0},{9,1},... | collective-permute-start | bytes 1327112 | tf_op jit(solution)/shard_map/ppermute | solution.py:374
  99.3 106.0 %collective-permute-start.24 = (bf16[4,256,1024]{2,1,0:T(8,128)(2,1)}, bf16[4,256,1024]{2,1,0:T(8,128)(2,1)}, u32[]{:S(2)}, u32[]{:S(2)}) collective-permute-start(bf16[4,256,1024]{2,1,0:T(8,128)(2,1)} %pad_maximum_fusion.refs_1_), channel_id=1, source_target_pairs={{0,16},{1,17},{2,18},{3,19},{4,20},{5,21},{6,22},{7,23},{8,24},{9,... | collective-permute-start | bytes 6291464 | tf_op jit(solution)/shard_map/ppermute | solution.py:374
  99.3 105.9 %collective-permute-start.23 = (bf16[4,256,1024]{2,1,0:T(8,128)(2,1)}, bf16[4,256,1024]{2,1,0:T(8,128)(2,1)}, u32[]{:S(2)}, u32[]{:S(2)}) collective-permute-start(bf16[4,256,1024]{2,1,0:T(8,128)(2,1)} %pad_maximum_fusion.refs_1_), channel_id=1, source_target_pairs={{0,8},{1,9},{2,10},{3,11},{4,12},{5,13},{6,14},{7,15},{8,0},{9,1},... | collective-permute-start | bytes 6291464 | tf_op jit(solution)/shard_map/ppermute | solution.py:374
  99.7 51.6 %collective-permute-start.17 = (bf16[4,64,512]{2,1,0:T(8,128)(2,1)S(1)}, bf16[4,64,512]{2,1,0:T(8,128)(2,1)S(1)}, u32[]{:S(2)}, u32[]{:S(2)}) collective-permute-start(bf16[4,64,512]{2,1,0:T(8,128)(2,1)S(1)} %pad_maximum_fusion.9.refs_1_), channel_id=1, source_target_pairs={{0,8},{1,9},{2,10},{3,11},{4,12},{5,13},{6,14},{7,15},{8,0},{9,1},... | collective-permute-start | bytes 786440 | tf_op jit(solution)/shard_map/ppermute | solution.py:374
  101.5 51.6 %collective-permute-start.18 = (bf16[4,64,512]{2,1,0:T(8,128)(2,1)S(1)}, bf16[4,64,512]{2,1,0:T(8,128)(2,1)S(1)}, u32[]{:S(2)}, u32[]{:S(2)}) collective-permute-start(bf16[4,64,512]{2,1,0:T(8,128)(2,1)S(1)} %pad_maximum_fusion.9.refs_1_), channel_id=1, source_target_pairs={{0,16},{1,17},{2,18},{3,19},{4,20},{5,21},{6,22},{7,23},{8,24},{9,... | collective-permute-start | bytes 786440 | tf_op jit(solution)/shard_map/ppermute | solution.py:374
  158.8 14.4 %collective-permute-start.22 = (bf16[512,384]{1,0:T(8,128)(2,1)}, bf16[512,384]{1,0:T(8,128)(2,1)}, u32[]{:S(2)}, u32[]{:S(2)}) collective-permute-start(bf16[512,384]{1,0:T(8,128)(2,1)} %get-tuple-element.138), channel_id=1, source_target_pairs={{0,6},{1,7},{2,4},{3,5},{4,2},{5,3},{6,0},{7,1},{8,14},{9,15},{10,... | collective-permute-start | bytes 1179656 | tf_op jit(solution)/shard_map/ppermute | solution.py:374
  162.8 30.9 %collective-permute-start.21 = (bf16[512,384]{1,0:T(8,128)(2,1)S(1)}, bf16[512,384]{1,0:T(8,128)(2,1)}, u32[]{:S(2)}, u32[]{:S(2)}) collective-permute-start(bf16[512,384]{1,0:T(8,128)(2,1)S(1)} %get-tuple-element.139), channel_id=1, source_target_pairs={{0,4},{1,5},{2,6},{3,7},{4,0},{5,1},{6,2},{7,3},{8,12},{9,13},{10,... | collective-permute-start | bytes 1179656 | tf_op jit(solution)/shard_map/ppermute | solution.py:374
  162.8 30.9 %collective-permute-start.20 = (bf16[512,384]{1,0:T(8,128)(2,1)S(1)}, bf16[512,384]{1,0:T(8,128)(2,1)}, u32[]{:S(2)}, u32[]{:S(2)}) collective-permute-start(bf16[512,384]{1,0:T(8,128)(2,1)S(1)} %get-tuple-element.140), channel_id=1, source_target_pairs={{0,2},{1,3},{2,0},{3,1},{4,6},{5,7},{6,4},{7,5},{8,10},{9,11},{10,... | collective-permute-start | bytes 1179656 | tf_op jit(solution)/shard_map/ppermute | solution.py:374
  173.2 50.0 %collective-permute-start.28 = (bf16[512,512]{1,0:T(8,128)(2,1)}, bf16[512,512]{1,0:T(8,128)(2,1)}, u32[]{:S(2)}, u32[]{:S(2)}) collective-permute-start(bf16[512,512]{1,0:T(8,128)(2,1)} %bitcast.20), channel_id=1, source_target_pairs={{0,1},{1,0},{2,3},{3,2},{4,5},{5,4},{6,7},{7,6},{8,9},{9,8},{10,11... | collective-permute-start | bytes 1572872 | tf_op jit(solution)/shard_map/ppermute | solution.py:374
  205.3 8.6 %collective-permute-start.25 = (bf16[512,128]{1,0:T(8,128)(2,1)}, bf16[512,128]{1,0:T(8,128)(2,1)S(1)}, u32[]{:S(2)}, u32[]{:S(2)}) collective-permute-start(bf16[512,128]{1,0:T(8,128)(2,1)} %get-tuple-element.92), channel_id=1, source_target_pairs={{0,2},{1,3},{2,0},{3,1},{4,6},{5,7},{6,4},{7,5},{8,10},{9,11},{10,... | collective-permute-start | bytes 393224 | tf_op jit(solution)/shard_map/ppermute | solution.py:374
  207.7 23.7 %collective-permute-start.31 = (bf16[2,256,1024]{2,1,0:T(8,128)(2,1)}, bf16[2,256,1024]{2,1,0:T(8,128)(2,1)}, u32[]{:S(2)}, u32[]{:S(2)}) collective-permute-start(bf16[2,256,1024]{2,1,0:T(8,128)(2,1)} %slice.564), channel_id=1, source_target_pairs={{0,8},{1,9},{2,10},{3,11},{4,12},{5,13},{6,14},{7,15},{8,0},{9,1},... | collective-permute-start | bytes 3145736 | tf_op jit(solution)/shard_map/ppermute | solution.py:374
  210.5 23.4 %collective-permute-start.30 = (bf16[2,256,1024]{2,1,0:T(8,128)(2,1)}, bf16[2,256,1024]{2,1,0:T(8,128)(2,1)}, u32[]{:S(2)}, u32[]{:S(2)}) collective-permute-start(bf16[2,256,1024]{2,1,0:T(8,128)(2,1)} %slice.563), channel_id=1, source_target_pairs={{0,16},{1,17},{2,18},{3,19},{4,20},{5,21},{6,22},{7,23},{8,24},{9,... | collective-permute-start | bytes 3145736 | tf_op jit(solution)/shard_map/ppermute | solution.py:374
  212.2 10.9 %collective-permute-start.26 = (bf16[512,128]{1,0:T(8,128)(2,1)S(1)}, bf16[512,128]{1,0:T(8,128)(2,1)S(1)}, u32[]{:S(2)}, u32[]{:S(2)}) collective-permute-start(bf16[512,128]{1,0:T(8,128)(2,1)S(1)} %copy-done.48), channel_id=1, source_target_pairs={{0,4},{1,5},{2,6},{3,7},{4,0},{5,1},{6,2},{7,3},{8,12},{9,13},{10,... | collective-permute-start | bytes 393224 | tf_op jit(solution)/shard_map/ppermute | solution.py:374
  213.9 9.3 %collective-permute-start.27 = (bf16[512,128]{1,0:T(8,128)(2,1)S(1)}, bf16[512,128]{1,0:T(8,128)(2,1)S(1)}, u32[]{:S(2)}, u32[]{:S(2)}) collective-permute-start(bf16[512,128]{1,0:T(8,128)(2,1)S(1)} %copy-done.47), channel_id=1, source_target_pairs={{0,6},{1,7},{2,4},{3,5},{4,2},{5,3},{6,0},{7,1},{8,14},{9,15},{10,... | collective-permute-start | bytes 393224 | tf_op jit(solution)/shard_map/ppermute | solution.py:374
  227.9 13.9 %collective-permute-start.29 = (bf16[512,1024]{1,0:T(8,128)(2,1)}, bf16[512,1024]{1,0:T(8,128)(2,1)}, u32[]{:S(2)}, u32[]{:S(2)}) collective-permute-start(bf16[512,1024]{1,0:T(8,128)(2,1)} %pad_maximum_fusion.3), channel_id=1, source_target_pairs={{0,1},{1,0},{2,3},{3,2},{4,5},{5,4},{6,7},{7,6},{8,9},{9,8},{10,11... | collective-permute-start | bytes 3145736 | tf_op jit(solution)/shard_map/ppermute | solution.py:374
  261.3 16.4 %collective-permute-start.32 = (bf16[256,1024]{1,0:T(8,128)(2,1)S(1)}, bf16[256,1024]{1,0:T(8,128)(2,1)S(1)}, u32[]{:S(2)}, u32[]{:S(2)}) collective-permute-start(bf16[256,1024]{1,0:T(8,128)(2,1)S(1)} %slice.769), channel_id=1, source_target_pairs={{0,1},{1,0},{2,3},{3,2},{4,5},{5,4},{6,7},{7,6},{8,9},{9,8},{10,11... | collective-permute-start | bytes 1572872 | tf_op jit(solution)/shard_map/ppermute | solution.py:374
  261.5 10.4 %collective-permute-start.33 = (bf16[512,1024]{1,0:T(8,128)(2,1)S(1)}, bf16[512,1024]{1,0:T(8,128)(2,1)S(1)}, u32[]{:S(2)}, u32[]{:S(2)}) collective-permute-start(bf16[512,1024]{1,0:T(8,128)(2,1)S(1)} %pad_maximum_fusion.5), channel_id=1, source_target_pairs={{0,1},{1,0},{2,3},{3,2},{4,5},{5,4},{6,7},{7,6},{8,9},{9,8},{10,11... | collective-permute-start | bytes 3145736 | tf_op jit(solution)/shard_map/ppermute | solution.py:374
  290.4 54.0 %collective-permute-start.41 = (bf16[4,288,1024]{2,1,0:T(8,128)(2,1)}, bf16[4,288,1024]{2,1,0:T(8,128)(2,1)}, u32[]{:S(2)}, u32[]{:S(2)}) collective-permute-start(bf16[4,288,1024]{2,1,0:T(8,128)(2,1)} %get-tuple-element.101), channel_id=1, source_target_pairs={{0,16},{1,17},{2,18},{3,19},{4,20},{5,21},{6,22},{7,23},{8,24},{9,... | collective-permute-start | bytes 7077896 | tf_op jit(solution)/shard_map/ppermute | solution.py:374
  294.8 54.3 %collective-permute-start.42 = (bf16[4,288,1024]{2,1,0:T(8,128)(2,1)}, bf16[4,288,1024]{2,1,0:T(8,128)(2,1)}, u32[]{:S(2)}, u32[]{:S(2)}) collective-permute-start(bf16[4,288,1024]{2,1,0:T(8,128)(2,1)} %get-tuple-element.103), channel_id=1, source_target_pairs={{0,8},{1,9},{2,10},{3,11},{4,12},{5,13},{6,14},{7,15},{8,0},{9,1},... | collective-permute-start | bytes 7077896 | tf_op jit(solution)/shard_map/ppermute | solution.py:374
  297.3 14.4 %collective-permute-start.35 = (bf16[512,128]{1,0:T(8,128)(2,1)S(1)}, bf16[512,128]{1,0:T(8,128)(2,1)}, u32[]{:S(2)}, u32[]{:S(2)}) collective-permute-start(bf16[512,128]{1,0:T(8,128)(2,1)S(1)} %get-tuple-element.159), channel_id=1, source_target_pairs={{0,4},{1,5},{2,6},{3,7},{4,0},{5,1},{6,2},{7,3},{8,12},{9,13},{10,... | collective-permute-start | bytes 393224 | tf_op jit(solution)/shard_map/ppermute | solution.py:374
  299.9 11.8 %collective-permute-start.34 = (bf16[512,128]{1,0:T(8,128)(2,1)S(1)}, bf16[512,128]{1,0:T(8,128)(2,1)}, u32[]{:S(2)}, u32[]{:S(2)}) collective-permute-start(bf16[512,128]{1,0:T(8,128)(2,1)S(1)} %get-tuple-element.160), channel_id=1, source_target_pairs={{0,2},{1,3},{2,0},{3,1},{4,6},{5,7},{6,4},{7,5},{8,10},{9,11},{10,... | collective-permute-start | bytes 393224 | tf_op jit(solution)/shard_map/ppermute | solution.py:374
  332.3 19.7 %collective-permute-start.38 = (bf16[512,384]{1,0:T(8,128)(2,1)}, bf16[512,384]{1,0:T(8,128)(2,1)S(1)}, u32[]{:S(2)}, u32[]{:S(2)}) collective-permute-start(bf16[512,384]{1,0:T(8,128)(2,1)} %get-tuple-element.109), channel_id=1, source_target_pairs={{0,2},{1,3},{2,0},{3,1},{4,6},{5,7},{6,4},{7,5},{8,10},{9,11},{10,... | collective-permute-start | bytes 1179656 | tf_op jit(solution)/shard_map/ppermute | solution.py:374
  332.3 30.0 %collective-permute-start.39 = (bf16[512,384]{1,0:T(8,128)(2,1)}, bf16[512,384]{1,0:T(8,128)(2,1)S(1)}, u32[]{:S(2)}, u32[]{:S(2)}) collective-permute-start(bf16[512,384]{1,0:T(8,128)(2,1)} %get-tuple-element.110), channel_id=1, source_target_pairs={{0,4},{1,5},{2,6},{3,7},{4,0},{5,1},{6,2},{7,3},{8,12},{9,13},{10,... | collective-permute-start | bytes 1179656 | tf_op jit(solution)/shard_map/ppermute | solution.py:374
  334.0 28.3 %collective-permute-start.40 = (bf16[512,384]{1,0:T(8,128)(2,1)}, bf16[512,384]{1,0:T(8,128)(2,1)S(1)}, u32[]{:S(2)}, u32[]{:S(2)}) collective-permute-start(bf16[512,384]{1,0:T(8,128)(2,1)} %get-tuple-element.111), channel_id=1, source_target_pairs={{0,6},{1,7},{2,4},{3,5},{4,2},{5,3},{6,0},{7,1},{8,14},{9,15},{10,... | collective-permute-start | bytes 1179656 | tf_op jit(solution)/shard_map/ppermute | solution.py:374
  347.6 27.9 %collective-permute-start.44 = (bf16[2,288,1024]{2,1,0:T(8,128)(2,1)}, bf16[2,288,1024]{2,1,0:T(8,128)(2,1)}, u32[]{:S(2)}, u32[]{:S(2)}) collective-permute-start(bf16[2,288,1024]{2,1,0:T(8,128)(2,1)} %add_convert_fusion.2), channel_id=1, source_target_pairs={{0,8},{1,9},{2,10},{3,11},{4,12},{5,13},{6,14},{7,15},{8,0},{9,1},... | collective-permute-start | bytes 3538952 | tf_op jit(solution)/shard_map/ppermute | solution.py:374
  364.8 25.2 %collective-permute-start.45 = (bf16[2,288,1024]{2,1,0:T(8,128)(2,1)}, bf16[2,288,1024]{2,1,0:T(8,128)(2,1)}, u32[]{:S(2)}, u32[]{:S(2)}) collective-permute-start(bf16[2,288,1024]{2,1,0:T(8,128)(2,1)} %add_convert_fusion.1), channel_id=1, source_target_pairs={{0,16},{1,17},{2,18},{3,19},{4,20},{5,21},{6,22},{7,23},{8,24},{9,... | collective-permute-start | bytes 3538952 | tf_op jit(solution)/shard_map/ppermute | solution.py:374
  368.0 31.6 %collective-permute-start.43 = (bf16[256,1024]{1,0:T(8,128)(2,1)}, bf16[256,1024]{1,0:T(8,128)(2,1)}, u32[]{:S(2)}, u32[]{:S(2)}) collective-permute-start(bf16[256,1024]{1,0:T(8,128)(2,1)} %slice.768), channel_id=1, source_target_pairs={{0,1},{1,0},{2,3},{3,2},{4,5},{5,4},{6,7},{7,6},{8,9},{9,8},{10,11... | collective-permute-start | bytes 1572872 | tf_op jit(solution)/shard_map/ppermute | solution.py:374
  398.6 17.8 %collective-permute-start.46 = (bf16[4,72,1536]{2,1,0:T(8,128)(2,1)}, bf16[4,72,1536]{2,1,0:T(8,128)(2,1)S(1)}, u32[]{:S(2)}, u32[]{:S(2)}) collective-permute-start(bf16[4,72,1536]{2,1,0:T(8,128)(2,1)} %get-tuple-element.117), channel_id=1, source_target_pairs={{0,16},{1,17},{2,18},{3,19},{4,20},{5,21},{6,22},{7,23},{8,24},{9,... | collective-permute-start | bytes 2654216 | tf_op jit(solution)/shard_map/ppermute | solution.py:374
  401.2 20.8 %collective-permute-start.49 = (bf16[4,72,1536]{2,1,0:T(8,128)(2,1)}, bf16[4,72,1536]{2,1,0:T(8,128)(2,1)S(1)}, u32[]{:S(2)}, u32[]{:S(2)}) collective-permute-start(bf16[4,72,1536]{2,1,0:T(8,128)(2,1)} %get-tuple-element.119), channel_id=1, source_target_pairs={{0,8},{1,9},{2,10},{3,11},{4,12},{5,13},{6,14},{7,15},{8,0},{9,1},... | collective-permute-start | bytes 2654216 | tf_op jit(solution)/shard_map/ppermute | solution.py:374
  404.6 34.6 %collective-permute-start.54 = (bf16[288,1024]{1,0:T(8,128)(2,1)S(1)}, bf16[288,1024]{1,0:T(8,128)(2,1)S(1)}, u32[]{:S(2)}, u32[]{:S(2)}) collective-permute-start(bf16[288,1024]{1,0:T(8,128)(2,1)S(1)} %fusion.17), channel_id=1, source_target_pairs={{0,2},{1,3},{2,0},{3,1},{4,6},{5,7},{6,4},{7,5},{8,10},{9,11},{10,... | collective-permute-start | bytes 1769480 | tf_op jit(solution)/shard_map/ppermute | solution.py:374
  413.5 29.2 %collective-permute-start.56 = (bf16[288,1024]{1,0:T(8,128)(2,1)S(1)}, bf16[288,1024]{1,0:T(8,128)(2,1)S(1)}, u32[]{:S(2)}, u32[]{:S(2)}) collective-permute-start(bf16[288,1024]{1,0:T(8,128)(2,1)S(1)} %copy-done.25), channel_id=1, source_target_pairs={{0,6},{1,7},{2,4},{3,5},{4,2},{5,3},{6,0},{7,1},{8,14},{9,15},{10,... | collective-permute-start | bytes 1769480 | tf_op jit(solution)/shard_map/ppermute | solution.py:374
  415.8 47.4 %collective-permute-start.55 = (bf16[288,1024]{1,0:T(8,128)(2,1)S(1)}, bf16[288,1024]{1,0:T(8,128)(2,1)S(1)}, u32[]{:S(2)}, u32[]{:S(2)}) collective-permute-start(bf16[288,1024]{1,0:T(8,128)(2,1)S(1)} %get-tuple-element.147), channel_id=1, source_target_pairs={{0,4},{1,5},{2,6},{3,7},{4,0},{5,1},{6,2},{7,3},{8,12},{9,13},{10,... | collective-permute-start | bytes 1769480 | tf_op jit(solution)/shard_map/ppermute | solution.py:374
  416.6 11.7 %collective-permute-start.47 = (bf16[2,72,1536]{2,1,0:T(8,128)(2,1)S(1)}, bf16[2,72,1536]{2,1,0:T(8,128)(2,1)S(1)}, u32[]{:S(2)}, u32[]{:S(2)}) collective-permute-start(bf16[2,72,1536]{2,1,0:T(8,128)(2,1)S(1)} %add_convert_fusion.7), channel_id=1, source_target_pairs={{0,8},{1,9},{2,10},{3,11},{4,12},{5,13},{6,14},{7,15},{8,0},{9,1},... | collective-permute-start | bytes 1327112 | tf_op jit(solution)/shard_map/ppermute | solution.py:374
  422.2 16.9 %collective-permute-start.50 = (bf16[2,72,1536]{2,1,0:T(8,128)(2,1)S(1)}, bf16[2,72,1536]{2,1,0:T(8,128)(2,1)S(1)}, u32[]{:S(2)}, u32[]{:S(2)}) collective-permute-start(bf16[2,72,1536]{2,1,0:T(8,128)(2,1)S(1)} %add_convert_fusion.6), channel_id=1, source_target_pairs={{0,16},{1,17},{2,18},{3,19},{4,20},{5,21},{6,22},{7,23},{8,24},{9,... | collective-permute-start | bytes 1327112 | tf_op jit(solution)/shard_map/ppermute | solution.py:374
  428.5 46.9 %collective-permute-start.48 = (bf16[72,1536]{1,0:T(8,128)(2,1)S(1)}, bf16[72,1536]{1,0:T(8,128)(2,1)S(1)}, u32[]{:S(2)}, u32[]{:S(2)}) collective-permute-start(bf16[72,1536]{1,0:T(8,128)(2,1)S(1)} %fusion.24), channel_id=1, source_target_pairs={{0,2},{1,3},{2,0},{3,1},{4,6},{5,7},{6,4},{7,5},{8,10},{9,11},{10,... | collective-permute-start | bytes 663560 | tf_op jit(solution)/shard_map/ppermute | solution.py:374
  464.4 10.9 %collective-permute-start.51 = (bf16[72,1536]{1,0:T(8,128)(2,1)S(1)}, bf16[72,1536]{1,0:T(8,128)(2,1)S(1)}, u32[]{:S(2)}, u32[]{:S(2)}) collective-permute-start(bf16[72,1536]{1,0:T(8,128)(2,1)S(1)} %get-tuple-element.166), channel_id=1, source_target_pairs={{0,4},{1,5},{2,6},{3,7},{4,0},{5,1},{6,2},{7,3},{8,12},{9,13},{10,... | collective-permute-start | bytes 663560 | tf_op jit(solution)/shard_map/ppermute | solution.py:374
  464.4 16.5 %collective-permute-start.52 = (bf16[72,1536]{1,0:T(8,128)(2,1)S(1)}, bf16[72,1536]{1,0:T(8,128)(2,1)S(1)}, u32[]{:S(2)}, u32[]{:S(2)}) collective-permute-start(bf16[72,1536]{1,0:T(8,128)(2,1)S(1)} %get-tuple-element.167), channel_id=1, source_target_pairs={{0,6},{1,7},{2,4},{3,5},{4,2},{5,3},{6,0},{7,1},{8,14},{9,15},{10,... | collective-permute-start | bytes 663560 | tf_op jit(solution)/shard_map/ppermute | solution.py:374
  (61 other events, 1093.1 us)

commit v5 on v4

--- a/solution.py
+++ b/solution.py
@@ -1,3 +1,5 @@
+import math
+
 import jax
 import jax.numpy as jnp
 from jax import lax
@@ -397,6 +399,9 @@
         + [pl.BlockSpec(memory_space=pl.ANY)] * len(sources),
         out_specs=[pl.BlockSpec(memory_space=pltpu.VMEM)] * len(shapes),
         scratch_shapes=[pltpu.SemaphoreType.DMA((len(plan),))],
+        cost_estimate=pl.CostEstimate(
+            flops=0, bytes_accessed=6 * sum(math.prod(shape) for shape in shapes), transcendentals=0
+        ),
         name="moved",
     )(table, *sources)
 
@@ -766,23 +771,21 @@
     pair_got = swapped(pair, CORE_BIT)
 
     units = expand_weight.shape[1] // 2
-    small = jnp.concatenate(
-        [
-            jnp.concatenate(
-                [
-                    first_gain,
-                    first_shift,
-                    query_bias,
-                    value_bias,
-                    mixer_bias,
-                    second_gain,
-                    second_shift,
-                    reduce_bias,
-                ]
-            ),
-            expand_bias,
-        ]
-    ).reshape(1, 384)
+    small, left = jnp.zeros((384,), low), 0
+    for item in (
+        first_gain,
+        first_shift,
+        query_bias,
+        value_bias,
+        mixer_bias,
+        second_gain,
+        second_shift,
+        reduce_bias,
+        expand_bias,
+    ):
+        small = small + jnp.pad(item, (left, 384 - left - item.shape[0]))
+        left += item.shape[0]
+    small = small.reshape(1, 384)
     joint_parts = joint_weight.reshape(share, 3, 2, 4, 128).transpose(2, 0, 3, 1, 4).reshape(2, share, 1536)
     small_rows = jnp.pad(small, ((0, 7), (0, 1536 - 384)))
     joint_mine = jnp.where(even, joint_parts[0], joint_parts[1])
@@ -849,9 +852,9 @@
         for item in (query_shift, value_shift)
     ]
     joint_shift = by_depth(jnp.concatenate([halves_of[0], jnp.zeros_like(halves_of[0]), halves_of[1]], axis=1))
+    normed = after(normed, mixer_arrays[1], mixer_arrays[2])
     joint_rows = (product(normed, joint_full) + joint_shift.reshape(1536)).astype(low)
-    hidden_line = after(hidden_line, joint_rows)
-    joint_rows = after(joint_rows, hidden_line[3], mixer_arrays)
+    hidden_line = after(hidden_line, joint_rows, mixer_arrays)
     hidden_arrays, hidden_at = collected(hidden_line)
     head_pieces = [joint_rows[:, at * 384 : (at + 1) * 384] for at in range(4)]
     head_pieces = [head_pieces[0]] + [swapped(head_pieces[at], Z_BITS[at]) for at in (1, 2, 3)]
@@ -894,7 +897,6 @@
     before = product(second, expand_full) + expand_shift
     active, gelu_pull = jax.vjp(gelu_tanh, before)
     active = active.astype(low)
-    result = middle[:own_rows] + (own_sum(product(active, reduce_full)) + reduce_shift)
 
     reduce_gradient = inner_rows(active, upstream).astype(low).reshape(16, 128, D)
     grad_before = gelu_pull(inner_cols(upstream, reduce_full))[0].astype(low)
@@ -904,8 +906,8 @@
     upstream_full = upstream.astype(full)
     grad_middle = upstream_full + norm_pull(grad_second, scaled_two, inverse_two, gain_two)
     grad_branch = grad_middle.astype(low)
-    mixer_gradient = inner_rows(mixed_rows, grad_branch).astype(low)
     grad_mixed = inner_cols(grad_branch, mixer_full).astype(low)
+    mixer_gradient = inner_rows(mixed_rows, after(grad_branch, grad_mixed)).astype(low)
     grad_pieces = [grad_mixed[:, at * 128 : (at + 1) * 128] for at in range(4)]
     grad_pieces = [grad_pieces[0]] + [swapped(grad_pieces[at], Z_BITS[at]) for at in (1, 2, 3)]
     mixer_keep = jnp.where(even, mixer_gradient[:, : D // 2], mixer_gradient[:, D // 2 :])
@@ -921,6 +923,7 @@
         for half in range(2):
             left = fixed(place, pl.ds(256, 32), pl.ds(half * (D // 2), D // 2))
             hidden_plan.append((2, slot_rows(20 + at, half * 32, 32), to, left))
+    expand_gradient = after(expand_gradient, grad_pieces[2])
     grouped = moved(
         table, (expand_gradient, reduce_gradient, mixer_whole), hidden_plan, [(4, 288, D)] * 4
     )
@@ -928,8 +931,9 @@
     grad_pieces = after(grad_pieces, grouped)
     grad_out = head_backward(joint_sorted, mixed_sorted, totals_sorted, grad_pieces, places)
     grad_got = [swapped(grad_out[at], Z_BITS[at]) for at in (1, 2, 3)]
+    hidden_state = summed_second(after(hidden_state, grad_got[0]))
     grad_got = after(grad_got, hidden_state)
-    hidden_state = summed_second(hidden_state)
+    result = middle[:own_rows] + (own_sum(product(after(active, grad_out), reduce_full)) + reduce_shift)
     grad_joint = jnp.concatenate([grad_out[0]] + grad_got, axis=1)
     joint_gradient = inner_rows(normed, grad_joint).astype(low).reshape(16, 64, 1536)
     grad_normed_part = inner_cols(grad_joint, joint_full)

time: 495 us -> 444 us (0.90)
  the two profiles are of different devices: /device:TPU:0 before, /device:TPU:9 now
where the time goes in v5:
time: 444 us; the launch traced here: 436 us
  waiting for transfers between devices  176 us (40%)
  starting transfers between devices  70.5 us (16%)
  Pallas kernels  62.1 us (14%)
  matrix products  45.1 us (10%)
  other arithmetic  44.5 us (10%)
  local copies, waits for them, and re-layouts  35.3 us (8%)
    ppermute x59, waiting for transfers between devices, swapped(): lax.ppermute(value, ALL, [(source, source ^ mask) for source in range(cou...  176 us
    ppermute x59, starting transfers between devices, swapped(): lax.ppermute(value, ALL, [(source, source ^ mask) for source in range(cou...  70.5 us
    pallas_call x5, Pallas kernels, moved(): pl.pallas_call(lambda *refs: moved_kernel(*refs, plan=plan, source_count=...  29.8 us
    pallas_call x1, Pallas kernels, head_backward(): pl.pallas_call(head_backward_kernel, out_shape=[jax.ShapeDtypeStruct((row...  20.6 us
    dot_general x4, matrix products, product(): return jnp.dot(left, right, preferred_element_type=jnp.float32)  16.1 us
    dot_general x4, matrix products, inner_rows(): lax.dot_general(left, right, (((0,), (0,)), ((), ())), preferred_element_...  14.9 us
    dot_general x4, matrix products, inner_cols(): lax.dot_general(left, right, (((1,), (1,)), ((), ())), preferred_element_...  14.1 us
    pallas_call x1, Pallas kernels, head_forward(): pl.pallas_call(head_forward_kernel, out_shape=[jax.ShapeDtypeStruct((rows...  11.7 us
  transfers between devices with their start and end apart: 59, of which 27 were waited for; matrix products, arithmetic and copies ran while one was open for 21% of the time, Pallas kernels for 12%

profile of v5, /device:TPU:9, one launch (start us, length us, event | category | flops | bytes accessed | tf_op | source)
XLA Modules:
  0.0 436.0 jit_solution(8139198837586760018)
XLA Ops:
  10.7 9.7 %collective-permute-done.3 = bf16[72,1536]{1,0:T(8,128)(2,1)S(1)} collective-permute-done((bf16[72,1536]{1,0:T(8,128)(2,1)S(1)}, bf16[72,1536]{1,0:T(8,128)(2,1)S(1)}, u32[]{:S(2)}, u32[]{:S(2)}) %collective-permute-start.3) | collective-permute-done | bytes 221216 | tf_op jit(solution)/shard_map/ppermute | solution.py:376
  20.4 9.2 %collective-permute-done.4 = bf16[72,1536]{1,0:T(8,128)(2,1)S(1)} collective-permute-done((bf16[72,1536]{1,0:T(8,128)(2,1)S(1)}, bf16[72,1536]{1,0:T(8,128)(2,1)S(1)}, u32[]{:S(2)}, u32[]{:S(2)}) %collective-permute-start.4) | collective-permute-done | bytes 221216 | tf_op jit(solution)/shard_map/ppermute | solution.py:376
  32.1 3.0 collective-permute-start.12
  45.6 4.9 %collective-permute-done.6.refs_3_ = bf16[4,72,1536]{2,1,0:T(8,128)(2,1)S(1)} collective-permute-done((bf16[4,72,1536]{2,1,0:T(8,128)(2,1)S(1)}, bf16[4,72,1536]{2,1,0:T(8,128)(2,1)S(1)}, u32[]{:S(2)}, u32[]{:S(2)}) %collective-permute-start.6) | collective-permute-done | bytes 884768 | tf_op jit(solution)/shard_map/ppermute | solution.py:376
  55.7 10.9 %collective-permute-done.13.refs_2_ = bf16[4,64,512]{2,1,0:T(8,128)(2,1)} collective-permute-done((bf16[4,64,512]{2,1,0:T(8,128)(2,1)}, bf16[4,64,512]{2,1,0:T(8,128)(2,1)}, u32[]{:S(2)}, u32[]{:S(2)}) %collective-permute-start.13) | collective-permute-done | bytes 262176 | tf_op jit(solution)/shard_map/ppermute | solution.py:376
  69.4 5.0 %moved.5 = (bf16[16,64,1536]{2,1,0:T(8,128)(2,1)}, bf16[16,8,768]{2,1,0:T(8,128)(2,1)}) custom-call(s32[36]{0:T(128)} %pad_add_fusion.1.refs_0_, bf16[4,72,1536]{2,1,0:T(8,128)(2,1)} %copy-done.17, bf16[4,72,1536]{2,1,0:T(8,128)(2,1)} %copy-done.23, bf16[4,72,1536]{2,1,0:T(8,128)(2,1)} %copy-done.22, bf16[2,72,1536]{2,1,0:T(8,128)(2,1)} %copy-done.33, ...), custom_call_target="tpu_custom_call" | custom-call | bytes 10027008 | tf_op jit(solution)/shard_map/moved/pallas_call | solution.py:395
  78.2 4.0 fusion.7
  82.3 5.0 %collective-permute-done.20 = bf16[256,1024]{1,0:T(8,128)(2,1)} collective-permute-done((bf16[256,1024]{1,0:T(8,128)(2,1)S(1)}, bf16[256,1024]{1,0:T(8,128)(2,1)}, u32[]{:S(2)}, u32[]{:S(2)}) %collective-permute-start.20) | collective-permute-done | bytes 524320 | tf_op jit(solution)/shard_map/ppermute | solution.py:376
  87.3 2.8 pad_maximum_fusion.refs_1_
  92.2 4.1 collective-permute-start.17
  100.6 3.0 moved.6
  105.9 15.1 %collective-permute-done.17.refs_3_ = bf16[512,384]{1,0:T(8,128)(2,1)} collective-permute-done((bf16[512,384]{1,0:T(8,128)(2,1)}, bf16[512,384]{1,0:T(8,128)(2,1)}, u32[]{:S(2)}, u32[]{:S(2)}) %collective-permute-start.17) | collective-permute-done | bytes 393248 | tf_op jit(solution)/shard_map/ppermute | solution.py:376
  121.0 4.7 %collective-permute-start.28 = (bf16[512,512]{1,0:T(8,128)(2,1)}, bf16[512,512]{1,0:T(8,128)(2,1)}, u32[]{:S(2)}, u32[]{:S(2)}) collective-permute-start(bf16[512,512]{1,0:T(8,128)(2,1)} %bitcast.20), channel_id=1, source_target_pairs={{0,1},{1,0},{2,3},{3,2},{4,5},{5,4},{6,7},{7,6},{8,9},{9,8},{10,11... | collective-permute-start | bytes 1572872 | tf_op jit(solution)/shard_map/ppermute | solution.py:376
  127.8 11.7 %head_forward.1 = (bf16[512,128]{1,0:T(8,128)(2,1)}, bf16[512,128]{1,0:T(8,128)(2,1)}, bf16[512,128]{1,0:T(8,128)(2,1)}, bf16[512,128]{1,0:T(8,128)(2,1)}, bf16[...) custom-call(s32[16]{0:T(128)} %gather_fusion, bf16[512,384]{1,0:T(8,128)(2,1)} %get-tuple-element.161.refs_0_, ...), custom_call_target="tpu_custom_call" | custom-call | flops 6442450944 | bytes 6291456 | tf_op jit(solution)/shard_map/head_forward/pallas_call | solution.py:556
  139.6 2.9 collective-permute-start.25
  148.7 3.5 collective-permute-done.26
  152.2 7.5 %collective-permute-done.27 = bf16[512,128]{1,0:T(8,128)(2,1)S(1)} collective-permute-done((bf16[512,128]{1,0:T(8,128)(2,1)S(1)}, bf16[512,128]{1,0:T(8,128)(2,1)S(1)}, u32[]{:S(2)}, u32[]{:S(2)}) %collective-permute-start.27) | collective-permute-done | bytes 131104 | tf_op jit(solution)/shard_map/ppermute | solution.py:376
  159.8 3.5 fusion.69
  168.4 7.9 %moved.7 = (bf16[16,64,2048]{2,1,0:T(8,128)(2,1)}, bf16[16,128,1024]{2,1,0:T(8,128)(2,1)}) custom-call(s32[36]{0:T(128)} %pad_add_fusion.1.refs_0_, bf16[4,256,1024]{2,1,0:T(8,128)(2,1)} %pad_maximum_fusion.refs_1_, bf16[4,256,1024]{2,1,0:T(8,128)(2,1)} %collective-permute-done.23.refs_2_, bf16[4,256,1024]{2,1,0:T(8,128)(2,1)} %copy-done.16, ...), custom_call_target="tpu_custom_call" | custom-call | bytes 25165824 | tf_op jit(solution)/shard_map/moved/pallas_call | solution.py:395
  183.0 3.3 multiply_convert_fusion
  186.4 6.2 %convert_reduce_fusion = (f32[2048]{0:T(1024)}, bf16[512,2048]{1,0:T(8,128)(2,1)S(1)}) fusion(f32[512,2048]{1,0:T(8,128)S(1)} %get-tuple-element.225, f32[2048]{0:T(1024)S(1)} %bitcast.181, bf16[2048,1024]{1,0:T(8,128)(2,1)S(1)} %bitcast.186, bf16[256,1024]{1,0:T(8,128)(2,1)S(1)} %copy-done.15, bf16[256,1024]{1,0:T(8,128)(2,1)S(1)} %bitcast.149), kind=kOutput, calls=%fused_computation.10 | convolution fusion | flops 2173696000 | bytes 11550720 | tf_op jit(solution)/shard_map/dot_general | solution.py:47
  195.1 4.0 collective-permute-start.32
  199.1 4.5 %convolution_convert_fusion.2 = bf16[1024,2048]{1,0:T(8,128)(2,1)} fusion(bf16[512,2048]{1,0:T(8,128)(2,1)S(1)} %get-tuple-element.229, f32[512,1024]{1,0:T(8,128)S(1)} %subtract_multiply_fusion, f32[1024]{0:T(1024)S(1)} %reshape.574, f32[1024]{0:T(1024)S(1)} %reshape.573), kind=kOutput, calls=%fused_computation.14 | convolution fusion | flops 2151153664 | bytes 8396800 | tf_op jit(solution)/shard_map/dot_general | solution.py:41
  211.1 4.5 %convolution_convert_fusion.1 = bf16[2048,1024]{1,0:T(8,128)(2,1)} fusion(bf16[512,2048]{1,0:T(8,128)(2,1)S(1)} %get-tuple-element.121, bf16[256,1024]{1,0:T(8,128)(2,1)S(1)} %copy-done.15, bf16[256,1024]{1,0:T(8,128)(2,1)S(1)} %bitcast.151), kind=kOutput, calls=%fused_computation.13 | convolution fusion | flops 2151677952 | bytes 7340032 | tf_op jit(solution)/shard_map/dot_general | solution.py:41
  217.5 8.7 %moved.8 = (bf16[4,288,1024]{2,1,0:T(8,128)(2,1)}, bf16[4,288,1024]{2,1,0:T(8,128)(2,1)}, bf16[4,288,1024]{2,1,0:T(8,128)(2,1)}, bf16[4,288,1024]{2,1,0:T(8,128)(2,1)}) custom-call(s32[36]{0:T(128)} %pad_add_fusion.1.refs_0_, bf16[16,64,2048]{2,1,0:T(8,128)(2,1)} %bitcast.152, bf16[16,128,1024]{2,1,0:T(8,128)(2,1)} %bitcast.153, bf16[16,64,512]{2,1,0:T(8,128)(2,1)} %bitcast.154), custom_call_target="tpu_custom_call" | custom-call | bytes 28311552 | tf_op jit(solution)/shard_map/moved/pallas_call | solution.py:395
  230.3 3.5 collective-permute-start.33
  234.7 3.8 collective-permute-done.33.refs_1_
  238.5 20.6 %head_backward.1 = (bf16[512,384]{1,0:T(8,128)(2,1)}, bf16[512,384]{1,0:T(8,128)(2,1)}, bf16[512,384]{1,0:T(8,128)(2,1)}, bf16[512,384]{1,0:T(8,128)(2,1)}) custom-call(s32[16]{0:T(128)} %gather_fusion, bf16[2048,384]{1,0:T(8,128)(2,1)} %get-tuple-element.103.joint_ref, f32[2048,128]{1,0:T(8,128)} %get-tuple-element.104.mixed_ref, ...), custom_call_target="tpu_custom_call" | custom-call | flops 16106127360 | bytes 6291456 | tf_op jit(solution)/shard_map/head_backward/pallas_call | solution.py:678
  260.3 17.6 %collective-permute-done.41 = bf16[4,288,1024]{2,1,0:T(8,128)(2,1)} collective-permute-done((bf16[4,288,1024]{2,1,0:T(8,128)(2,1)}, bf16[4,288,1024]{2,1,0:T(8,128)(2,1)}, u32[]{:S(2)}, u32[]{:S(2)}) %collective-permute-start.41) | collective-permute-done | bytes 2359328 | tf_op jit(solution)/shard_map/ppermute | solution.py:376
  277.9 5.2 %convert_add_fusion.3 = (f32[2,288,1024]{2,1,0:T(8,128)}, bf16[2,288,1024]{2,1,0:T(8,128)(2,1)}) fusion(bf16[4,288,1024]{2,1,0:T(8,128)(2,1)} %collective-permute-done.41, bf16[4,288,1024]{2,1,0:T(8,128)(2,1)} %get-tuple-element.109), kind=kLoop, calls=%fused_computation.26 | loop fusion | flops 4128768 | bytes 8257536 | tf_op jit(solution)/shard_map/add | solution.py:467
  283.1 4.7 %convert_add_fusion.2 = (f32[2,288,1024]{2,1,0:T(8,128)}, bf16[2,288,1024]{2,1,0:T(8,128)(2,1)}) fusion(bf16[4,288,1024]{2,1,0:T(8,128)(2,1)} %collective-permute-done.42, bf16[4,288,1024]{2,1,0:T(8,128)(2,1)S(1)} %copy-done.21), kind=kLoop, calls=%fused_computation.25 | loop fusion | flops 4128768 | bytes 8257536 | tf_op jit(solution)/shard_map/add | solution.py:468
  294.6 3.1 collective-permute-start.39
  298.6 5.3 %fusion.71 = f32[512,1024]{1,0:T(8,128)S(1)} fusion(bf16[512,2048]{1,0:T(8,128)(2,1)} %copy-done.62, bf16[2048,1024]{1,0:T(8,128)(2,1)} %bitcast.185), kind=kOutput, calls=%fused_computation.255 | convolution fusion | flops 2147483648 | bytes 8388608 | tf_op jit(solution)/shard_map/dot_general | solution.py:37
  305.0 3.4 collective-permute-start.37
  308.4 4.9 %collective-permute-done.43 = bf16[2,288,1024]{2,1,0:T(8,128)(2,1)} collective-permute-done((bf16[2,288,1024]{2,1,0:T(8,128)(2,1)}, bf16[2,288,1024]{2,1,0:T(8,128)(2,1)}, u32[]{:S(2)}, u32[]{:S(2)}) %collective-permute-start.43) | collective-permute-done | bytes 1179680 | tf_op jit(solution)/shard_map/ppermute | solution.py:376
  319.7 3.5 collective-permute-done.39
  323.2 9.6 %collective-permute-done.40 = bf16[512,384]{1,0:T(8,128)(2,1)S(1)} collective-permute-done((bf16[512,384]{1,0:T(8,128)(2,1)}, bf16[512,384]{1,0:T(8,128)(2,1)S(1)}, u32[]{:S(2)}, u32[]{:S(2)}) %collective-permute-start.40) | collective-permute-done | bytes 393248 | tf_op jit(solution)/shard_map/ppermute | solution.py:376
  333.0 3.2 fusion.54
  339.8 5.2 %convolution_convert_fusion = bf16[1024,1536]{1,0:T(8,128)(2,1)} fusion(bf16[512,1024]{1,0:T(8,128)(2,1)} %copy-done.26, bf16[512,1536]{1,0:T(8,128)(2,1)} %copy-done.18), kind=kOutput, calls=%fused_computation.12 | convolution fusion | flops 1612185600 | bytes 5767168 | tf_op jit(solution)/shard_map/dot_general | solution.py:41
  345.0 5.1 %moved.9 = (bf16[4,72,1536]{2,1,0:T(8,128)(2,1)}, bf16[4,72,1536]{2,1,0:T(8,128)(2,1)}, bf16[4,72,1536]{2,1,0:T(8,128)(2,1)}, bf16[4,72,1536]{2,1,0:T(8,128)(2,1)}) custom-call(s32[36]{0:T(128)} %pad_add_fusion.1.refs_0_, bf16[16,64,1536]{2,1,0:T(8,128)(2,1)} %bitcast.155, bf16[16,8,768]{2,1,0:T(8,128)(2,1)} %pad.60.refs_2_), custom_call_target="tpu_custom_call" | custom-call | bytes 10616832 | tf_op jit(solution)/shard_map/moved/pallas_call | solution.py:395
  350.7 2.7 fusion.18
  361.7 10.0 %collective-permute-done.46 = bf16[4,72,1536]{2,1,0:T(8,128)(2,1)S(1)} collective-permute-done((bf16[4,72,1536]{2,1,0:T(8,128)(2,1)}, bf16[4,72,1536]{2,1,0:T(8,128)(2,1)S(1)}, u32[]{:S(2)}, u32[]{:S(2)}) %collective-permute-start.46) | collective-permute-done | bytes 884768 | tf_op jit(solution)/shard_map/ppermute | solution.py:376
  372.4 5.1 %collective-permute-done.49 = bf16[4,72,1536]{2,1,0:T(8,128)(2,1)S(1)} collective-permute-done((bf16[4,72,1536]{2,1,0:T(8,128)(2,1)}, bf16[4,72,1536]{2,1,0:T(8,128)(2,1)S(1)}, u32[]{:S(2)}, u32[]{:S(2)}) %collective-permute-start.49) | collective-permute-done | bytes 884768 | tf_op jit(solution)/shard_map/ppermute | solution.py:376
  378.2 8.8 %collective-permute-done.47 = bf16[2,72,1536]{2,1,0:T(8,128)(2,1)S(1)} collective-permute-done((bf16[2,72,1536]{2,1,0:T(8,128)(2,1)S(1)}, bf16[2,72,1536]{2,1,0:T(8,128)(2,1)S(1)}, u32[]{:S(2)}, u32[]{:S(2)}) %collective-permute-start.47) | collective-permute-done | bytes 442400 | tf_op jit(solution)/shard_map/ppermute | solution.py:376
  387.6 17.9 %collective-permute-done.55 = bf16[288,1024]{1,0:T(8,128)(2,1)S(1)} collective-permute-done((bf16[288,1024]{1,0:T(8,128)(2,1)}, bf16[288,1024]{1,0:T(8,128)(2,1)S(1)}, u32[]{:S(2)}, u32[]{:S(2)}) %collective-permute-start.55) | collective-permute-done | bytes 589856 | tf_op jit(solution)/shard_map/ppermute | solution.py:376
  406.9 3.0 collective-permute-start.51
  412.1 11.5 %collective-permute-done.51 = bf16[72,1536]{1,0:T(8,128)(2,1)S(1)} collective-permute-done((bf16[72,1536]{1,0:T(8,128)(2,1)S(1)}, bf16[72,1536]{1,0:T(8,128)(2,1)S(1)}, u32[]{:S(2)}, u32[]{:S(2)}) %collective-permute-start.51) | collective-permute-done | bytes 221216 | tf_op jit(solution)/shard_map/ppermute | solution.py:376
  423.6 6.4 %collective-permute-done.52 = bf16[72,1536]{1,0:T(8,128)(2,1)S(1)} collective-permute-done((bf16[72,1536]{1,0:T(8,128)(2,1)S(1)}, bf16[72,1536]{1,0:T(8,128)(2,1)S(1)}, u32[]{:S(2)}, u32[]{:S(2)}) %collective-permute-start.52) | collective-permute-done | bytes 221216 | tf_op jit(solution)/shard_map/ppermute | solution.py:376
  (400 shorter events, 119.8 us)
Async XLA Ops:
  6.9 36.0 %collective-permute-start = (bf16[512,1024]{1,0:T(8,128)(2,1)}, bf16[512,1024]{1,0:T(8,128)(2,1)}, u32[]{:S(2)}, u32[]{:S(2)}) collective-permute-start(bf16[512,1024]{1,0:T(8,128)(2,1)} %pad_maximum_fusion.1), channel_id=1, source_target_pairs={{0,1},{1,0},{2,3},{3,2},{4,5},{5,4},{6,7},{7,6},{8,9},{9,8},{10,11... | collective-permute-start | bytes 3145736 | tf_op jit(solution)/shard_map/ppermute | solution.py:376
  7.9 12.5 %collective-permute-start.3 = (bf16[72,1536]{1,0:T(8,128)(2,1)S(1)}, bf16[72,1536]{1,0:T(8,128)(2,1)S(1)}, u32[]{:S(2)}, u32[]{:S(2)}) collective-permute-start(bf16[72,1536]{1,0:T(8,128)(2,1)S(1)} %get-tuple-element.195), channel_id=1, source_target_pairs={{0,4},{1,5},{2,6},{3,7},{4,0},{5,1},{6,2},{7,3},{8,12},{9,13},{10,... | collective-permute-start | bytes 663560 | tf_op jit(solution)/shard_map/ppermute | solution.py:376
  10.3 10.1 %collective-permute-start.2 = (bf16[72,1536]{1,0:T(8,128)(2,1)S(1)}, bf16[72,1536]{1,0:T(8,128)(2,1)S(1)}, u32[]{:S(2)}, u32[]{:S(2)}) collective-permute-start(bf16[72,1536]{1,0:T(8,128)(2,1)S(1)} %get-tuple-element.195), channel_id=1, source_target_pairs={{0,2},{1,3},{2,0},{3,1},{4,6},{5,7},{6,4},{7,5},{8,10},{9,11},{10,... | collective-permute-start | bytes 663560 | tf_op jit(solution)/shard_map/ppermute | solution.py:376
  10.5 19.1 %collective-permute-start.4 = (bf16[72,1536]{1,0:T(8,128)(2,1)S(1)}, bf16[72,1536]{1,0:T(8,128)(2,1)S(1)}, u32[]{:S(2)}, u32[]{:S(2)}) collective-permute-start(bf16[72,1536]{1,0:T(8,128)(2,1)S(1)} %get-tuple-element.195), channel_id=1, source_target_pairs={{0,6},{1,7},{2,4},{3,5},{4,2},{5,3},{6,0},{7,1},{8,14},{9,15},{10,... | collective-permute-start | bytes 663560 | tf_op jit(solution)/shard_map/ppermute | solution.py:376
  29.7 20.8 %collective-permute-start.6 = (bf16[4,72,1536]{2,1,0:T(8,128)(2,1)S(1)}, bf16[4,72,1536]{2,1,0:T(8,128)(2,1)S(1)}, u32[]{:S(2)}, u32[]{:S(2)}) collective-permute-start(bf16[4,72,1536]{2,1,0:T(8,128)(2,1)S(1)} %pad_maximum_fusion.7.refs_1_), channel_id=1, source_target_pairs={{0,16},{1,17},{2,18},{3,19},{4,20},{5,21},{6,22},{7,23},{8,24},{9,... | collective-permute-start | bytes 2654216 | tf_op jit(solution)/shard_map/ppermute | solution.py:376
  31.0 20.5 %collective-permute-start.5 = (bf16[4,72,1536]{2,1,0:T(8,128)(2,1)S(1)}, bf16[4,72,1536]{2,1,0:T(8,128)(2,1)S(1)}, u32[]{:S(2)}, u32[]{:S(2)}) collective-permute-start(bf16[4,72,1536]{2,1,0:T(8,128)(2,1)S(1)} %pad_maximum_fusion.7.refs_1_), channel_id=1, source_target_pairs={{0,8},{1,9},{2,10},{3,11},{4,12},{5,13},{6,14},{7,15},{8,0},{9,1},... | collective-permute-start | bytes 2654216 | tf_op jit(solution)/shard_map/ppermute | solution.py:376
  40.5 41.7 %collective-permute-start.21 = (bf16[256,1024]{1,0:T(8,128)(2,1)S(1)}, bf16[256,1024]{1,0:T(8,128)(2,1)}, u32[]{:S(2)}, u32[]{:S(2)}) collective-permute-start(bf16[256,1024]{1,0:T(8,128)(2,1)S(1)} %pad_maximum_fusion.8), channel_id=1, source_target_pairs={{0,6},{1,7},{2,4},{3,5},{4,2},{5,3},{6,0},{7,1},{8,14},{9,15},{10,... | collective-permute-start | bytes 1572872 | tf_op jit(solution)/shard_map/ppermute | solution.py:376
  42.3 45.0 %collective-permute-start.20 = (bf16[256,1024]{1,0:T(8,128)(2,1)S(1)}, bf16[256,1024]{1,0:T(8,128)(2,1)}, u32[]{:S(2)}, u32[]{:S(2)}) collective-permute-start(bf16[256,1024]{1,0:T(8,128)(2,1)S(1)} %pad_maximum_fusion.8), channel_id=1, source_target_pairs={{0,4},{1,5},{2,6},{3,7},{4,0},{5,1},{6,2},{7,3},{8,12},{9,13},{10,... | collective-permute-start | bytes 1572872 | tf_op jit(solution)/shard_map/ppermute | solution.py:376
  50.5 16.1 %collective-permute-start.8 = (bf16[2,72,1536]{2,1,0:T(8,128)(2,1)S(1)}, bf16[2,72,1536]{2,1,0:T(8,128)(2,1)S(1)}, u32[]{:S(2)}, u32[]{:S(2)}) collective-permute-start(bf16[2,72,1536]{2,1,0:T(8,128)(2,1)S(1)} %slice.541), channel_id=1, source_target_pairs={{0,8},{1,9},{2,10},{3,11},{4,12},{5,13},{6,14},{7,15},{8,0},{9,1},... | collective-permute-start | bytes 1327112 | tf_op jit(solution)/shard_map/ppermute | solution.py:376
  51.6 16.4 %collective-permute-start.7 = (bf16[2,72,1536]{2,1,0:T(8,128)(2,1)S(1)}, bf16[2,72,1536]{2,1,0:T(8,128)(2,1)S(1)}, u32[]{:S(2)}, u32[]{:S(2)}) collective-permute-start(bf16[2,72,1536]{2,1,0:T(8,128)(2,1)S(1)} %slice.540), channel_id=1, source_target_pairs={{0,16},{1,17},{2,18},{3,19},{4,20},{5,21},{6,22},{7,23},{8,24},{9,... | collective-permute-start | bytes 1327112 | tf_op jit(solution)/shard_map/ppermute | solution.py:376
  52.9 13.8 %collective-permute-start.13 = (bf16[4,64,512]{2,1,0:T(8,128)(2,1)}, bf16[4,64,512]{2,1,0:T(8,128)(2,1)}, u32[]{:S(2)}, u32[]{:S(2)}) collective-permute-start(bf16[4,64,512]{2,1,0:T(8,128)(2,1)} %pad_maximum_fusion.9.refs_1_), channel_id=1, source_target_pairs={{0,8},{1,9},{2,10},{3,11},{4,12},{5,13},{6,14},{7,15},{8,0},{9,1},... | collective-permute-start | bytes 786440 | tf_op jit(solution)/shard_map/ppermute | solution.py:376
  66.6 20.6 %collective-permute-start.19 = (bf16[256,1024]{1,0:T(8,128)(2,1)S(1)}, bf16[256,1024]{1,0:T(8,128)(2,1)S(1)}, u32[]{:S(2)}, u32[]{:S(2)}) collective-permute-start(bf16[256,1024]{1,0:T(8,128)(2,1)S(1)} %pad_maximum_fusion.8), channel_id=1, source_target_pairs={{0,2},{1,3},{2,0},{3,1},{4,6},{5,7},{6,4},{7,5},{8,10},{9,11},{10,... | collective-permute-start | bytes 1572872 | tf_op jit(solution)/shard_map/ppermute | solution.py:376
  66.6 11.5 %collective-permute-start.14 = (bf16[4,64,512]{2,1,0:T(8,128)(2,1)}, bf16[4,64,512]{2,1,0:T(8,128)(2,1)S(1)}, u32[]{:S(2)}, u32[]{:S(2)}) collective-permute-start(bf16[4,64,512]{2,1,0:T(8,128)(2,1)} %pad_maximum_fusion.9.refs_1_), channel_id=1, source_target_pairs={{0,16},{1,17},{2,18},{3,19},{4,20},{5,21},{6,22},{7,23},{8,24},{9,... | collective-permute-start | bytes 786440 | tf_op jit(solution)/shard_map/ppermute | solution.py:376
  68.7 18.6 %collective-permute-start.22 = (bf16[4,64,512]{2,1,0:T(8,128)(2,1)}, bf16[4,64,512]{2,1,0:T(8,128)(2,1)}, u32[]{:S(2)}, u32[]{:S(2)}) collective-permute-start(bf16[4,64,512]{2,1,0:T(8,128)(2,1)} %collective-permute-done.13.refs_2_), channel_id=1, source_target_pairs={{0,16},{1,17},{2,18},{3,19},{4,20},{5,21},{6,22},{7,23},{8,24},{9,... | collective-permute-start | bytes 786440 | tf_op jit(solution)/shard_map/ppermute | solution.py:376
  90.0 49.5 %collective-permute-start.24 = (bf16[4,256,1024]{2,1,0:T(8,128)(2,1)}, bf16[4,256,1024]{2,1,0:T(8,128)(2,1)S(1)}, u32[]{:S(2)}, u32[]{:S(2)}) collective-permute-start(bf16[4,256,1024]{2,1,0:T(8,128)(2,1)} %pad_maximum_fusion.refs_1_), channel_id=1, source_target_pairs={{0,16},{1,17},{2,18},{3,19},{4,20},{5,21},{6,22},{7,23},{8,24},{9,... | collective-permute-start | bytes 6291464 | tf_op jit(solution)/shard_map/ppermute | solution.py:376
  91.1 48.5 %collective-permute-start.23 = (bf16[4,256,1024]{2,1,0:T(8,128)(2,1)}, bf16[4,256,1024]{2,1,0:T(8,128)(2,1)}, u32[]{:S(2)}, u32[]{:S(2)}) collective-permute-start(bf16[4,256,1024]{2,1,0:T(8,128)(2,1)} %pad_maximum_fusion.refs_1_), channel_id=1, source_target_pairs={{0,8},{1,9},{2,10},{3,11},{4,12},{5,13},{6,14},{7,15},{8,0},{9,1},... | collective-permute-start | bytes 6291464 | tf_op jit(solution)/shard_map/ppermute | solution.py:376
  92.2 28.9 %collective-permute-start.17 = (bf16[512,384]{1,0:T(8,128)(2,1)}, bf16[512,384]{1,0:T(8,128)(2,1)}, u32[]{:S(2)}, u32[]{:S(2)}) collective-permute-start(bf16[512,384]{1,0:T(8,128)(2,1)} %get-tuple-element.158), channel_id=1, source_target_pairs={{0,6},{1,7},{2,4},{3,5},{4,2},{5,3},{6,0},{7,1},{8,14},{9,15},{10,... | collective-permute-start | bytes 1179656 | tf_op jit(solution)/shard_map/ppermute | solution.py:376
  96.3 31.5 %collective-permute-start.16 = (bf16[512,384]{1,0:T(8,128)(2,1)}, bf16[512,384]{1,0:T(8,128)(2,1)}, u32[]{:S(2)}, u32[]{:S(2)}) collective-permute-start(bf16[512,384]{1,0:T(8,128)(2,1)} %get-tuple-element.159), channel_id=1, source_target_pairs={{0,4},{1,5},{2,6},{3,7},{4,0},{5,1},{6,2},{7,3},{8,12},{9,13},{10,... | collective-permute-start | bytes 1179656 | tf_op jit(solution)/shard_map/ppermute | solution.py:376
  98.2 29.6 %collective-permute-start.15 = (bf16[512,384]{1,0:T(8,128)(2,1)S(1)}, bf16[512,384]{1,0:T(8,128)(2,1)}, u32[]{:S(2)}, u32[]{:S(2)}) collective-permute-start(bf16[512,384]{1,0:T(8,128)(2,1)S(1)} %get-tuple-element.160), channel_id=1, source_target_pairs={{0,2},{1,3},{2,0},{3,1},{4,6},{5,7},{6,4},{7,5},{8,10},{9,11},{10,... | collective-permute-start | bytes 1179656 | tf_op jit(solution)/shard_map/ppermute | solution.py:376
  121.0 38.8 %collective-permute-start.28 = (bf16[512,512]{1,0:T(8,128)(2,1)}, bf16[512,512]{1,0:T(8,128)(2,1)}, u32[]{:S(2)}, u32[]{:S(2)}) collective-permute-start(bf16[512,512]{1,0:T(8,128)(2,1)} %bitcast.20), channel_id=1, source_target_pairs={{0,1},{1,0},{2,3},{3,2},{4,5},{5,4},{6,7},{7,6},{8,9},{9,8},{10,11... | collective-permute-start | bytes 1572872 | tf_op jit(solution)/shard_map/ppermute | solution.py:376
  139.6 8.1 %collective-permute-start.25 = (bf16[512,128]{1,0:T(8,128)(2,1)}, bf16[512,128]{1,0:T(8,128)(2,1)S(1)}, u32[]{:S(2)}, u32[]{:S(2)}) collective-permute-start(bf16[512,128]{1,0:T(8,128)(2,1)} %get-tuple-element.99), channel_id=1, source_target_pairs={{0,2},{1,3},{2,0},{3,1},{4,6},{5,7},{6,4},{7,5},{8,10},{9,11},{10,... | collective-permute-start | bytes 393224 | tf_op jit(solution)/shard_map/ppermute | solution.py:376
  143.6 22.2 %collective-permute-start.31 = (bf16[2,256,1024]{2,1,0:T(8,128)(2,1)}, bf16[2,256,1024]{2,1,0:T(8,128)(2,1)}, u32[]{:S(2)}, u32[]{:S(2)}) collective-permute-start(bf16[2,256,1024]{2,1,0:T(8,128)(2,1)} %slice.568), channel_id=1, source_target_pairs={{0,8},{1,9},{2,10},{3,11},{4,12},{5,13},{6,14},{7,15},{8,0},{9,1},... | collective-permute-start | bytes 3145736 | tf_op jit(solution)/shard_map/ppermute | solution.py:376
  146.5 21.9 %collective-permute-start.30 = (bf16[2,256,1024]{2,1,0:T(8,128)(2,1)}, bf16[2,256,1024]{2,1,0:T(8,128)(2,1)}, u32[]{:S(2)}, u32[]{:S(2)}) collective-permute-start(bf16[2,256,1024]{2,1,0:T(8,128)(2,1)} %slice.567), channel_id=1, source_target_pairs={{0,16},{1,17},{2,18},{3,19},{4,20},{5,21},{6,22},{7,23},{8,24},{9,... | collective-permute-start | bytes 3145736 | tf_op jit(solution)/shard_map/ppermute | solution.py:376
  147.7 12.0 %collective-permute-start.27 = (bf16[512,128]{1,0:T(8,128)(2,1)S(1)}, bf16[512,128]{1,0:T(8,128)(2,1)S(1)}, u32[]{:S(2)}, u32[]{:S(2)}) collective-permute-start(bf16[512,128]{1,0:T(8,128)(2,1)S(1)} %copy-done.60), channel_id=1, source_target_pairs={{0,6},{1,7},{2,4},{3,5},{4,2},{5,3},{6,0},{7,1},{8,14},{9,15},{10,... | collective-permute-start | bytes 393224 | tf_op jit(solution)/shard_map/ppermute | solution.py:376
  163.5 12.9 %collective-permute-start.29 = (bf16[512,1024]{1,0:T(8,128)(2,1)S(1)}, bf16[512,1024]{1,0:T(8,128)(2,1)S(1)}, u32[]{:S(2)}, u32[]{:S(2)}) collective-permute-start(bf16[512,1024]{1,0:T(8,128)(2,1)S(1)} %pad_maximum_fusion.3), channel_id=1, source_target_pairs={{0,1},{1,0},{2,3},{3,2},{4,5},{5,4},{6,7},{7,6},{8,9},{9,8},{10,11... | collective-permute-start | bytes 3145736 | tf_op jit(solution)/shard_map/ppermute | solution.py:376
  195.1 8.5 %collective-permute-start.32 = (bf16[512,1024]{1,0:T(8,128)(2,1)S(1)}, bf16[512,1024]{1,0:T(8,128)(2,1)S(1)}, u32[]{:S(2)}, u32[]{:S(2)}) collective-permute-start(bf16[512,1024]{1,0:T(8,128)(2,1)S(1)} %pad_maximum_fusion.5), channel_id=1, source_target_pairs={{0,1},{1,0},{2,3},{3,2},{4,5},{5,4},{6,7},{7,6},{8,9},{9,8},{10,11... | collective-permute-start | bytes 3145736 | tf_op jit(solution)/shard_map/ppermute | solution.py:376
  226.1 51.7 %collective-permute-start.41 = (bf16[4,288,1024]{2,1,0:T(8,128)(2,1)}, bf16[4,288,1024]{2,1,0:T(8,128)(2,1)}, u32[]{:S(2)}, u32[]{:S(2)}) collective-permute-start(bf16[4,288,1024]{2,1,0:T(8,128)(2,1)} %get-tuple-element.110), channel_id=1, source_target_pairs={{0,16},{1,17},{2,18},{3,19},{4,20},{5,21},{6,22},{7,23},{8,24},{9,... | collective-permute-start | bytes 7077896 | tf_op jit(solution)/shard_map/ppermute | solution.py:376
  227.1 55.9 %collective-permute-start.42 = (bf16[4,288,1024]{2,1,0:T(8,128)(2,1)}, bf16[4,288,1024]{2,1,0:T(8,128)(2,1)}, u32[]{:S(2)}, u32[]{:S(2)}) collective-permute-start(bf16[4,288,1024]{2,1,0:T(8,128)(2,1)} %get-tuple-element.112), channel_id=1, source_target_pairs={{0,8},{1,9},{2,10},{3,11},{4,12},{5,13},{6,14},{7,15},{8,0},{9,1},... | collective-permute-start | bytes 7077896 | tf_op jit(solution)/shard_map/ppermute | solution.py:376
  230.3 8.1 %collective-permute-start.33 = (bf16[512,128]{1,0:T(8,128)(2,1)S(1)}, bf16[512,128]{1,0:T(8,128)(2,1)}, u32[]{:S(2)}, u32[]{:S(2)}) collective-permute-start(bf16[512,128]{1,0:T(8,128)(2,1)S(1)} %get-tuple-element.180), channel_id=1, source_target_pairs={{0,2},{1,3},{2,0},{3,1},{4,6},{5,7},{6,4},{7,5},{8,10},{9,11},{10,... | collective-permute-start | bytes 393224 | tf_op jit(solution)/shard_map/ppermute | solution.py:376
  259.1 28.8 %collective-permute-start.38 = (bf16[512,384]{1,0:T(8,128)(2,1)}, bf16[512,384]{1,0:T(8,128)(2,1)S(1)}, u32[]{:S(2)}, u32[]{:S(2)}) collective-permute-start(bf16[512,384]{1,0:T(8,128)(2,1)} %get-tuple-element.118), channel_id=1, source_target_pairs={{0,2},{1,3},{2,0},{3,1},{4,6},{5,7},{6,4},{7,5},{8,10},{9,11},{10,... | collective-permute-start | bytes 1179656 | tf_op jit(solution)/shard_map/ppermute | solution.py:376
  287.8 25.5 %collective-permute-start.43 = (bf16[2,288,1024]{2,1,0:T(8,128)(2,1)}, bf16[2,288,1024]{2,1,0:T(8,128)(2,1)}, u32[]{:S(2)}, u32[]{:S(2)}) collective-permute-start(bf16[2,288,1024]{2,1,0:T(8,128)(2,1)} %get-tuple-element.123), channel_id=1, source_target_pairs={{0,8},{1,9},{2,10},{3,11},{4,12},{5,13},{6,14},{7,15},{8,0},{9,1},... | collective-permute-start | bytes 3538952 | tf_op jit(solution)/shard_map/ppermute | solution.py:376
  290.1 25.2 %collective-permute-start.44 = (bf16[2,288,1024]{2,1,0:T(8,128)(2,1)}, bf16[2,288,1024]{2,1,0:T(8,128)(2,1)}, u32[]{:S(2)}, u32[]{:S(2)}) collective-permute-start(bf16[2,288,1024]{2,1,0:T(8,128)(2,1)} %get-tuple-element.125), channel_id=1, source_target_pairs={{0,16},{1,17},{2,18},{3,19},{4,20},{5,21},{6,22},{7,23},{8,24},{9,... | collective-permute-start | bytes 3538952 | tf_op jit(solution)/shard_map/ppermute | solution.py:376
  294.6 28.6 %collective-permute-start.39 = (bf16[512,384]{1,0:T(8,128)(2,1)}, bf16[512,384]{1,0:T(8,128)(2,1)S(1)}, u32[]{:S(2)}, u32[]{:S(2)}) collective-permute-start(bf16[512,384]{1,0:T(8,128)(2,1)} %get-tuple-element.119), channel_id=1, source_target_pairs={{0,4},{1,5},{2,6},{3,7},{4,0},{5,1},{6,2},{7,3},{8,12},{9,13},{10,... | collective-permute-start | bytes 1179656 | tf_op jit(solution)/shard_map/ppermute | solution.py:376
  297.7 35.1 %collective-permute-start.40 = (bf16[512,384]{1,0:T(8,128)(2,1)}, bf16[512,384]{1,0:T(8,128)(2,1)S(1)}, u32[]{:S(2)}, u32[]{:S(2)}) collective-permute-start(bf16[512,384]{1,0:T(8,128)(2,1)} %get-tuple-element.120), channel_id=1, source_target_pairs={{0,6},{1,7},{2,4},{3,5},{4,2},{5,3},{6,0},{7,1},{8,14},{9,15},{10,... | collective-permute-start | bytes 1179656 | tf_op jit(solution)/shard_map/ppermute | solution.py:376
  305.0 45.8 %collective-permute-start.37 = (bf16[256,1024]{1,0:T(8,128)(2,1)}, bf16[256,1024]{1,0:T(8,128)(2,1)}, u32[]{:S(2)}, u32[]{:S(2)}) collective-permute-start(bf16[256,1024]{1,0:T(8,128)(2,1)} %slice.765), channel_id=1, source_target_pairs={{0,1},{1,0},{2,3},{3,2},{4,5},{5,4},{6,7},{7,6},{8,9},{9,8},{10,11... | collective-permute-start | bytes 1572872 | tf_op jit(solution)/shard_map/ppermute | solution.py:376
  339.2 17.8 %collective-permute-start.45 = (bf16[256,1024]{1,0:T(8,128)(2,1)S(1)}, bf16[256,1024]{1,0:T(8,128)(2,1)S(1)}, u32[]{:S(2)}, u32[]{:S(2)}) collective-permute-start(bf16[256,1024]{1,0:T(8,128)(2,1)S(1)} %slice.764), channel_id=1, source_target_pairs={{0,1},{1,0},{2,3},{3,2},{4,5},{5,4},{6,7},{7,6},{8,9},{9,8},{10,11... | collective-permute-start | bytes 1572872 | tf_op jit(solution)/shard_map/ppermute | solution.py:376
  350.2 21.5 %collective-permute-start.46 = (bf16[4,72,1536]{2,1,0:T(8,128)(2,1)}, bf16[4,72,1536]{2,1,0:T(8,128)(2,1)S(1)}, u32[]{:S(2)}, u32[]{:S(2)}) collective-permute-start(bf16[4,72,1536]{2,1,0:T(8,128)(2,1)} %get-tuple-element.131), channel_id=1, source_target_pairs={{0,16},{1,17},{2,18},{3,19},{4,20},{5,21},{6,22},{7,23},{8,24},{9,... | collective-permute-start | bytes 2654216 | tf_op jit(solution)/shard_map/ppermute | solution.py:376
  353.5 34.1 %collective-permute-start.54 = (bf16[288,1024]{1,0:T(8,128)(2,1)S(1)}, bf16[288,1024]{1,0:T(8,128)(2,1)S(1)}, u32[]{:S(2)}, u32[]{:S(2)}) collective-permute-start(bf16[288,1024]{1,0:T(8,128)(2,1)S(1)} %copy-done.29), channel_id=1, source_target_pairs={{0,2},{1,3},{2,0},{3,1},{4,6},{5,7},{6,4},{7,5},{8,10},{9,11},{10,... | collective-permute-start | bytes 1769480 | tf_op jit(solution)/shard_map/ppermute | solution.py:376
  353.5 34.0 %collective-permute-start.56 = (bf16[288,1024]{1,0:T(8,128)(2,1)}, bf16[288,1024]{1,0:T(8,128)(2,1)S(1)}, u32[]{:S(2)}, u32[]{:S(2)}) collective-permute-start(bf16[288,1024]{1,0:T(8,128)(2,1)} %get-tuple-element.166), channel_id=1, source_target_pairs={{0,6},{1,7},{2,4},{3,5},{4,2},{5,3},{6,0},{7,1},{8,14},{9,15},{10,... | collective-permute-start | bytes 1769480 | tf_op jit(solution)/shard_map/ppermute | solution.py:376
  354.5 50.9 %collective-permute-start.55 = (bf16[288,1024]{1,0:T(8,128)(2,1)}, bf16[288,1024]{1,0:T(8,128)(2,1)S(1)}, u32[]{:S(2)}, u32[]{:S(2)}) collective-permute-start(bf16[288,1024]{1,0:T(8,128)(2,1)} %get-tuple-element.167), channel_id=1, source_target_pairs={{0,4},{1,5},{2,6},{3,7},{4,0},{5,1},{6,2},{7,3},{8,12},{9,13},{10,... | collective-permute-start | bytes 1769480 | tf_op jit(solution)/shard_map/ppermute | solution.py:376
  357.1 20.5 %collective-permute-start.49 = (bf16[4,72,1536]{2,1,0:T(8,128)(2,1)}, bf16[4,72,1536]{2,1,0:T(8,128)(2,1)S(1)}, u32[]{:S(2)}, u32[]{:S(2)}) collective-permute-start(bf16[4,72,1536]{2,1,0:T(8,128)(2,1)} %get-tuple-element.133), channel_id=1, source_target_pairs={{0,8},{1,9},{2,10},{3,11},{4,12},{5,13},{6,14},{7,15},{8,0},{9,1},... | collective-permute-start | bytes 2654216 | tf_op jit(solution)/shard_map/ppermute | solution.py:376
  371.8 15.2 %collective-permute-start.47 = (bf16[2,72,1536]{2,1,0:T(8,128)(2,1)S(1)}, bf16[2,72,1536]{2,1,0:T(8,128)(2,1)S(1)}, u32[]{:S(2)}, u32[]{:S(2)}) collective-permute-start(bf16[2,72,1536]{2,1,0:T(8,128)(2,1)S(1)} %add_convert_fusion.7), channel_id=1, source_target_pairs={{0,8},{1,9},{2,10},{3,11},{4,12},{5,13},{6,14},{7,15},{8,0},{9,1},... | collective-permute-start | bytes 1327112 | tf_op jit(solution)/shard_map/ppermute | solution.py:376
  377.6 9.7 %collective-permute-start.50 = (bf16[2,72,1536]{2,1,0:T(8,128)(2,1)S(1)}, bf16[2,72,1536]{2,1,0:T(8,128)(2,1)S(1)}, u32[]{:S(2)}, u32[]{:S(2)}) collective-permute-start(bf16[2,72,1536]{2,1,0:T(8,128)(2,1)S(1)} %add_convert_fusion.6), channel_id=1, source_target_pairs={{0,16},{1,17},{2,18},{3,19},{4,20},{5,21},{6,22},{7,23},{8,24},{9,... | collective-permute-start | bytes 1327112 | tf_op jit(solution)/shard_map/ppermute | solution.py:376
  387.2 24.9 %collective-permute-start.48 = (bf16[72,1536]{1,0:T(8,128)(2,1)S(1)}, bf16[72,1536]{1,0:T(8,128)(2,1)S(1)}, u32[]{:S(2)}, u32[]{:S(2)}) collective-permute-start(bf16[72,1536]{1,0:T(8,128)(2,1)S(1)} %fusion.24), channel_id=1, source_target_pairs={{0,2},{1,3},{2,0},{3,1},{4,6},{5,7},{6,4},{7,5},{8,10},{9,11},{10,... | collective-permute-start | bytes 663560 | tf_op jit(solution)/shard_map/ppermute | solution.py:376
  406.9 16.7 %collective-permute-start.51 = (bf16[72,1536]{1,0:T(8,128)(2,1)S(1)}, bf16[72,1536]{1,0:T(8,128)(2,1)S(1)}, u32[]{:S(2)}, u32[]{:S(2)}) collective-permute-start(bf16[72,1536]{1,0:T(8,128)(2,1)S(1)} %get-tuple-element.186), channel_id=1, source_target_pairs={{0,4},{1,5},{2,6},{3,7},{4,0},{5,1},{6,2},{7,3},{8,12},{9,13},{10,... | collective-permute-start | bytes 663560 | tf_op jit(solution)/shard_map/ppermute | solution.py:376
  409.9 20.1 %collective-permute-start.52 = (bf16[72,1536]{1,0:T(8,128)(2,1)S(1)}, bf16[72,1536]{1,0:T(8,128)(2,1)S(1)}, u32[]{:S(2)}, u32[]{:S(2)}) collective-permute-start(bf16[72,1536]{1,0:T(8,128)(2,1)S(1)} %get-tuple-element.187), channel_id=1, source_target_pairs={{0,6},{1,7},{2,4},{3,5},{4,2},{5,3},{6,0},{7,1},{8,14},{9,15},{10,... | collective-permute-start | bytes 663560 | tf_op jit(solution)/shard_map/ppermute | solution.py:376
  410.4 20.4 %collective-permute-start.57 = (f32[32,512]{1,0:T(8,128)S(1)}, f32[32,512]{1,0:T(8,128)S(1)}, u32[]{:S(2)}, u32[]{:S(2)}) collective-permute-start(f32[32,512]{1,0:T(8,128)S(1)} %get-tuple-element.165), channel_id=1, source_target_pairs={{0,1},{1,0},{2,3},{3,2},{4,5},{5,4},{6,7},{7,6},{8,9},{9,8},{10,11... | collective-permute-start | bytes 196616 | tf_op jit(solution)/shard_map/ppermute | solution.py:376
  412.0 19.6 %collective-permute-start.58 = (f32[2,32,8,128]{3,2,1,0:T(8,128)S(1)}, f32[2,32,8,128]{3,2,1,0:T(8,128)S(1)}, u32[]{:S(2)}, u32[]{:S(2)}) collective-permute-start(f32[2,32,8,128]{3,2,1,0:T(8,128)S(1)} %select_bitcast_fusion), channel_id=1, source_target_pairs={{0,1},{1,0},{2,3},{3,2},{4,5},{5,4},{6,7},{7,6},{8,9},{9,8},{10,11... | collective-permute-start | bytes 786440 | tf_op jit(solution)/shard_map/ppermute | solution.py:376
  (76 other events, 798.2 us)
